TPU v7x, 128 devices: a whole 4x4x4 slice. The times are simulated.
128 devices in a mesh: scan: 16 (over x, z_hi, core), grp: 8 (over z_lo, y).
Axes of the slice: x: 4, y: 4, z: 4 (z_hi: 2, z_lo: 2; z = z_hi * 2 + z_lo), core: 2. Of those that a mesh axis runs over, the one named last changes fastest.
Arguments:
- frames: bfloat16 [256, 1024, 1024], P('scan', 'grp'), may hold values from -6 to 6
- dark_frame: int32 [36864], replicated, may hold values from 0 to 15
- gain_frame: int32 [36864], replicated, may hold values from 3072 to 5120
- bf_index: int32 [1024], replicated, may hold values from 0 to 36863
- row_level: float32 [256], P('scan'), may hold values from 0.5 to 2
- shift_num: int32 [2, 1024], P(None, ('scan', 'grp')), may hold values from -32 to 32
Outputs:
- upsampled: float32 [512, 2048], P(('scan', 'grp'))
- correlation: float32 [1024, 256], P(('scan', 'grp'))
All inputs are finite; a program needn't handle non-finite values.
Results may differ from a plain program's by a relative error of at most 0.0085.
Values may be sent and summed in bfloat16 or wider, within the bound.
No kernel may reach another device: no remote copies, remote signals or barrier semaphores. Data moves between devices by JAX's collectives and lax.ppermute only.
A program may use at most 64 MiB of HBM per device.

v0:
```python
import math

import jax
import jax.numpy as jnp
from jax import lax
from jax.sharding import PartitionSpec as P

BF = 1024
LAGS = 16
DEN = 4


def laid_out(blocks, dim):
    shape = list(blocks.shape[1:])
    shape[dim] *= blocks.shape[0]
    return jnp.moveaxis(blocks, 0, dim).reshape(shape)


def from_everyone(value, axis):
    peers = lax.axis_size(axis)
    return lax.all_to_all(
        jnp.broadcast_to(value[None], (peers, *value.shape)), axis, 0, 0, tiled=True
    )


def gather_directly(value, axis, dim):
    return laid_out(from_everyone(value, axis), dim)


def signed_freq(length):
    indices = jnp.arange(length, dtype=jnp.int32)
    return jnp.where(indices < length // 2, indices, indices - length)


def phase_pair(leading, trailing, period):
    product = jnp.mod(leading[:, None] * trailing[None, :], period)
    angles = product.astype(jnp.float32) * (2.0 * math.pi / period)
    return (jnp.cos(angles), jnp.sin(angles))


def low_dot(left, right):
    return jnp.dot(left, right, preferred_element_type=jnp.float32)


def exact_dot(left, right):
    return jnp.dot(left, right, precision=lax.Precision.HIGHEST, preferred_element_type=jnp.float32)


def forward_pair(picture, cosine_cols, sine_cols, cosine_rows, sine_rows):
    real_rows = low_dot(picture, cosine_cols).astype(jnp.bfloat16)
    imag_rows = (-low_dot(picture, sine_cols)).astype(jnp.bfloat16)
    real_part = low_dot(cosine_rows, real_rows) + low_dot(sine_rows, imag_rows)
    imag_part = low_dot(cosine_rows, imag_rows) - low_dot(sine_rows, real_rows)
    anchor = (jnp.arange(real_part.shape[0])[:, None] == 0) & (
        jnp.arange(real_part.shape[1])[None, :] == 0
    )
    return (jnp.where(anchor, 0.0, real_part), jnp.where(anchor, 0.0, imag_part))


def axis_phase(length, amount):
    product = jnp.mod(signed_freq(length) * amount, DEN * length)
    angles = product.astype(jnp.float32) * (2.0 * math.pi / (DEN * length))
    return (jnp.cos(angles), jnp.sin(angles))


def shift_apply(real_part, imag_part, amounts):
    cosine_y, sine_y = axis_phase(real_part.shape[0], amounts[0])
    cosine_x, sine_x = axis_phase(real_part.shape[1], amounts[1])
    cos_phi = cosine_y[:, None] * cosine_x[None, :] - sine_y[:, None] * sine_x[None, :]
    sin_phi = sine_y[:, None] * cosine_x[None, :] + cosine_y[:, None] * sine_x[None, :]
    real_shift = (real_part * cos_phi + imag_part * sin_phi).astype(jnp.bfloat16)
    imag_shift = (imag_part * cos_phi - real_part * sin_phi).astype(jnp.bfloat16)
    return (real_shift, imag_shift)


def correlate(real_part, imag_part, ref_real, ref_imag, lag_tables, scale):
    lag_rows_cos, lag_rows_sin, lag_cols_cos, lag_cols_sin = lag_tables
    cross_real = (real_part * ref_real + imag_part * ref_imag).astype(jnp.bfloat16)
    cross_imag = (imag_part * ref_real - real_part * ref_imag).astype(jnp.bfloat16)
    half_real = low_dot(lag_rows_cos, cross_real) - low_dot(lag_rows_sin, cross_imag)
    half_imag = low_dot(lag_rows_cos, cross_imag) + low_dot(lag_rows_sin, cross_real)
    return (
        (exact_dot(half_real, lag_cols_cos) - exact_dot(half_imag, lag_cols_sin)) * scale
    ).reshape(-1)


def local(frames, dark_frame, gain_frame, bf_index, row_level, shift_num):
    dark_pixel = jnp.take(dark_frame, bf_index).astype(jnp.float32) / 256.0
    gain_pixel = jnp.take(gain_frame, bf_index).astype(jnp.float32) / 4096.0
    corrected = (frames.astype(jnp.float32) - row_level[:, None, None] * dark_pixel) * gain_pixel
    ref_local = jnp.sum(corrected, axis=2).astype(jnp.bfloat16)
    strips = jnp.transpose(corrected, (2, 0, 1)).astype(jnp.bfloat16)
    ref_strip = gather_directly(ref_local, "grp", 1)
    ref_image = gather_directly(ref_strip, "scan", 0)
    mixed = lax.all_to_all(strips, ("scan", "grp"), split_axis=0, concat_axis=1, tiled=True)
    scan_count = lax.axis_size("scan")
    grp_count = lax.axis_size("grp")
    owned = mixed.shape[0]
    strip_rows = strips.shape[1]
    strip_cols = strips.shape[2]
    pictures = mixed.reshape(owned, scan_count, grp_count, strip_rows, strip_cols)
    pictures = pictures.transpose(0, 1, 3, 2, 4).reshape(
        owned, scan_count * strip_rows, grp_count * strip_cols
    )
    rows = pictures.shape[1]
    cols = pictures.shape[2]
    row_range = jnp.arange(rows, dtype=jnp.int32)
    col_range = jnp.arange(cols, dtype=jnp.int32)
    cosine_cols, sine_cols = phase_pair(col_range, col_range, cols)
    cosine_rows, sine_rows = phase_pair(row_range, row_range, rows)
    tables = (
        cosine_cols.astype(jnp.bfloat16),
        sine_cols.astype(jnp.bfloat16),
        cosine_rows.astype(jnp.bfloat16),
        sine_rows.astype(jnp.bfloat16),
    )
    up_rows_cos, up_rows_sin = phase_pair(
        jnp.arange(2 * rows, dtype=jnp.int32), signed_freq(rows), 2 * rows
    )
    up_rows_cos = up_rows_cos.astype(jnp.bfloat16)
    up_rows_sin = up_rows_sin.astype(jnp.bfloat16)
    up_cols_cos, up_cols_sin = phase_pair(
        signed_freq(cols), jnp.arange(2 * cols, dtype=jnp.int32), 2 * cols
    )
    up_cols_cos = up_cols_cos.astype(jnp.bfloat16)
    up_cols_sin = up_cols_sin.astype(jnp.bfloat16)
    lag_values = jnp.arange(LAGS, dtype=jnp.int32) - LAGS // 2
    lag_rows_cos, lag_rows_sin = phase_pair(lag_values, row_range, rows)
    lag_rows_cos = lag_rows_cos.astype(jnp.bfloat16)
    lag_rows_sin = lag_rows_sin.astype(jnp.bfloat16)
    lag_cols_cos, lag_cols_sin = phase_pair(col_range, lag_values, cols)
    lag_tables = (lag_rows_cos, lag_rows_sin, lag_cols_cos, lag_cols_sin)
    corr_scale = 1.0 / (rows * cols * math.sqrt(BF * rows * cols))
    ref_real, ref_imag = forward_pair(ref_image, *tables)

    def accumulate(totals, real_shift, imag_shift):
        total_real = totals[0] + low_dot(up_rows_cos, real_shift) - low_dot(up_rows_sin, imag_shift)
        total_imag = totals[1] + low_dot(up_rows_cos, imag_shift) + low_dot(up_rows_sin, real_shift)
        return (total_real, total_imag)

    start_totals = (
        jnp.zeros((2 * rows, cols), jnp.float32),
        jnp.zeros((2 * rows, cols), jnp.float32),
    )

    def visit(totals, element):
        picture, amounts = element
        real_part, imag_part = forward_pair(picture, *tables)
        correl = correlate(real_part, imag_part, ref_real, ref_imag, lag_tables, corr_scale)
        real_shift, imag_shift = shift_apply(real_part, imag_part, amounts)
        return (accumulate(totals, real_shift, imag_shift), correl)

    totals, correls = lax.scan(visit, start_totals, (pictures, shift_num.T))
    summed_real, summed_imag = (
        lax.psum_scatter(totals[0], ("scan", "grp"), scatter_dimension=0, tiled=True),
        lax.psum_scatter(totals[1], ("scan", "grp"), scatter_dimension=0, tiled=True),
    )
    rows_real = summed_real.astype(jnp.bfloat16)
    rows_imag = summed_imag.astype(jnp.bfloat16)
    upsampled = (low_dot(rows_real, up_cols_cos) - low_dot(rows_imag, up_cols_sin)) * (
        1.0 / (rows * cols * math.sqrt(BF))
    )
    return (upsampled, correls)


def solution(mesh):
    return jax.shard_map(
        local,
        mesh=mesh,
        in_specs=(P("scan", "grp", None), P(), P(), P(), P("scan"), P(None, ("scan", "grp"))),
        out_specs=(P(("scan", "grp"), None), P(("scan", "grp"), None)),
        check_vma=False,
    )
```

profile of v0, /device:TPU:0, one launch (start us, length us, event | category | flops | bytes accessed | tf_op | source)
XLA Modules:
  0.0 828.6 jit_solution(7339321201497513612)
XLA Ops:
  1.5 6.1 gather_fusion
  7.7 6.2 gather_fusion.1
  13.9 6.9 copy.19
  21.1 8.6 %fusion.158 = (bf16[16,128]{1,0:T(8,128)(2,1)S(1)}, bf16[1024,16,128]{2,1,0:T(8,128)(2,1)}) fusion(bf16[16,128,1024]{1,0,2:T(8,128)(2,1)} %copy.19, f32[1024]{0:T(1024)S(1)} %fusion.191, f32[16,1024]{0,1:T(8,128)S(1)} %broadcast_multiply_fusion), kind=kLoop, calls=%fused_computation.201 | loop fusion | flops 10483712 | bytes 8462336 | tf_op jit(solution)/shard_map/reduce_sum | solution.py:91
  29.6 12.0 %all_to_all.25 = bf16[8,16,128]{2,1,0:T(8,128)(2,1)S(1)} all-to-all(bf16[8,16,128]{2,1,0:T(8,128)(2,1)S(1)} %broadcast_in_dim.36), channel_id=1, replica_groups=mesh['scan'=16,'grp'=8] {'grp'}, dimensions={0} | all-to-all | bytes 65536 | tf_op jit(solution)/shard_map/all_to_all | solution.py:21
  41.7 19.6 %all_to_all.26 = bf16[16,16,1024]{2,1,0:T(8,128)(2,1)S(1)} all-to-all(bf16[16,16,1024]{2,1,0:T(8,128)(2,1)S(1)} %broadcast_in_dim.38), channel_id=1, replica_groups=mesh['scan'=16,'grp'=8] {'scan'}, dimensions={0} | all-to-all | bytes 1048576 | tf_op jit(solution)/shard_map/all_to_all | solution.py:21
  61.3 6.4 all-to-all-start
  67.7 16.1 %fusion.182 = bf16[256,1024]{1,0:T(8,128)(2,1)S(1)} fusion(bf16[256,1024]{1,0:T(8,128)(2,1)S(1)} %bitcast.116), kind=kOutput, calls=%fused_computation.228 | convolution fusion | flops 552861696 | bytes 1048576 | tf_op jit(solution)/shard_map/dot_general | solution.py:42
  85.0 16.5 %fusion.181 = bf16[256,1024]{1,0:T(8,128)(2,1)S(1)} fusion(bf16[256,1024]{1,0:T(8,128)(2,1)S(1)} %bitcast.117), kind=kOutput, calls=%fused_computation.227 | convolution fusion | flops 553123840 | bytes 1048576 | tf_op jit(solution)/shard_map/dot_general | solution.py:42
  110.7 10.1 %all-to-all-done = bf16[1024,16,128]{2,1,0:T(8,128)(2,1)} async-done(((bf16[1024,16,128]{2,1,0:T(8,128)(2,1)}), bf16[1024,16,128]{2,1,0:T(8,128)(2,1)}, u32[]{:S(2)}, u32[]{:S(2)}) %all-to-all-start) | async-done | bytes 4194336 | tf_op jit(solution)/shard_map/all_to_all | solution.py:95
  120.8 9.0 %copy.21 = bf16[8,16,16,8,128]{4,3,2,1,0:T(8,128)(2,1)} copy(bf16[8,16,16,8,128]{4,2,0,3,1:T(8,128)(2,1)} %bitcast.5) | data formatting | bytes 8388608 | tf_op jit(solution)/shard_map/transpose | solution.py:102
  129.8 7.3 reshape.145
  137.1 519.8 %while.21 = (s32[]{:T(128)}, f32[512,1024]{0,1:T(8,128)S(1)}, f32[512,1024]{0,1:T(8,128)}, f32[8,256]{1,0:T(8,128)S(1)}, bf16[8,256,1024]{2,1,0:T(8,128)(2,1)}, ...) while((s32[]{:T(128)}, f32[512,1024]{0,1:T(8,128)S(1)}, ...), condition=%wide.region_2.4_spmd.clone.clone.clone.clone, body=%wide.region_1.3_spmd.clone.clone.clone.clone.sunk | while | flops 2779487232 | bytes 44601700 | solution.py:153
  154.9 17.4 %fusion.300 = bf16[256,1024]{1,0:T(8,128)(2,1)S(1)} fusion(bf16[8,256,1024]{2,1,0:T(8,128)(2,1)} %get-tuple-element.674, s32[]{:T(128)} %get-tuple-element.658), kind=kOutput, calls=%fused_computation.36.clone.1 | convolution fusion | flops 553123840 | bytes 1049088 | tf_op jit(solution)/shard_map/while/body/eval_jaxpr/dot_general | solution.py:42
  173.6 17.2 %fusion.302 = bf16[256,1024]{1,0:T(8,128)(2,1)S(1)} fusion(bf16[8,256,1024]{2,1,0:T(8,128)(2,1)} %get-tuple-element.674, s32[]{:T(128)} %get-tuple-element.658), kind=kOutput, calls=%fused_computation.37.clone.1 | convolution fusion | flops 552861696 | bytes 1049088 | tf_op jit(solution)/shard_map/while/body/eval_jaxpr/dot_general | solution.py:42
  216.4 17.4 %fusion.300 = bf16[256,1024]{1,0:T(8,128)(2,1)S(1)} fusion(bf16[8,256,1024]{2,1,0:T(8,128)(2,1)} %get-tuple-element.674, s32[]{:T(128)} %get-tuple-element.658), kind=kOutput, calls=%fused_computation.36.clone.1 | convolution fusion | flops 553123840 | bytes 1049088 | tf_op jit(solution)/shard_map/while/body/eval_jaxpr/dot_general | solution.py:42
  235.0 17.2 %fusion.302 = bf16[256,1024]{1,0:T(8,128)(2,1)S(1)} fusion(bf16[8,256,1024]{2,1,0:T(8,128)(2,1)} %get-tuple-element.674, s32[]{:T(128)} %get-tuple-element.658), kind=kOutput, calls=%fused_computation.37.clone.1 | convolution fusion | flops 552861696 | bytes 1049088 | tf_op jit(solution)/shard_map/while/body/eval_jaxpr/dot_general | solution.py:42
  278.3 17.4 %fusion.300 = bf16[256,1024]{1,0:T(8,128)(2,1)S(1)} fusion(bf16[8,256,1024]{2,1,0:T(8,128)(2,1)} %get-tuple-element.674, s32[]{:T(128)} %get-tuple-element.658), kind=kOutput, calls=%fused_computation.36.clone.1 | convolution fusion | flops 553123840 | bytes 1049088 | tf_op jit(solution)/shard_map/while/body/eval_jaxpr/dot_general | solution.py:42
  296.9 17.2 %fusion.302 = bf16[256,1024]{1,0:T(8,128)(2,1)S(1)} fusion(bf16[8,256,1024]{2,1,0:T(8,128)(2,1)} %get-tuple-element.674, s32[]{:T(128)} %get-tuple-element.658), kind=kOutput, calls=%fused_computation.37.clone.1 | convolution fusion | flops 552861696 | bytes 1049088 | tf_op jit(solution)/shard_map/while/body/eval_jaxpr/dot_general | solution.py:42
  340.1 17.4 %fusion.300 = bf16[256,1024]{1,0:T(8,128)(2,1)S(1)} fusion(bf16[8,256,1024]{2,1,0:T(8,128)(2,1)} %get-tuple-element.674, s32[]{:T(128)} %get-tuple-element.658), kind=kOutput, calls=%fused_computation.36.clone.1 | convolution fusion | flops 553123840 | bytes 1049088 | tf_op jit(solution)/shard_map/while/body/eval_jaxpr/dot_general | solution.py:42
  358.7 17.2 %fusion.302 = bf16[256,1024]{1,0:T(8,128)(2,1)S(1)} fusion(bf16[8,256,1024]{2,1,0:T(8,128)(2,1)} %get-tuple-element.674, s32[]{:T(128)} %get-tuple-element.658), kind=kOutput, calls=%fused_computation.37.clone.1 | convolution fusion | flops 552861696 | bytes 1049088 | tf_op jit(solution)/shard_map/while/body/eval_jaxpr/dot_general | solution.py:42
  401.9 17.4 %fusion.300 = bf16[256,1024]{1,0:T(8,128)(2,1)S(1)} fusion(bf16[8,256,1024]{2,1,0:T(8,128)(2,1)} %get-tuple-element.674, s32[]{:T(128)} %get-tuple-element.658), kind=kOutput, calls=%fused_computation.36.clone.1 | convolution fusion | flops 553123840 | bytes 1049088 | tf_op jit(solution)/shard_map/while/body/eval_jaxpr/dot_general | solution.py:42
  420.5 17.2 %fusion.302 = bf16[256,1024]{1,0:T(8,128)(2,1)S(1)} fusion(bf16[8,256,1024]{2,1,0:T(8,128)(2,1)} %get-tuple-element.674, s32[]{:T(128)} %get-tuple-element.658), kind=kOutput, calls=%fused_computation.37.clone.1 | convolution fusion | flops 552861696 | bytes 1049088 | tf_op jit(solution)/shard_map/while/body/eval_jaxpr/dot_general | solution.py:42
  463.7 17.4 %fusion.300 = bf16[256,1024]{1,0:T(8,128)(2,1)S(1)} fusion(bf16[8,256,1024]{2,1,0:T(8,128)(2,1)} %get-tuple-element.674, s32[]{:T(128)} %get-tuple-element.658), kind=kOutput, calls=%fused_computation.36.clone.1 | convolution fusion | flops 553123840 | bytes 1049088 | tf_op jit(solution)/shard_map/while/body/eval_jaxpr/dot_general | solution.py:42
  482.3 17.2 %fusion.302 = bf16[256,1024]{1,0:T(8,128)(2,1)S(1)} fusion(bf16[8,256,1024]{2,1,0:T(8,128)(2,1)} %get-tuple-element.674, s32[]{:T(128)} %get-tuple-element.658), kind=kOutput, calls=%fused_computation.37.clone.1 | convolution fusion | flops 552861696 | bytes 1049088 | tf_op jit(solution)/shard_map/while/body/eval_jaxpr/dot_general | solution.py:42
  525.6 17.4 %fusion.300 = bf16[256,1024]{1,0:T(8,128)(2,1)S(1)} fusion(bf16[8,256,1024]{2,1,0:T(8,128)(2,1)} %get-tuple-element.674, s32[]{:T(128)} %get-tuple-element.658), kind=kOutput, calls=%fused_computation.36.clone.1 | convolution fusion | flops 553123840 | bytes 1049088 | tf_op jit(solution)/shard_map/while/body/eval_jaxpr/dot_general | solution.py:42
  544.2 17.2 %fusion.302 = bf16[256,1024]{1,0:T(8,128)(2,1)S(1)} fusion(bf16[8,256,1024]{2,1,0:T(8,128)(2,1)} %get-tuple-element.674, s32[]{:T(128)} %get-tuple-element.658), kind=kOutput, calls=%fused_computation.37.clone.1 | convolution fusion | flops 552861696 | bytes 1049088 | tf_op jit(solution)/shard_map/while/body/eval_jaxpr/dot_general | solution.py:42
  587.4 17.4 %fusion.300 = bf16[256,1024]{1,0:T(8,128)(2,1)S(1)} fusion(bf16[8,256,1024]{2,1,0:T(8,128)(2,1)} %get-tuple-element.674, s32[]{:T(128)} %get-tuple-element.658), kind=kOutput, calls=%fused_computation.36.clone.1 | convolution fusion | flops 553123840 | bytes 1049088 | tf_op jit(solution)/shard_map/while/body/eval_jaxpr/dot_general | solution.py:42
  606.0 17.2 %fusion.302 = bf16[256,1024]{1,0:T(8,128)(2,1)S(1)} fusion(bf16[8,256,1024]{2,1,0:T(8,128)(2,1)} %get-tuple-element.674, s32[]{:T(128)} %get-tuple-element.658), kind=kOutput, calls=%fused_computation.37.clone.1 | convolution fusion | flops 552861696 | bytes 1049088 | tf_op jit(solution)/shard_map/while/body/eval_jaxpr/dot_general | solution.py:42
  657.0 106.9 %all-reduce.4 = (bf16[512,1024]{0,1:T(8,128)(2,1)}, bf16[512,1024]{0,1:T(8,128)(2,1)S(1)}) all-reduce(f32[512,1024]{0,1:T(8,128)S(1)} %get-tuple-element.298, f32[512,1024]{0,1:T(8,128)} %get-tuple-element.299), channel_id=2, replica_groups=mesh['scan'=16,'grp'=8] {'scan','grp'}, use_global_device_ids=true, to_apply=%region_3.5.clone | all-reduce | flops 1048576 | bytes 6291456
  763.9 32.1 %fusion.165 = f32[4,2048]{1,0:T(4,128)S(1)} fusion(s32[1024]{0:T(1024)S(1)} %compare_select_fusion.5, bf16[512,1024]{0,1:T(8,128)(2,1)} %get-tuple-element.547, u32[]{:T(128)S(6)} %multiply.3), kind=kOutput, calls=%fused_computation.211 | convolution fusion | flops 48234496 | bytes 299012 | tf_op jit(solution)/shard_map/dot_general | solution.py:42
  796.0 32.4 %fusion.173 = f32[4,2048]{1,0:T(4,128)} fusion(f32[4,2048]{1,0:T(4,128)S(1)} %fusion.165, s32[1024]{0:T(1024)S(1)} %compare_select_fusion.5, bf16[512,1024]{0,1:T(8,128)(2,1)S(1)} %get-tuple-element.548, u32[]{:T(128)S(6)} %multiply.3), kind=kOutput, calls=%fused_computation.219 | convolution fusion | flops 48250880 | bytes 331780 | tf_op jit(solution)/shard_map/dot_general | solution.py:42
  (245 shorter events, 228.3 us)
Async XLA Ops:
  0.6 0.9 copy-start
  0.6 7.1 copy-start.7
  0.7 7.1 copy-start.1
  13.9 7.0 copy-start.8
  61.3 59.5 %all-to-all-start = ((bf16[1024,16,128]{2,1,0:T(8,128)(2,1)}), bf16[1024,16,128]{2,1,0:T(8,128)(2,1)}, u32[]{:S(2)}, u32[]{:S(2)}) async-start(bf16[1024,16,128]{2,1,0:T(8,128)(2,1)} %get-tuple-element.564), calls=%async_computation | async-start | bytes 8388608 | tf_op jit(solution)/shard_map/all_to_all | solution.py:95
  83.8 17.7 %copy-start.4 = (bf16[256,1024]{1,0:T(8,128)(2,1)}, bf16[256,1024]{1,0:T(8,128)(2,1)S(1)}, u32[]{:S(2)}) copy-start(bf16[256,1024]{1,0:T(8,128)(2,1)S(1)} %fusion.182) | copy-start | bytes 1572868
  101.5 0.8 copy-start.5
  129.8 7.3 copy-start.6
  190.8 4.5 copy-start.2
  190.8 4.5 copy-start.3
  252.3 4.5 copy-start.2
  252.3 4.5 copy-start.3
  314.1 4.5 copy-start.2
  314.1 4.5 copy-start.3
  375.9 4.5 copy-start.2
  375.9 4.5 copy-start.3
  437.7 4.5 copy-start.2
  437.7 4.5 copy-start.3
  499.6 4.5 copy-start.2
  499.6 4.5 copy-start.3
  561.4 4.5 copy-start.2
  561.4 4.5 copy-start.3
  623.2 4.5 copy-start.2
  623.2 4.5 copy-start.3
  657.0 139.0 %copy-start.9 = (f32[8,256]{1,0:T(8,128)}, f32[8,256]{1,0:T(8,128)S(1)}, u32[]{:S(2)}) copy-start(f32[8,256]{1,0:T(8,128)S(1)} %get-tuple-element.297) | copy-start | bytes 24580
where the time goes:
time: 833 us; the launch traced here: 829 us
  matrix products  581 us (70%)
  blocking collectives  138 us (17%)
  local copies, waits for them, and re-layouts  45 us (5%)
  loops' own time  26.6 us (3%)
  other arithmetic  20 us (2%)
  waiting for transfers between devices  10.1 us (1%)
    dot_general x120, matrix products, low_dot(): return jnp.dot(left, right, preferred_element_type=jnp.float32)  544 us
    unnamed x1, blocking collectives  107 us
    dot_general x16, matrix products, exact_dot(): jnp.dot(left, right, precision=lax.Precision.HIGHEST, preferred_element_t...  37.2 us
    all_to_all x2, blocking collectives, from_everyone(): lax.all_to_all(jnp.broadcast_to(value[None], (peers, *value.shape)), axis...  31.6 us
    another operation x1, loops' own time, local(): totals, correls = lax.scan(visit, start_totals, (pictures, shift_num.T))  26.6 us
  transfers between devices with their start and end apart: 1, of which 1 were waited for; matrix products, arithmetic and copies ran while one was open for 5% of the time, Pallas kernels for 0%

commit v1 on v0

v1 whole, which is shorter than its diff:
```python
import math

import jax
import jax.numpy as jnp
import ml_dtypes
import numpy as np
from jax import lax
from jax.experimental import pallas as pl
from jax.experimental.pallas import tpu as pltpu
from jax.sharding import PartitionSpec as P

SY = 256
SX = 1024
BF = 1024
DET = 36864
AXES = ("scan", "grp")
S = 16
G = 8
N = S * G
YS = SY // S
XS = SX // G
ROWS = DET // 128
BX = 17
F32 = jnp.float32
BF16 = jnp.bfloat16
NT = (((1,), (1,)), ((), ()))
TN = (((0,), (0,)), ((), ()))
VMEM_LIMIT = 56 * 1024 * 1024


def row_kernel():
    k = np.arange(-128, 128)
    q = np.arange(1024)
    d = np.cos(2 * np.pi * k[None, :] * q[:, None] / 1024).sum(1) / 256
    yp = np.arange(1024) % 512
    yy = np.repeat(np.arange(32), 4)
    fy = np.tile(np.arange(4), 32)
    return d[(2 * yp[:, None] - fy[None, :] - 4 * (yy[None, :] - 8)) % 1024].astype(ml_dtypes.bfloat16)


def col_tables():
    x = np.arange(512) - 8
    out = []
    for par in (0, 1):
        k = 2 * np.arange(256) + par
        ang = 2 * np.pi * ((x[:, None] * k[None, :]) % 1024) / 1024
        c, s = np.cos(ang), np.sin(ang)
        if par == 0:
            s[:, 0] = np.where(x % 2 == 0, 1.0, -1.0)
        out.append(np.concatenate([c, s], 1).astype(ml_dtypes.bfloat16))
    xp = np.arange(1024)
    for par in (0, 1):
        k = 2 * np.arange(256) + par
        w = np.where(k == 0, 1.0, 2.0)[:, None]
        ang = 2 * np.pi * ((k[:, None] * xp[None, :]) % 2048) / 2048
        out.append(np.concatenate([w * np.cos(ang), -w * np.sin(ang)], 0).astype(ml_dtypes.bfloat16))
    phase = np.zeros((16, 256), np.float32)
    for par in (0, 1):
        k = 2 * np.arange(256) + par
        for fx in range(4):
            phase[par * 8 + fx] = np.cos(2 * np.pi * k * fx / 4096)
            phase[par * 8 + 4 + fx] = np.sin(2 * np.pi * k * fx / 4096)
    return (*out, phase)


def nyquist_tables():
    w = np.zeros((16, 128), np.float32)
    for yp in range(4):
        for fx in range(4):
            for fy in range(4):
                sy = math.sin(math.pi * (2 * yp - fy) / 4) / 256
                for base in (64, 80):
                    w[yp, base + fx * 4 + fy] = sy * math.sin(math.pi * fx / 4)
                    w[8 + yp, base + fx * 4 + fy] = -sy * math.cos(math.pi * fx / 4)
    return w


def correct_kernel(level, frames, dark, gain, index, v_out, r_out, dark_px, gain_px):
    y = pl.program_id(0)

    @pl.when(y == 0)
    def _():
        g = gain[...]
        table = jnp.concatenate(
            [dark[...].astype(F32), (g >> 5).astype(F32), (g & 31).astype(F32)], axis=1
        ).astype(BF16)
        idx = index[...]
        hot = (lax.broadcasted_iota(jnp.int32, (ROWS, BF), 0) == (idx >> 7)).astype(F32).astype(BF16)
        picked = lax.dot_general(table, hot, TN, preferred_element_type=F32)
        mine = lax.broadcasted_iota(jnp.int32, (128, BF), 0) == (idx & 127)

        def pick(i):
            return jnp.sum(jnp.where(mine, picked[128 * i : 128 * (i + 1)], 0.0), axis=0, keepdims=True)

        dark_px[...] = pick(0) * (1.0 / 256.0)
        gain_px[...] = (pick(1) * 32.0 + pick(2)) * (1.0 / 4096.0)

    value = (frames[0].astype(F32) - level[y] * dark_px[...]) * gain_px[...]
    value = value.astype(BF16)
    v_out[0] = value
    total = lax.dot_general(jnp.ones((8, BF), BF16), value, NT, preferred_element_type=F32)
    r_out[pl.ds(y, 1), :] = total[0:1]


def shift_kernel(strip, shifts, v, rows, z_out, moved, hot, main, over):
    for t in range(8):
        lanes = slice(128 * t, 128 * (t + 1))
        sy = shifts[t, 0:1, :]
        sx = shifts[t, 1:2, :]
        by = (sy >> 2) + 8
        code = ((sx >> 2) + 8) * 16 + (sx & 3) * 4 + (sy & 3)
        hot[:, lanes] = (
            (lax.broadcasted_iota(jnp.int32, (BX * 16, 128), 0) == code).astype(F32).astype(BF16)
        )
        masks = [
            jnp.broadcast_to(((by >> b) & 1).astype(F32), (16, 128)).astype(BF16) > 0.5 for b in range(5)
        ]

        def barrel(i, _, lanes=lanes, masks=masks):
            x0 = pl.multiple_of(i * 16, 16)
            rows_in = [v[y, pl.ds(x0, 16), lanes] for y in range(YS)]
            zero = jnp.zeros((16, 128), BF16)
            for b in range(5):
                step = 1 << b
                size = min(len(rows_in) + step, 32)
                old = rows_in
                rows_in = [
                    jnp.where(
                        masks[b],
                        old[j - step] if 0 <= j - step < len(old) else zero,
                        old[j] if j < len(old) else zero,
                    )
                    for j in range(size)
                ]
            for j in range(32):
                moved[j, pl.ds(x0, 16), lanes] = rows_in[j]
            return 0

        lax.fori_loop(0, 8, barrel, 0)

    lane = lax.broadcasted_iota(jnp.int32, (16, 128), 1)

    def group(j, _):
        block = moved[pl.ds(2 * j, 2)].reshape(256, BF)
        sums = lax.dot_general(hot[...], block, NT, preferred_element_type=F32)
        for h in range(2):
            acc_main = sums[0:16, 128 * h : 128 * (h + 1)]
            acc_over = jnp.zeros((16, 128), F32)
            for b in range(1, BX):
                piece = pltpu.roll(sums[16 * b : 16 * (b + 1), 128 * h : 128 * (h + 1)], b, 1)
                acc_main = acc_main + jnp.where(lane >= b, piece, 0.0)
                acc_over = acc_over + jnp.where(lane < b, piece, 0.0)
            main[2 * j + h] = acc_main
            over[2 * j + h] = acc_over
        return 0

    lax.fori_loop(0, 16, group, 0)

    sign_y = 1.0 - 2.0 * (lax.broadcasted_iota(jnp.int32, (32, 16, 128), 0) & 1).astype(F32)
    sign_x = 1.0 - 2.0 * (lax.broadcasted_iota(jnp.int32, (8, 128), 1) & 1).astype(F32)
    folded = jnp.sum((main[...] + over[...]) * sign_y, axis=0)
    folded = jnp.concatenate([jnp.zeros((64, 128), F32), folded, jnp.zeros((48, 128), F32)], axis=0)
    q_row = lax.dot_general(sign_x, folded, NT, precision=lax.Precision.HIGHEST, preferred_element_type=F32)[0:1]
    q_high = q_row.astype(BF16).astype(F32)
    q_row = q_high + pltpu.roll(q_row - q_high, 16, 1)

    spread = (
        (lax.broadcasted_iota(jnp.int32, (128, 512), 0) >> 2)
        == (lax.broadcasted_iota(jnp.int32, (128, 512), 1) >> 4)
    ) & (
        (lax.broadcasted_iota(jnp.int32, (128, 512), 0) & 3)
        == (lax.broadcasted_iota(jnp.int32, (128, 512), 1) & 3)
    )
    start = pl.multiple_of(512 - 32 * strip[0], 32)
    left = jnp.dot(
        rows[pl.ds(start, 512), :], spread.astype(F32).astype(BF16), preferred_element_type=F32
    ).astype(BF16)
    kind = (lax.broadcasted_iota(jnp.int32, (512, 128), 0) >> 2) & 3
    u_main = main[...].reshape(512, 128)
    u_over = over[...].reshape(512, 128)
    tail = jnp.zeros((512, 128), F32)
    for fx in range(4):
        part = jnp.where(kind == fx, u_main, 0.0).astype(BF16)
        z_out[:, 128 * fx : 128 * (fx + 1)] = jnp.dot(left, part, preferred_element_type=F32).astype(BF16)
        piece = jnp.where(kind == fx, u_over, 0.0)
        tail = tail + (pltpu.roll(piece, 16 * fx, 1) if fx else piece)
    z_out[:, 512:640] = (jnp.dot(left, tail.astype(BF16), preferred_element_type=F32) + q_row).astype(BF16)


def correlate_kernel(place, v, r_all, c_out, total_out, window, table):
    s = place[0]
    g = place[1]
    whole = r_all[...].astype(F32)
    total = jnp.sum(jnp.sum(whole, axis=0), keepdims=True)
    mean = total * (1.0 / (SY * SX))
    rest = jnp.sum(jnp.sum((whole - mean).astype(BF16).astype(F32), axis=0), keepdims=True) * (1.0 / (SY * SX))
    total_out[...] = jnp.broadcast_to(total, (8, 128))
    for dg in range(3):
        gg = lax.rem(g + (dg + G - 1), G)
        above = r_all[lax.rem(s + (S - 1), S) * G + gg].astype(F32)
        here = r_all[s * G + gg].astype(F32)
        below = r_all[lax.rem(s + 1, S) * G + gg].astype(F32)
        window[0:8, 128 * dg : 128 * (dg + 1)] = above[8:16] - mean
        window[8:24, 128 * dg : 128 * (dg + 1)] = here - mean
        window[24:32, 128 * dg : 128 * (dg + 1)] = below[0:8] - mean
    for b in range(16):
        moved = pltpu.roll(window[...], (b - 8) % 384, 1)[:, 128:256]
        for yy in range(32):
            table[31 - yy, b : b + 1, :] = moved[yy : yy + 1]
    acc = jnp.zeros((256, BF), F32)
    sums = jnp.zeros((8, BF), F32)
    for j in range(0, YS, 2):
        left = jnp.concatenate(
            [table[15 - i : 31 - i].reshape(256, 128).astype(BF16) for i in (j, j + 1)], axis=1
        )
        right = v[j : j + 2].reshape(256, BF)
        acc = acc + jnp.dot(left, right, preferred_element_type=F32)
        sums = sums + jnp.dot(jnp.ones((8, 256), BF16), right, preferred_element_type=F32)
    acc = acc - rest * sums[0:1]
    c_out[...] = acc.T.astype(BF16)


def finish_kernel(zs, total, t1e, t1o, t2e, t2o, phase, nyquist, out, full):
    full[...] = jnp.zeros((32, SX), F32)
    for g in range(G):
        for fx in range(4):
            full[8 * fx : 8 * fx + 4, 128 * g : 128 * (g + 1)] = zs[g, :, 128 * fx : 128 * (fx + 1)]
    lane = lax.broadcasted_iota(jnp.int32, (4, 128), 1)
    q_rows = jnp.zeros((4, 128), F32)
    for g in range(G):
        nxt = (g + 1) % G
        tail = zs[g, :, 512:640]
        q_rows = q_rows + tail
        for fx in range(4):
            piece = pltpu.roll(tail, (128 - 16 * fx) % 128, 1) if fx else tail
            full[8 * fx : 8 * fx + 4, 128 * nxt : 128 * (nxt + 1)] += jnp.where(lane < 16, piece, 0.0)
    low = full[:, 0:512]
    high = full[:, 512:1024]
    lane_e = lax.broadcasted_iota(jnp.int32, (8, 256), 1)
    results = []
    for par, (t1, t2, part) in enumerate(((t1e, t2e, low + high), (t1o, t2o, low - high))):
        spec = jnp.dot(part.astype(BF16), t1[...], preferred_element_type=F32)
        re = jnp.zeros((8, 256), F32)
        im = jnp.zeros((8, 256), F32)
        for fx in range(4):
            c = spec[8 * fx : 8 * fx + 8, 0:256]
            s = spec[8 * fx : 8 * fx + 8, 256:512]
            if par == 0:
                ny = s[:, 0:1]
                if fx == 0:
                    ny_cos = ny
                    ny_sin = jnp.zeros_like(ny)
                else:
                    ny_cos = ny_cos + ny * math.cos(math.pi * fx / 4)
                    ny_sin = ny_sin + ny * math.sin(math.pi * fx / 4)
                s = jnp.where(lane_e == 0, 0.0, s)
            pc = phase[8 * par + fx : 8 * par + fx + 1, :]
            ps = phase[8 * par + 4 + fx : 8 * par + 5 + fx, :]
            re = re + c * pc - s * ps
            im = im - (s * pc + c * ps)
        if par == 0:
            re = jnp.where(lane_e == 0, re - total[0:1, 0:1] * (1.0 / SY), re)
        coef = jnp.concatenate([re, im], axis=1).astype(BF16)
        results.append(jnp.dot(coef, t2[...], preferred_element_type=F32))
    q_cos = jnp.sum(q_rows * nyquist[0:4, :], axis=1, keepdims=True)
    q_sin = jnp.sum(q_rows * nyquist[8:12, :], axis=1, keepdims=True)
    place = lax.broadcasted_iota(jnp.int32, (4, 1024), 1) & 3
    wave_cos = jnp.where(place == 0, 1.0, jnp.where(place == 2, -1.0, 0.0))
    wave_sin = jnp.where(place == 1, 1.0, jnp.where(place == 3, -1.0, 0.0))
    wave = (ny_cos[0:4] + q_cos) * wave_cos + (ny_sin[0:4] + q_sin) * wave_sin
    scale = 1.0 / (SX * math.sqrt(BF))
    even = results[0][0:4] + wave
    odd = results[1][0:4]
    out[:, 0:1024] = (even + odd) * scale
    out[:, 1024:2048] = (even - odd) * scale


def exchange(value):
    return lax.all_to_all(value, AXES, split_axis=0, concat_axis=0, tiled=True)


def local(frames, dark_frame, gain_frame, bf_index, row_level, shift_num):
    s = lax.axis_index("scan")
    g = lax.axis_index("grp")
    place = jnp.stack([s, g]).astype(jnp.int32)
    smem = pl.BlockSpec(memory_space=pltpu.SMEM)
    vmem = pl.BlockSpec(memory_space=pltpu.VMEM)
    params = pltpu.CompilerParams(vmem_limit_bytes=VMEM_LIMIT)

    slot = (s * G + g) % 16
    spread = jnp.tile(shift_num, (1, 16))
    spread = jnp.where(jnp.arange(128) // 8 == slot, spread, 0)
    shifts = exchange(jnp.broadcast_to(spread[None], (N, 2, 128)))
    shifts = shifts.reshape(8, 16, 2, 128).sum(axis=1)

    v, r = pl.pallas_call(
        correct_kernel,
        grid=(YS,),
        in_specs=[
            smem,
            pl.BlockSpec((1, XS, BF), lambda i: (i, 0, 0)),
            pl.BlockSpec((ROWS, 128), lambda i: (0, 0)),
            pl.BlockSpec((ROWS, 128), lambda i: (0, 0)),
            pl.BlockSpec((1, BF), lambda i: (0, 0)),
        ],
        out_specs=[
            pl.BlockSpec((1, XS, BF), lambda i: (i, 0, 0)),
            pl.BlockSpec((YS, XS), lambda i: (0, 0)),
        ],
        out_shape=[
            jax.ShapeDtypeStruct((YS, XS, BF), BF16),
            jax.ShapeDtypeStruct((YS, XS), F32),
        ],
        scratch_shapes=[pltpu.VMEM((1, BF), F32), pltpu.VMEM((1, BF), F32)],
        compiler_params=params,
        name="correct",
    )(
        row_level,
        frames,
        dark_frame.reshape(ROWS, 128),
        gain_frame.reshape(ROWS, 128),
        bf_index.reshape(1, BF),
    )
    r_all = exchange(jnp.broadcast_to(r.astype(BF16)[None], (N, YS, XS)))

    z = pl.pallas_call(
        shift_kernel,
        in_specs=[smem, vmem, vmem, vmem],
        out_specs=vmem,
        out_shape=jax.ShapeDtypeStruct((2 * SY, 640), BF16),
        scratch_shapes=[
            pltpu.VMEM((32, XS, BF), BF16),
            pltpu.VMEM((BX * 16, BF), BF16),
            pltpu.VMEM((32, 16, 128), F32),
            pltpu.VMEM((32, 16, 128), F32),
        ],
        compiler_params=params,
        name="shift",
    )(place, shifts, v, jnp.asarray(row_kernel()))
    z_all = exchange(z.reshape(N, 4, 640))

    c, total = pl.pallas_call(
        correlate_kernel,
        in_specs=[smem, vmem, vmem],
        out_specs=[vmem, vmem],
        out_shape=[
            jax.ShapeDtypeStruct((BF, 256), BF16),
            jax.ShapeDtypeStruct((8, 128), F32),
        ],
        scratch_shapes=[pltpu.VMEM((32, 384), F32), pltpu.VMEM((32, 16, 128), F32)],
        compiler_params=params,
        name="correlate",
    )(place, v, r_all)
    c_all = exchange(c.reshape(N, 8, 256))

    z_sum = z_all.reshape(S, G, 4, 640).astype(F32).sum(axis=0)
    tables = tuple(jnp.asarray(t) for t in col_tables())
    upsampled = pl.pallas_call(
        finish_kernel,
        in_specs=[vmem] * 8,
        out_specs=vmem,
        out_shape=jax.ShapeDtypeStruct((4, 2 * SX), F32),
        scratch_shapes=[pltpu.VMEM((32, SX), F32)],
        compiler_params=params,
        name="finish",
    )(z_sum, total, *tables, jnp.asarray(nyquist_tables()))
    correlation = c_all.astype(F32).sum(axis=0) * (1.0 / math.sqrt(BF * SY * SX))
    return (upsampled, correlation)


def solution(mesh):
    return jax.shard_map(
        local,
        mesh=mesh,
        in_specs=(P("scan", "grp", None), P(), P(), P(), P("scan"), P(None, AXES)),
        out_specs=(P(AXES, None), P(AXES, None)),
        check_vma=False,
    )
```

time: 833 us -> 98.8 us (0.12)
  matrix products: 581 us -> 0 us
  blocking collectives: 138 us -> 0 us
  local copies, waits for them, and re-layouts: 45 us -> 4.65 us
  Pallas kernels: 0 us -> 34.2 us
  starting transfers between devices: 6.36 us -> 35.3 us
  loops' own time: 26.6 us -> 0 us
  other arithmetic: 20 us -> 3.65 us
  waiting for transfers between devices: 10.1 us -> 19.1 us
    dot_general x136 -> x0, matrix products: 581 us -> none  [the longest x120 544 us: low_dot(): return jnp.dot(left, right, preferred_element_type=jnp.float32)]
    unnamed x1 -> x0, blocking collectives: 107 us -> none
    pallas_call x0 -> x4, Pallas kernels: none -> 34.2 us  [the longest x1 14 us: local(): pl.pallas_call(shift_kernel, in_specs=[smem, vmem, vmem, vmem], out_specs...]
    all_to_all x2 -> x0, blocking collectives: 31.6 us -> none  [from_everyone(): lax.all_to_all(jnp.broadcast_to(value[None], (peers, *value.shape)), axis...]
    all_to_all x1 -> x4, starting transfers between devices: 6.36 us -> 35.3 us  [exchange(): return lax.all_to_all(value, AXES, split_axis=0, concat_axis=0, tiled=True)]
    another operation x1 -> x0, loops' own time: 26.6 us -> none  [local(): totals, correls = lax.scan(visit, start_totals, (pictures, shift_num.T))]
    gather x2 -> x0, local copies, waits for them, and re-layouts: 12.3 us -> none  [the longest x1 6.15 us: local(): gain_pixel = jnp.take(gain_frame, bf_index).astype(jnp.float32) / 4096.0]
    unnamed x19 -> x2, local copies, waits for them, and re-layouts: 10.6 us -> 0.01 us
  transfers between devices with their start and end apart: 1 -> 4, of which waited for: 1 -> 2; matrix products, arithmetic and copies ran while one was open for 5% -> 5% of each run, Pallas kernels for 0% -> 35%
where the time goes in v1:
time: 98.8 us; the launch traced here: 97.6 us
  starting transfers between devices  35.3 us (36%)
  Pallas kernels  34.2 us (35%)
  waiting for transfers between devices  19.1 us (19%)
  local copies, waits for them, and re-layouts  4.65 us (5%)
  other arithmetic  3.65 us (4%)
    all_to_all x4, starting transfers between devices, exchange(): return lax.all_to_all(value, AXES, split_axis=0, concat_axis=0, tiled=True)  35.3 us
    all_to_all x4, waiting for transfers between devices, exchange(): return lax.all_to_all(value, AXES, split_axis=0, concat_axis=0, tiled=True)  19.1 us
    pallas_call x1, Pallas kernels, local(): pl.pallas_call(shift_kernel, in_specs=[smem, vmem, vmem, vmem], out_specs...  14 us
    pallas_call x1, Pallas kernels, local(): pl.pallas_call(correct_kernel, grid=(YS,), in_specs=[smem, pl.BlockSpec((...  11.3 us
    pallas_call x1, Pallas kernels, local(): pl.pallas_call(correlate_kernel, in_specs=[smem, vmem, vmem], out_specs=[...  5.63 us
    pallas_call x1, Pallas kernels, local(): pl.pallas_call(finish_kernel, in_specs=[vmem] * 8, out_specs=vmem, out_sh...  3.3 us
    reshape x1, local copies, waits for them, and re-layouts, local(): z_all = exchange(z.reshape(N, 4, 640))  2.3 us
  transfers between devices with their start and end apart: 4, of which 2 were waited for; matrix products, arithmetic and copies ran while one was open for 5% of the time, Pallas kernels for 35%

profile of v1, /device:TPU:0, one launch (start us, length us, event | category | flops | bytes accessed | tf_op | source)
XLA Modules:
  0.0 97.6 jit_solution(17355073861269612655)
XLA Ops:
  0.7 0.7 tile.4
  1.3 0.1 tile.10
  1.4 0.7 broadcast_in_dim.22
  2.1 11.1 %all-to-all-start = ((s32[128,2,128]{2,1,0:T(2,128)}), s32[128,2,128]{2,1,0:T(2,128)S(1)}, u32[]{:S(2)}, u32[]{:S(2)}) async-start(s32[128,2,128]{2,1,0:T(2,128)} %broadcast_in_dim.22), calls=%async_computation | async-start | bytes 262144 | tf_op jit(solution)/shard_map/all_to_all | solution.py:279
  13.3 11.3 %correct.1 = (bf16[16,128,1024]{2,1,0:T(8,128)(2,1)}, f32[16,128]{1,0:T(8,128)}) custom-call(f32[16]{0:T(128)} %level.1, bf16[16,128,1024]{2,1,0:T(8,128)(2,1)} %frames.1, s32[288,128]{1,0:T(8,128)} %bitcast.12, s32[288,128]{1,0:T(8,128)} %bitcast.13, s32[1,1024]{1,0:T(1,128)} %bitcast.14), custom_call_target="tpu_custom_call" | custom-call | tf_op jit(solution)/shard_map/correct/pallas_call | solution.py:296
  24.6 0.7 convert_element_type.14
  25.3 0.0 all-to-all-done
  25.3 0.9 broadcast_in_dim.23
  26.2 9.8 %all-to-all-start.2 = ((bf16[128,16,128]{2,1,0:T(8,128)(2,1)}), bf16[128,16,128]{2,1,0:T(8,128)(2,1)S(1)}, u32[]{:S(2)}, u32[]{:S(2)}) async-start(bf16[128,16,128]{2,1,0:T(8,128)(2,1)} %broadcast_in_dim.23), calls=%async_computation.2 | async-start | bytes 1048576 | tf_op jit(solution)/shard_map/all_to_all | solution.py:279
  36.0 0.7 pad_add_fusion.strip.place
  36.6 0.6 bitcast_reduce_fusion.shifts
  37.3 14.0 %shift.1 = bf16[512,640]{1,0:T(8,128)(2,1)} custom-call(s32[2]{0:T(128)} %pad_add_fusion.strip.place, s32[8,2,128]{2,1,0:T(2,128)} %bitcast_reduce_fusion.shifts, bf16[16,128,1024]{2,1,0:T(8,128)(2,1)} %get-tuple-element.6.v, bf16[1024,128]{1,0:T(8,128)(2,1)} %constant.59.clone.rows), custom_call_target="tpu_custom_call" | custom-call | tf_op jit(solution)/shard_map/shift/pallas_call | solution.py:326
  51.2 2.3 %reshape.54 = bf16[128,4,640]{2,1,0:T(4,128)(2,1)} reshape(bf16[512,640]{1,0:T(8,128)(2,1)} %shift.1) | data formatting | bytes 1310720 | tf_op jit(solution)/shard_map/reshape | solution.py:340
  53.5 0.0 all-to-all-done.2.r_all
  53.5 0.0 copy-start
  53.5 9.8 %all-to-all-start.1 = ((bf16[128,4,640]{2,1,0:T(4,128)(2,1)}), bf16[128,4,640]{2,1,0:T(4,128)(2,1)S(1)}, u32[]{:S(2)}, u32[]{:S(2)}) async-start(bf16[128,4,640]{2,1,0:T(4,128)(2,1)} %reshape.54), calls=%async_computation.1 | async-start | bytes 1310720 | tf_op jit(solution)/shard_map/all_to_all | solution.py:279
  63.3 0.0 copy-done
  63.3 5.6 %correlate.1 = (bf16[1024,256]{1,0:T(8,128)(2,1)}, f32[8,128]{1,0:T(8,128)}) custom-call(s32[2]{0:T(128)} %pad_add_fusion.strip.place, bf16[16,128,1024]{2,1,0:T(8,128)(2,1)} %get-tuple-element.6.v, bf16[128,16,128]{2,1,0:T(8,128)(2,1)} %copy-done), custom_call_target="tpu_custom_call" | custom-call | tf_op jit(solution)/shard_map/correlate/pallas_call | solution.py:342
  68.9 9.5 %all-to-all-done.1 = bf16[128,4,640]{2,1,0:T(4,128)(2,1)S(1)} async-done(((bf16[128,4,640]{2,1,0:T(4,128)(2,1)}), bf16[128,4,640]{2,1,0:T(4,128)(2,1)S(1)}, u32[]{:S(2)}, u32[]{:S(2)}) %all-to-all-start.1) | async-done | bytes 655392 | tf_op jit(solution)/shard_map/all_to_all | solution.py:279
  78.5 4.6 %all-to-all-start.3 = ((bf16[128,8,256]{2,1,0:T(8,128)(2,1)}), bf16[128,8,256]{2,1,0:T(8,128)(2,1)S(1)}, u32[]{:S(2)}, u32[]{:S(2)}) async-start(bf16[128,8,256]{2,1,0:T(8,128)(2,1)} %bitcast.11), calls=%async_computation.3 | async-start | bytes 1048576 | tf_op jit(solution)/shard_map/all_to_all | solution.py:279
  83.1 0.9 convert_reduce_fusion.zs
  84.0 3.3 %finish.1 = f32[4,2048]{1,0:T(4,128)} custom-call(f32[8,4,640]{2,1,0:T(4,128)} %convert_reduce_fusion.zs, f32[8,128]{1,0:T(8,128)} %get-tuple-element.8.total, bf16[512,512]{1,0:T(8,128)(2,1)} %constant.60.clone.t1e, bf16[512,512]{1,0:T(8,128)(2,1)} %constant.61.clone.t1o, bf16[512,1024]{1,0:T(8,128)(2,1)} %constant.62.clone.t2e, ...), custom_call_target="tpu_custom_call" | custom-call | tf_op jit(solution)/shard_map/finish/pallas_call | solution.py:358
  87.3 9.6 %all-to-all-done.3 = bf16[128,8,256]{2,1,0:T(8,128)(2,1)S(1)} async-done(((bf16[128,8,256]{2,1,0:T(8,128)(2,1)}), bf16[128,8,256]{2,1,0:T(8,128)(2,1)S(1)}, u32[]{:S(2)}, u32[]{:S(2)}) %all-to-all-start.3) | async-done | bytes 524320 | tf_op jit(solution)/shard_map/all_to_all | solution.py:279
  96.8 0.1 convert_reduce_fusion.1
  97.0 0.6 broadcast_multiply_fusion
  (2 shorter events, 0.0 us)
Async XLA Ops:
  2.1 23.2 %all-to-all-start = ((s32[128,2,128]{2,1,0:T(2,128)}), s32[128,2,128]{2,1,0:T(2,128)S(1)}, u32[]{:S(2)}, u32[]{:S(2)}) async-start(s32[128,2,128]{2,1,0:T(2,128)} %broadcast_in_dim.22), calls=%async_computation | async-start | bytes 262144 | tf_op jit(solution)/shard_map/all_to_all | solution.py:279
  26.2 27.3 %all-to-all-start.2 = ((bf16[128,16,128]{2,1,0:T(8,128)(2,1)}), bf16[128,16,128]{2,1,0:T(8,128)(2,1)S(1)}, u32[]{:S(2)}, u32[]{:S(2)}) async-start(bf16[128,16,128]{2,1,0:T(8,128)(2,1)} %broadcast_in_dim.23), calls=%async_computation.2 | async-start | bytes 1048576 | tf_op jit(solution)/shard_map/all_to_all | solution.py:279
  53.5 9.8 %copy-start = (bf16[128,16,128]{2,1,0:T(8,128)(2,1)}, bf16[128,16,128]{2,1,0:T(8,128)(2,1)S(1)}, u32[]{:S(2)}) copy-start(bf16[128,16,128]{2,1,0:T(8,128)(2,1)S(1)} %all-to-all-done.2.r_all) | copy-start | bytes 1572868
  53.5 24.9 %all-to-all-start.1 = ((bf16[128,4,640]{2,1,0:T(4,128)(2,1)}), bf16[128,4,640]{2,1,0:T(4,128)(2,1)S(1)}, u32[]{:S(2)}, u32[]{:S(2)}) async-start(bf16[128,4,640]{2,1,0:T(4,128)(2,1)} %reshape.54), calls=%async_computation.1 | async-start | bytes 1310720 | tf_op jit(solution)/shard_map/all_to_all | solution.py:279
  78.5 18.4 %all-to-all-start.3 = ((bf16[128,8,256]{2,1,0:T(8,128)(2,1)}), bf16[128,8,256]{2,1,0:T(8,128)(2,1)S(1)}, u32[]{:S(2)}, u32[]{:S(2)}) async-start(bf16[128,8,256]{2,1,0:T(8,128)(2,1)} %bitcast.11), calls=%async_computation.3 | async-start | bytes 1048576 | tf_op jit(solution)/shard_map/all_to_all | solution.py:279

commit v2 on v1

v2 whole, which is shorter than its diff:
```python
import math

import jax
import jax.numpy as jnp
import ml_dtypes
import numpy as np
from jax import lax
from jax.experimental import pallas as pl
from jax.experimental.pallas import tpu as pltpu
from jax.sharding import PartitionSpec as P

SY = 256
SX = 1024
BF = 1024
DET = 36864
AXES = ("scan", "grp")
S = 16
G = 8
N = S * G
YS = SY // S
XS = SX // G
ROWS = DET // 128
BX = 17
PARTS = 4
F32 = jnp.float32
BF16 = jnp.bfloat16
NT = (((1,), (1,)), ((), ()))
TN = (((0,), (0,)), ((), ()))
MIB = 1024 * 1024


def iota(shape, dim):
    return lax.broadcasted_iota(jnp.int32, shape, dim)


def row_kernel():
    k = np.arange(-128, 128)
    q = np.arange(1024)
    d = np.cos(2 * np.pi * k[None, :] * q[:, None] / 1024).sum(1) / 256
    r = np.arange(2048) % 1024
    yp = 4 * (r // 8) + r % 4
    yy = np.repeat(np.arange(32), 4)
    fy = np.tile(np.arange(4), 32)
    return d[(2 * yp[:, None] - fy[None, :] - 4 * (yy[None, :] - 8)) % 1024].astype(ml_dtypes.bfloat16)


def col_tables():
    x = np.arange(512) - 8
    out = []
    for par in (0, 1):
        k = 2 * np.arange(256) + par
        ang = 2 * np.pi * ((x[:, None] * k[None, :]) % 1024) / 1024
        c, s = np.cos(ang), np.sin(ang)
        if par == 0:
            s[:, 0] = np.where(x % 2 == 0, 1.0, -1.0)
        out.append(np.concatenate([c, s], 1).astype(ml_dtypes.bfloat16))
    xp = np.arange(1024)
    for par in (0, 1):
        k = 2 * np.arange(256) + par
        w = np.where(k == 0, 1.0, 2.0)[:, None]
        ang = 2 * np.pi * ((k[:, None] * xp[None, :]) % 2048) / 2048
        out.append(np.concatenate([w * np.cos(ang), -w * np.sin(ang)], 0).astype(ml_dtypes.bfloat16))
    return out


def phase_tables():
    out = np.zeros((2, 2, 2, 8, 256), np.float32)
    for par in (0, 1):
        k = 2 * np.arange(256) + par
        for fx in range(4):
            rows = slice(4 * (fx >> 1), 4 * (fx >> 1) + 4)
            out[par, 0, fx & 1, rows] = np.cos(2 * np.pi * k * fx / 4096)
            out[par, 1, fx & 1, rows] = np.sin(2 * np.pi * k * fx / 4096)
    return out.reshape(64, 256)


def nyquist_tables():
    w = np.zeros((2, 8, 128), np.float32)
    for i in range(8):
        for fx in range(4):
            for fy in range(4):
                sy = math.sin(math.pi * (2 * (i % 4) - fy) / 4) / 256
                for base in (64, 80):
                    w[0, i, base + fx * 4 + fy] = sy * math.sin(math.pi * fx / 4)
                    w[1, i, base + fx * 4 + fy] = -sy * math.cos(math.pi * fx / 4)
    v = np.zeros((2, 2, 8, 128), np.float32)
    for fx in range(4):
        rows = slice(4 * (fx >> 1), 4 * (fx >> 1) + 4)
        v[fx & 1, 0, rows] = math.cos(math.pi * fx / 4)
        v[fx & 1, 1, rows] = math.sin(math.pi * fx / 4)
    return np.concatenate([w.reshape(16, 128), v.reshape(32, 128)], 0)


def three_parts(value):
    high = value.astype(BF16).astype(F32)
    mid = (value - high).astype(BF16).astype(F32)
    return high, mid, value - high - mid


def reference_kernel(place, level, amounts, frames, dark, gain, index, send, r_out, pixel_out, held, sems):
    def part(i):
        span = pl.ds(i * (YS // PARTS), YS // PARTS)
        return pltpu.make_async_copy(frames.at[span], held.at[span], sems.at[i])

    for i in range(PARTS):
        part(i).start()
    g = gain[...]
    table = jnp.concatenate(
        [dark[...].astype(F32), (g >> 5).astype(F32), (g & 31).astype(F32)], axis=1
    ).astype(BF16)
    idx = index[...]
    hot = (iota((ROWS, BF), 0) == (idx >> 7)).astype(F32).astype(BF16)
    picked = lax.dot_general(table, hot, TN, preferred_element_type=F32)
    mine = iota((128, BF), 0) == (idx & 127)

    def pick(i):
        return jnp.sum(jnp.where(mine, picked[128 * i : 128 * (i + 1)], 0.0), axis=0, keepdims=True)

    dark_px = pick(0) * (1.0 / 256.0)
    gain_px = (pick(1) * 32.0 + pick(2)) * (1.0 / 4096.0)
    pixel_out[0:1, :] = dark_px
    pixel_out[1:2, :] = gain_px
    offset = jnp.sum(dark_px * gain_px)
    for i in range(PARTS):
        part(i).wait()
        for y in range(i * (YS // PARTS), (i + 1) * (YS // PARTS)):
            acc = None
            for t in range(8):
                lanes = slice(128 * t, 128 * (t + 1))
                term = held[y, :, lanes].astype(F32) * gain_px[:, lanes]
                acc = term if acc is None else acc + term
            high = acc.astype(BF16)
            low = (acc - high.astype(F32)).astype(BF16)
            total = lax.dot_general(
                jnp.ones((8, 256), BF16), jnp.concatenate([high, low], 1), NT, preferred_element_type=F32
            )
            r_out[y : y + 1, :] = total[0:1] - level[y] * offset
    s = place[0]
    g = place[1]
    r = r_out[...]
    center = jnp.sum(r) * (1.0 / (YS * XS))
    rest = r - center
    lane = iota((1, 128), 1)
    base = 8 * lax.rem(s * G + g, 16)
    row_sy = jnp.zeros((1, 128), F32)
    row_sx = jnp.zeros((1, 128), F32)
    for i in range(8):
        row_sy = jnp.where(lane == base + i, amounts[0, i].astype(F32), row_sy)
        row_sx = jnp.where(lane == base + i, amounts[1, i].astype(F32), row_sx)
    row_center = jnp.zeros((1, 128), F32)
    for i, piece in enumerate(three_parts(jnp.full((1, 128), center))):
        row_center = jnp.where(lane == i, piece, row_center)
    foot = jnp.concatenate([row_sy, row_sx, row_center, jnp.zeros((5, 128), F32)], axis=0)

    def chunk(top):
        return jnp.concatenate([top, foot], axis=0).astype(BF16)

    plain = chunk(jnp.zeros((8, 128), F32))
    for d in range(N):
        send[d] = plain
    lanes = iota((8, 128), 1)
    sides = jnp.where((lanes >= 32) & (lanes < 96), pltpu.roll(rest[8:16], 64, 1), rest[0:8])
    for ds, top in ((S - 1, rest[0:8]), (0, sides), (1, rest[8:16])):
        for dg in (G - 1, 0, 1):
            if ds or dg:
                send[lax.rem(s + ds, S) * G + lax.rem(g + dg, G)] = chunk(top)


def correct_kernel(level, frames, pixel, v_out):
    y = pl.program_id(0) * (YS // PARTS)
    for i in range(YS // PARTS):
        value = (frames[i].astype(F32) - level[y + i] * pixel[0:1, :]) * pixel[1:2, :]
        v_out[i] = value.astype(BF16)


def strip_kernel(
    place, recv, r_own, v_hbm, rows, out, total_out, v, moved, hot, main, over, window, table, sems
):
    s = place[0]
    g = place[1]

    def part(i):
        span = pl.ds(i * (YS // PARTS), YS // PARTS)
        return pltpu.make_async_copy(v_hbm.at[span], v.at[span], sems.at[i])

    for i in range(PARTS):
        part(i).start()

    centers = jnp.zeros((8, 128), F32)
    feet = []
    for t in range(8):
        foot = jnp.zeros((8, 128), F32)
        for i in range(16):
            foot = foot + recv[16 * t + i].astype(F32)[8:16]
        feet.append(foot)
        centers = centers + foot
    mean = jnp.sum(jnp.where(iota((1, 128), 1) < 3, centers[2:3], 0.0), axis=1, keepdims=True) * (1.0 / N)
    total_out[...] = jnp.broadcast_to(mean * (SY * SX), (8, 128))

    def neighbour(ds, dg):
        got = recv[lax.rem(s + ds, S) * G + lax.rem(g + dg, G)].astype(F32)
        center = jnp.sum(jnp.where(iota((1, 128), 1) < 3, got[10:11], 0.0), axis=1, keepdims=True)
        return got[0:8] + (center - mean)

    for j, dg in enumerate((G - 1, 0, 1)):
        lanes = slice(128 * j, 128 * (j + 1))
        window[0:8, lanes] = neighbour(S - 1, dg)
        window[24:32, lanes] = neighbour(1, dg)
        if dg:
            side = neighbour(0, dg)
            window[8:16, lanes] = side
            window[16:24, lanes] = pltpu.roll(side, 64, 1)
        else:
            window[8:24, lanes] = r_own[...] - mean
    for b in range(16):
        table[b] = pltpu.roll(window[...], (b - 8) % 384, 1)[:, 128:256]

    row = iota((BX * 16, 128), 0)
    for t in range(8):
        sy = feet[t][0:1].astype(jnp.int32)
        sx = feet[t][1:2].astype(jnp.int32)
        code = ((sx >> 2) + 8) * 16 + (sx & 3) * 4 + (sy & 3)
        hot[:, 128 * t : 128 * (t + 1)] = (row == code).astype(F32).astype(BF16)

    for i in range(PARTS):
        part(i).wait()

    acc = jnp.zeros((256, BF), F32)
    for j in range(0, YS, 2):
        left = jnp.concatenate(
            [
                jnp.concatenate([table[b, i + 1 : i + 17, :] for b in range(16)], axis=0).astype(BF16)
                for i in (j, j + 1)
            ],
            axis=1,
        )
        acc = acc + jnp.dot(left, v[j : j + 2].reshape(256, BF), preferred_element_type=F32)
    out[:, 384:640] = acc.T.astype(BF16)

    for t in range(8):
        lanes = slice(128 * t, 128 * (t + 1))
        by = (feet[t][0:1].astype(jnp.int32) >> 2) + 8
        masks = [
            jnp.broadcast_to(((by >> b) & 1).astype(F32), (16, 128)).astype(BF16) > 0.5 for b in range(5)
        ]

        def barrel(i, _, lanes=lanes, masks=masks):
            x0 = pl.multiple_of(i * 16, 16)
            rows_in = [v[y, pl.ds(x0, 16), lanes] for y in range(YS)]
            zero = jnp.zeros((16, 128), BF16)
            for b in range(5):
                step = 1 << b
                size = min(len(rows_in) + step, 32)
                old = rows_in
                rows_in = [
                    jnp.where(
                        masks[b],
                        old[j - step] if 0 <= j - step < len(old) else zero,
                        old[j] if j < len(old) else zero,
                    )
                    for j in range(size)
                ]
            for j in range(32):
                moved[j, pl.ds(x0, 16), lanes] = rows_in[j]
            return 0

        lax.fori_loop(0, 8, barrel, 0)

    lane = iota((16, 128), 1)

    def group(j, _):
        block = moved[pl.ds(2 * j, 2)].reshape(256, BF)
        sums = lax.dot_general(hot[...], block, NT, preferred_element_type=F32)
        for h in range(2):
            acc_main = sums[0:16, 128 * h : 128 * (h + 1)]
            acc_over = jnp.zeros((16, 128), F32)
            for b in range(1, BX):
                piece = pltpu.roll(sums[16 * b : 16 * (b + 1), 128 * h : 128 * (h + 1)], b, 1)
                acc_main = acc_main + jnp.where(lane >= b, piece, 0.0)
                acc_over = acc_over + jnp.where(lane < b, piece, 0.0)
            main[2 * j + h] = acc_main
            over[2 * j + h] = acc_over
        return 0

    lax.fori_loop(0, 16, group, 0)

    sign_y = 1.0 - 2.0 * (iota((32, 16, 128), 0) & 1).astype(F32)
    sign_x = 1.0 - 2.0 * (iota((8, 128), 1) & 1).astype(F32)
    folded = jnp.sum((main[...] + over[...]) * sign_y, axis=0)
    folded = jnp.concatenate([jnp.zeros((64, 128), F32), folded, jnp.zeros((48, 128), F32)], axis=0)
    q_row = lax.dot_general(sign_x, folded, NT, precision=lax.Precision.HIGHEST, preferred_element_type=F32)[0:1]
    q_high = q_row.astype(BF16).astype(F32)
    q_row = q_high + pltpu.roll(q_row - q_high, 16, 1)

    col = iota((128, 512), 1)
    spread = ((iota((128, 512), 0) >> 2) == (col >> 4)) & ((iota((128, 512), 0) & 3) == (col & 3))
    start = pl.multiple_of(1024 - 64 * s, 64)
    left = jnp.dot(rows[pl.ds(start, 1024), :], spread.astype(F32).astype(BF16), preferred_element_type=F32)
    left = jnp.where(
        ((iota((1024, 512), 0) >> 2) & 1) == ((iota((1024, 512), 1) >> 3) & 1), left, 0.0
    ).astype(BF16)
    kind = (iota((512, 128), 0) >> 2) & 1
    u_main = main[...].reshape(512, 128)
    u_over = over[...].reshape(512, 128)
    first = jnp.where(kind == 0, u_over, 0.0)
    second = jnp.where(kind == 1, u_over, 0.0)
    right = jnp.concatenate(
        [
            jnp.where(kind == 0, u_main, 0.0),
            jnp.where(kind == 1, u_main, 0.0),
            first + pltpu.roll(second, 16, 1),
        ],
        axis=1,
    ).astype(BF16)
    z = jnp.dot(left, right, preferred_element_type=F32)
    out[:, 0:256] = z[:, 0:256].astype(BF16)
    out[:, 256:384] = (z[:, 256:384] + q_row).astype(BF16)


def finish_kernel(recv, total, t1e, t1o, t2e, t2o, phase, nyquist, out, corr_out, full):
    corr = jnp.zeros((8, 256), F32)
    sums = []
    for g in range(G):
        acc = jnp.zeros((8, 384), F32)
        for s in range(S):
            got = recv[s * G + g].astype(F32)
            acc = acc + got[:, 0:384]
            corr = corr + got[:, 384:640]
        sums.append(acc)
    n = iota((256, 256), 0)
    m = iota((256, 256), 1)
    order = ((n >> 4) == (m & 15)) & ((15 - (n & 15)) == (m >> 4))
    corr_out[...] = jnp.dot(
        corr * (1.0 / math.sqrt(BF * SY * SX)),
        order.astype(F32),
        precision=lax.Precision.HIGHEST,
        preferred_element_type=F32,
    )
    lane = iota((8, 128), 1)
    q_rows = jnp.zeros((8, 128), F32)
    for g in range(G):
        tail = sums[(g - 1) % G][:, 256:384]
        q_rows = q_rows + tail
        lanes = slice(128 * g, 128 * (g + 1))
        full[0:8, lanes] = sums[g][:, 0:128] + jnp.where(lane < 16, tail, 0.0)
        full[8:16, lanes] = sums[g][:, 128:256] + jnp.where(lane < 16, pltpu.roll(tail, 112, 1), 0.0)
    low = full[:, 0:512]
    high = full[:, 512:1024]
    lane_e = iota((8, 256), 1)
    results = []
    wave_cos = jnp.sum(q_rows * nyquist[0:8, :], axis=1, keepdims=True)
    wave_sin = jnp.sum(q_rows * nyquist[8:16, :], axis=1, keepdims=True)

    def both(value):
        return value + pltpu.roll(value, 4, 0)

    real_cos = jnp.zeros((8, 128), F32)
    real_sin = jnp.zeros((8, 128), F32)
    for par, (t1, t2, part) in enumerate(((t1e, t2e, low + high), (t1o, t2o, low - high))):
        spec = jnp.dot(part.astype(BF16), t1[...], preferred_element_type=F32)
        re = jnp.zeros((8, 256), F32)
        im = jnp.zeros((8, 256), F32)
        for fxl in range(2):
            c = spec[8 * fxl : 8 * fxl + 8, 0:256]
            s = spec[8 * fxl : 8 * fxl + 8, 256:512]
            if par == 0:
                ny = s[:, 0:1]
                real_cos = real_cos + ny * nyquist[16 + 16 * fxl : 24 + 16 * fxl, :]
                real_sin = real_sin + ny * nyquist[24 + 16 * fxl : 32 + 16 * fxl, :]
                s = jnp.where(lane_e == 0, 0.0, s)
            pc = phase[32 * par + 8 * fxl : 32 * par + 8 * fxl + 8, :]
            ps = phase[32 * par + 16 + 8 * fxl : 32 * par + 24 + 8 * fxl, :]
            re = re + c * pc - s * ps
            im = im - (s * pc + c * ps)
        re = both(re)
        im = both(im)
        if par == 0:
            re = jnp.where(lane_e == 0, re - total[0:1, 0:1] * (1.0 / SY), re)
        coef = jnp.concatenate([re, im], axis=1).astype(BF16)
        results.append(jnp.dot(coef, t2[...], preferred_element_type=F32))
    wave_cos = wave_cos + both(real_cos)[:, 0:1]
    wave_sin = wave_sin + both(real_sin)[:, 0:1]
    turn = iota((8, 1024), 1) & 3
    wave = wave_cos * jnp.where(turn == 0, 1.0, jnp.where(turn == 2, -1.0, 0.0))
    wave = wave + wave_sin * jnp.where(turn == 1, 1.0, jnp.where(turn == 3, -1.0, 0.0))
    scale = 1.0 / (SX * math.sqrt(BF))
    even = results[0] + wave
    odd = results[1]
    out[:, 0:1024] = ((even + odd) * scale)[0:4]
    out[:, 1024:2048] = ((even - odd) * scale)[0:4]


def exchange(value):
    return lax.all_to_all(value, AXES, split_axis=0, concat_axis=0, tiled=True)


def limit(mib):
    return pltpu.CompilerParams(vmem_limit_bytes=mib * MIB)


def local(frames, dark_frame, gain_frame, bf_index, row_level, shift_num):
    place = jnp.stack([lax.axis_index("scan"), lax.axis_index("grp")]).astype(jnp.int32)
    smem = pl.BlockSpec(memory_space=pltpu.SMEM)
    vmem = pl.BlockSpec(memory_space=pltpu.VMEM)
    hbm = pl.BlockSpec(memory_space=pl.ANY)

    send, r_own, pixel = pl.pallas_call(
        reference_kernel,
        in_specs=[smem, smem, smem, hbm, vmem, vmem, vmem],
        out_specs=[vmem, vmem, vmem],
        out_shape=[
            jax.ShapeDtypeStruct((N, 16, 128), BF16),
            jax.ShapeDtypeStruct((YS, XS), F32),
            jax.ShapeDtypeStruct((8, BF), F32),
        ],
        scratch_shapes=[pltpu.VMEM((YS, XS, BF), BF16), pltpu.SemaphoreType.DMA((PARTS,))],
        compiler_params=limit(60),
        name="reference_image",
    )(
        place,
        row_level,
        shift_num,
        frames,
        dark_frame.reshape(ROWS, 128),
        gain_frame.reshape(ROWS, 128),
        bf_index.reshape(1, BF),
    )
    recv = exchange(send)
    v = pl.pallas_call(
        correct_kernel,
        grid=(PARTS,),
        in_specs=[
            smem,
            pl.BlockSpec((YS // PARTS, XS, BF), lambda i: (i, 0, 0)),
            pl.BlockSpec((8, BF), lambda i: (0, 0)),
        ],
        out_specs=pl.BlockSpec((YS // PARTS, XS, BF), lambda i: (i, 0, 0)),
        out_shape=jax.ShapeDtypeStruct((YS, XS, BF), BF16),
        compiler_params=limit(24),
        cost_estimate=pl.CostEstimate(flops=8 * YS * XS * BF, bytes_accessed=4 * YS * XS * BF, transcendentals=0),
        name="correct",
    )(row_level, frames, pixel)
    sums, total = pl.pallas_call(
        strip_kernel,
        in_specs=[smem, vmem, vmem, hbm, vmem],
        out_specs=[vmem, vmem],
        out_shape=[
            jax.ShapeDtypeStruct((BF, 640), BF16),
            jax.ShapeDtypeStruct((8, 128), F32),
        ],
        scratch_shapes=[
            pltpu.VMEM((YS, XS, BF), BF16),
            pltpu.VMEM((32, XS, BF), BF16),
            pltpu.VMEM((BX * 16, BF), BF16),
            pltpu.VMEM((32, 16, 128), F32),
            pltpu.VMEM((32, 16, 128), F32),
            pltpu.VMEM((32, 384), F32),
            pltpu.VMEM((16, 32, 128), F32),
            pltpu.SemaphoreType.DMA((PARTS,)),
        ],
        compiler_params=limit(30),
        name="strip",
    )(place, recv, r_own, v, jnp.asarray(row_kernel()))
    parts = exchange(sums.reshape(N, 8, 640))
    tables = [jnp.asarray(t) for t in (*col_tables(), phase_tables(), nyquist_tables())]
    return pl.pallas_call(
        finish_kernel,
        in_specs=[vmem] * 8,
        out_specs=[vmem, vmem],
        out_shape=[
            jax.ShapeDtypeStruct((4, 2 * SX), F32),
            jax.ShapeDtypeStruct((8, 256), F32),
        ],
        scratch_shapes=[pltpu.VMEM((16, SX), F32)],
        compiler_params=limit(24),
        name="finish",
    )(parts, total, *tables)


def solution(mesh):
    return jax.shard_map(
        local,
        mesh=mesh,
        in_specs=(P("scan", "grp", None), P(), P(), P(), P("scan"), P(None, AXES)),
        out_specs=(P(AXES, None), P(AXES, None)),
        check_vma=False,
    )
```

time: 98.8 us -> 76 us (0.77)
  blocking collectives: 0 us -> 26.2 us
  starting transfers between devices: 35.3 us -> 11.1 us
  Pallas kernels: 34.2 us -> 21.3 us
  waiting for transfers between devices: 19.1 us -> 7.14 us
  local copies, waits for them, and re-layouts: 4.65 us -> 8.17 us
  other arithmetic: 3.65 us -> 0.58 us
    all_to_all x0 -> x1, blocking collectives: none -> 26.2 us  [exchange(): return lax.all_to_all(value, AXES, split_axis=0, concat_axis=0, tiled=True)]
    all_to_all x4 -> x1, starting transfers between devices: 35.3 us -> 11.1 us  [exchange(): return lax.all_to_all(value, AXES, split_axis=0, concat_axis=0, tiled=True)]
    pallas_call x4, Pallas kernels: 34.2 us -> 21.3 us  [the longest x1 13.2 us: local(): pl.pallas_call(strip_kernel, in_specs=[smem, vmem, vmem, hbm, vmem], out_...]
    all_to_all x4 -> x1, waiting for transfers between devices: 19.1 us -> 7.14 us  [exchange(): return lax.all_to_all(value, AXES, split_axis=0, concat_axis=0, tiled=True)]
    unnamed x2 -> x28, local copies, waits for them, and re-layouts: 0.01 us -> 8.17 us
    reshape x1 -> x0, local copies, waits for them, and re-layouts: 2.3 us -> none  [local(): z_all = exchange(z.reshape(N, 4, 640))]
    reduce_sum x3 -> x0, other arithmetic: 1.67 us -> none  [the longest x1 0.9 us: local(): z_sum = z_all.reshape(S, G, 4, 640).astype(F32).sum(axis=0)]
    broadcast_in_dim x2 -> x0, local copies, waits for them, and re-layouts: 1.58 us -> none  [the longest x1 0.9 us: local(): r_all = exchange(jnp.broadcast_to(r.astype(BF16)[None], (N, YS, XS)))]
  transfers between devices with their start and end apart: 4 -> 1, of which waited for: 2 -> 1; matrix products, arithmetic and copies ran while one was open for 5% -> 0% of each run, Pallas kernels for 35% -> 2%
where the time goes in v2:
time: 76 us; the launch traced here: 75.3 us
  blocking collectives  26.2 us (34%)
  Pallas kernels  21.3 us (28%)
  starting transfers between devices  11.1 us (15%)
  local copies, waits for them, and re-layouts  8.17 us (11%)
  waiting for transfers between devices  7.14 us (9%)
  between operations  0.76 us (1%)
    all_to_all x1, blocking collectives, exchange(): return lax.all_to_all(value, AXES, split_axis=0, concat_axis=0, tiled=True)  26.2 us
    pallas_call x1, Pallas kernels, local(): pl.pallas_call(strip_kernel, in_specs=[smem, vmem, vmem, hbm, vmem], out_...  13.2 us
    all_to_all x1, starting transfers between devices, exchange(): return lax.all_to_all(value, AXES, split_axis=0, concat_axis=0, tiled=True)  11.1 us
    unnamed x28, local copies, waits for them, and re-layouts  8.17 us
    all_to_all x1, waiting for transfers between devices, exchange(): return lax.all_to_all(value, AXES, split_axis=0, concat_axis=0, tiled=True)  7.14 us
    pallas_call x1, Pallas kernels, local(): pl.pallas_call(reference_kernel, in_specs=[smem, smem, smem, hbm, vmem, v...  4.76 us
    pallas_call x1, Pallas kernels, local(): pl.pallas_call(correct_kernel, grid=(PARTS,), in_specs=[smem, pl.BlockSpe...  1.64 us
    pallas_call x1, Pallas kernels, local(): pl.pallas_call(finish_kernel, in_specs=[vmem] * 8, out_specs=[vmem, vmem]...  1.62 us
  transfers between devices with their start and end apart: 1, of which 1 were waited for; matrix products, arithmetic and copies ran while one was open for 0% of the time, Pallas kernels for 2%

profile of v2, /device:TPU:0, one launch (start us, length us, event | category | flops | bytes accessed | tf_op | source)
XLA Modules:
  0.0 75.3 jit_solution(3872363264940280764)
XLA Ops:
  0.6 0.0 copy-start.12
  0.6 0.6 pad_add_fusion.place
  1.2 4.8 %reference_image.1 = (bf16[128,16,128]{2,1,0:T(8,128)(2,1)}, f32[16,128]{1,0:T(8,128)}, f32[8,1024]{1,0:T(8,128)}) custom-call(s32[2]{0:T(128)} %pad_add_fusion.place, f32[16]{0:T(128)} %level.3, s32[2,8]{1,0:T(2,128)} %amounts.1, bf16[16,128,1024]{2,1,0:T(8,128)(2,1)} %frames.3, s32[288,128]{1,0:T(8,128)} %bitcast.7, s32[288,128]{1,0:T(8,128)} %bitcast.8, ...), custom_call_target="tpu_custom_call" | custom-call | tf_op jit(solution)/shard_map/reference_image/pallas_call | solution.py:407
  6.0 11.1 %all-to-all-start = ((bf16[128,16,128]{2,1,0:T(8,128)(2,1)}), bf16[128,16,128]{2,1,0:T(8,128)(2,1)S(1)}, u32[]{:S(2)}, u32[]{:S(2)}) async-start(bf16[128,16,128]{2,1,0:T(8,128)(2,1)} %get-tuple-element.7), calls=%async_computation | async-start | bytes 1048576 | tf_op jit(solution)/shard_map/all_to_all | solution.py:394
  17.2 0.0 copy-done.12
  17.2 0.0 copy-start
  17.2 2.2 %copy-done = bf16[16,128,1024]{2,1,0:T(8,128)(2,1)S(1)} copy-done((bf16[16,128,1024]{2,1,0:T(8,128)(2,1)S(1)}, bf16[16,128,1024]{2,1,0:T(8,128)(2,1)}, u32[]{:S(2)}) %copy-start) | copy-done | bytes 4194328
  19.4 0.0 copy-start.9
  19.4 0.8 %copy-done.9 = f32[8,1024]{1,0:T(8,128)S(1)} copy-done((f32[8,1024]{1,0:T(8,128)S(1)}, f32[8,1024]{1,0:T(8,128)}, u32[]{:S(2)}) %copy-start.9) | copy-done | bytes 32792
  20.1 0.0 copy-start.11
  20.1 0.0 copy-start.13
  20.1 0.0 copy-start.3
  20.1 0.0 copy-start.5
  20.1 0.0 copy-start.8
  20.2 0.0 copy-start.10
  20.2 1.6 %correct.1.v_hbm = bf16[16,128,1024]{2,1,0:T(8,128)(2,1)S(1)} custom-call(f32[16]{0:T(128)S(1)} %copy-done.12, bf16[16,128,1024]{2,1,0:T(8,128)(2,1)S(1)} %copy-done, f32[8,1024]{1,0:T(8,128)S(1)} %copy-done.9), custom_call_target="tpu_custom_call" | custom-call | flops 16777216 | bytes 8388608 | tf_op jit(solution)/shard_map/correct/pallas_call | solution.py:429
  21.8 0.0 copy-start.1
  21.8 2.0 %copy-done.1 = bf16[16,128,1024]{2,1,0:T(8,128)(2,1)} copy-done((bf16[16,128,1024]{2,1,0:T(8,128)(2,1)}, bf16[16,128,1024]{2,1,0:T(8,128)(2,1)S(1)}, u32[]{:S(2)}) %copy-start.1) | copy-done | bytes 4194328
  23.8 7.1 %all-to-all-done.recv = bf16[128,16,128]{2,1,0:T(8,128)(2,1)S(1)} async-done(((bf16[128,16,128]{2,1,0:T(8,128)(2,1)}), bf16[128,16,128]{2,1,0:T(8,128)(2,1)S(1)}, u32[]{:S(2)}, u32[]{:S(2)}) %all-to-all-start) | async-done | bytes 524320 | tf_op jit(solution)/shard_map/all_to_all | solution.py:394
  30.9 0.0 copy-done.11
  30.9 0.0 copy-done.13
  30.9 2.2 %copy-done.2 = bf16[16,128,1024]{2,1,0:T(8,128)(2,1)S(1)} copy-done((bf16[16,128,1024]{2,1,0:T(8,128)(2,1)S(1)}, bf16[16,128,1024]{2,1,0:T(8,128)(2,1)}, u32[]{:S(2)}) %copy-start.2) | copy-done | bytes 4194328
  33.1 1.0 %copy-done.7 = bf16[2048,128]{1,0:T(8,128)(2,1)S(1)} copy-done((bf16[2048,128]{1,0:T(8,128)(2,1)S(1)}, bf16[2048,128]{1,0:T(8,128)(2,1)}, u32[]{:S(2)}) %copy-start.7) | copy-done | bytes 524312
  34.2 13.2 %strip.1 = (bf16[1024,640]{1,0:T(8,128)(2,1)S(1)}, f32[8,128]{1,0:T(8,128)S(1)}) custom-call(s32[2]{0:T(128)S(1)} %copy-done.13, bf16[128,16,128]{2,1,0:T(8,128)(2,1)S(1)} %all-to-all-done.recv, f32[16,128]{1,0:T(8,128)S(1)} %copy-done.11, bf16[16,128,1024]{2,1,0:T(8,128)(2,1)S(1)} %copy-done.2, bf16[2048,128]{1,0:T(8,128)(2,1)S(1)} %copy-done.7), custom_call_target="tpu_custom_call" | custom-call | tf_op jit(solution)/shard_map/strip/pallas_call | solution.py:443
  47.4 26.2 %all_to_all.10.recv = bf16[128,8,640]{2,1,0:T(8,128)(2,1)S(1)} all-to-all(bf16[128,8,640]{2,1,0:T(8,128)(2,1)S(1)} %bitcast.6), channel_id=1, replica_groups=mesh['scan'=16,'grp'=8] {'scan','grp'}, dimensions={0} | all-to-all | bytes 2621440 | tf_op jit(solution)/shard_map/all_to_all | solution.py:394
  73.6 0.0 copy-done.3
  73.6 0.0 copy-done.4
  73.6 0.0 copy-done.5
  73.6 0.0 copy-done.8
  73.7 0.0 copy-done.10
  73.7 0.0 copy-done.6
  73.7 1.6 %finish.1 = (f32[4,2048]{1,0:T(4,128)}, f32[8,256]{1,0:T(8,128)}) custom-call(bf16[128,8,640]{2,1,0:T(8,128)(2,1)S(1)} %all_to_all.10.recv, f32[8,128]{1,0:T(8,128)S(1)} %get-tuple-element.11.total, bf16[512,512]{1,0:T(8,128)(2,1)S(1)} %copy-done.6, bf16[512,512]{1,0:T(8,128)(2,1)S(1)} %copy-done.5, bf16[512,1024]{1,0:T(8,128)(2,1)S(1)} %copy-done.4, ...), custom_call_target="tpu_custom_call" | custom-call | tf_op jit(solution)/shard_map/finish/pallas_call | solution.py:466
  (4 shorter events, 0.0 us)
Async XLA Ops:
  0.6 16.5 %copy-start.12 = (f32[16]{0:T(128)S(1)}, f32[16]{0:T(128)}, u32[]{:S(2)}) copy-start(f32[16]{0:T(128)} %level.3) | copy-start | bytes 196
  6.0 24.9 %all-to-all-start = ((bf16[128,16,128]{2,1,0:T(8,128)(2,1)}), bf16[128,16,128]{2,1,0:T(8,128)(2,1)S(1)}, u32[]{:S(2)}, u32[]{:S(2)}) async-start(bf16[128,16,128]{2,1,0:T(8,128)(2,1)} %get-tuple-element.7), calls=%async_computation | async-start | bytes 1048576 | tf_op jit(solution)/shard_map/all_to_all | solution.py:394
  17.2 2.2 %copy-start = (bf16[16,128,1024]{2,1,0:T(8,128)(2,1)S(1)}, bf16[16,128,1024]{2,1,0:T(8,128)(2,1)}, u32[]{:S(2)}) copy-start(bf16[16,128,1024]{2,1,0:T(8,128)(2,1)} %frames.3) | copy-start | bytes 12582916
  19.4 0.8 %copy-start.9 = (f32[8,1024]{1,0:T(8,128)S(1)}, f32[8,1024]{1,0:T(8,128)}, u32[]{:S(2)}) copy-start(f32[8,1024]{1,0:T(8,128)} %get-tuple-element.9.pixel) | copy-start | bytes 98308
  20.1 10.8 %copy-start.11 = (f32[16,128]{1,0:T(8,128)S(1)}, f32[16,128]{1,0:T(8,128)}, u32[]{:S(2)}) copy-start(f32[16,128]{1,0:T(8,128)} %get-tuple-element.8.r_own) | copy-start | bytes 24580
  20.1 10.8 %copy-start.13 = (s32[2]{0:T(128)S(1)}, s32[2]{0:T(128)}, u32[]{:S(2)}) copy-start(s32[2]{0:T(128)} %pad_add_fusion.place) | copy-start | bytes 28
  20.1 53.5 %copy-start.3 = (bf16[512,1024]{1,0:T(8,128)(2,1)S(1)}, bf16[512,1024]{1,0:T(8,128)(2,1)}, u32[]{:S(2)}) copy-start(bf16[512,1024]{1,0:T(8,128)(2,1)} %constant.27.clone.t2o) | copy-start | bytes 3145732
  20.1 53.5 %copy-start.4 = (bf16[512,1024]{1,0:T(8,128)(2,1)S(1)}, bf16[512,1024]{1,0:T(8,128)(2,1)}, u32[]{:S(2)}) copy-start(bf16[512,1024]{1,0:T(8,128)(2,1)} %constant.26.clone.t2e) | copy-start | bytes 3145732
  20.1 53.5 %copy-start.5 = (bf16[512,512]{1,0:T(8,128)(2,1)S(1)}, bf16[512,512]{1,0:T(8,128)(2,1)}, u32[]{:S(2)}) copy-start(bf16[512,512]{1,0:T(8,128)(2,1)} %constant.25.clone.t1o) | copy-start | bytes 1572868
  20.1 53.5 %copy-start.8 = (f32[64,256]{1,0:T(8,128)S(1)}, f32[64,256]{1,0:T(8,128)}, u32[]{:S(2)}) copy-start(f32[64,256]{1,0:T(8,128)} %constant.28.clone.phase) | copy-start | bytes 196612
  20.2 53.5 %copy-start.10 = (f32[48,128]{1,0:T(8,128)S(1)}, f32[48,128]{1,0:T(8,128)}, u32[]{:S(2)}) copy-start(f32[48,128]{1,0:T(8,128)} %constant.29.clone.nyquist) | copy-start | bytes 73732
  21.8 2.0 %copy-start.1 = (bf16[16,128,1024]{2,1,0:T(8,128)(2,1)}, bf16[16,128,1024]{2,1,0:T(8,128)(2,1)S(1)}, u32[]{:S(2)}) copy-start(bf16[16,128,1024]{2,1,0:T(8,128)(2,1)S(1)} %correct.1.v_hbm) | copy-start | bytes 12582916
  30.9 2.2 %copy-start.2 = (bf16[16,128,1024]{2,1,0:T(8,128)(2,1)S(1)}, bf16[16,128,1024]{2,1,0:T(8,128)(2,1)}, u32[]{:S(2)}) copy-start(bf16[16,128,1024]{2,1,0:T(8,128)(2,1)} %copy-done.1) | copy-start | bytes 12582916
  33.1 1.0 %copy-start.7 = (bf16[2048,128]{1,0:T(8,128)(2,1)S(1)}, bf16[2048,128]{1,0:T(8,128)(2,1)}, u32[]{:S(2)}) copy-start(bf16[2048,128]{1,0:T(8,128)(2,1)} %constant.23.clone.rows) | copy-start | bytes 1572868
  34.2 39.5 %copy-start.6 = (bf16[512,512]{1,0:T(8,128)(2,1)S(1)}, bf16[512,512]{1,0:T(8,128)(2,1)}, u32[]{:S(2)}) copy-start(bf16[512,512]{1,0:T(8,128)(2,1)} %constant.24.clone.t1e) | copy-start | bytes 1572868

commit v3 on v2

--- a/solution.py
+++ b/solution.py
@@ -27,6 +27,7 @@
 NT = (((1,), (1,)), ((), ()))
 TN = (((0,), (0,)), ((), ()))
 MIB = 1024 * 1024
+YP = YS // PARTS
 
 
 def iota(shape, dim):
@@ -37,7 +38,7 @@
     k = np.arange(-128, 128)
     q = np.arange(1024)
     d = np.cos(2 * np.pi * k[None, :] * q[:, None] / 1024).sum(1) / 256
-    r = np.arange(2048) % 1024
+    r = np.arange(1024)
     yp = 4 * (r // 8) + r % 4
     yy = np.repeat(np.arange(32), 4)
     fy = np.tile(np.arange(4), 32)
@@ -45,33 +46,31 @@
 
 
 def col_tables():
-    x = np.arange(512) - 8
-    out = []
-    for par in (0, 1):
-        k = 2 * np.arange(256) + par
+    x = np.arange(256) - 8
+    xp = np.arange(512)
+    forward, inverse = [], []
+    for par in range(4):
+        k = 4 * np.arange(128) + par
         ang = 2 * np.pi * ((x[:, None] * k[None, :]) % 1024) / 1024
         c, s = np.cos(ang), np.sin(ang)
         if par == 0:
             s[:, 0] = np.where(x % 2 == 0, 1.0, -1.0)
-        out.append(np.concatenate([c, s], 1).astype(ml_dtypes.bfloat16))
-    xp = np.arange(1024)
-    for par in (0, 1):
-        k = 2 * np.arange(256) + par
+        forward.append(np.concatenate([c, s], 1))
         w = np.where(k == 0, 1.0, 2.0)[:, None]
         ang = 2 * np.pi * ((k[:, None] * xp[None, :]) % 2048) / 2048
-        out.append(np.concatenate([w * np.cos(ang), -w * np.sin(ang)], 0).astype(ml_dtypes.bfloat16))
-    return out
+        inverse.append(np.concatenate([w * np.cos(ang), -w * np.sin(ang)], 0))
+    return [np.stack(t).astype(ml_dtypes.bfloat16) for t in (forward, inverse)]
 
 
 def phase_tables():
-    out = np.zeros((2, 2, 2, 8, 256), np.float32)
-    for par in (0, 1):
-        k = 2 * np.arange(256) + par
+    out = np.zeros((4, 2, 2, 8, 128), np.float32)
+    for par in range(4):
+        k = 4 * np.arange(128) + par
         for fx in range(4):
             rows = slice(4 * (fx >> 1), 4 * (fx >> 1) + 4)
             out[par, 0, fx & 1, rows] = np.cos(2 * np.pi * k * fx / 4096)
             out[par, 1, fx & 1, rows] = np.sin(2 * np.pi * k * fx / 4096)
-    return out.reshape(64, 256)
+    return out.reshape(128, 128)
 
 
 def nyquist_tables():
@@ -97,7 +96,7 @@
     return high, mid, value - high - mid
 
 
-def reference_kernel(place, level, amounts, frames, dark, gain, index, send, r_out, pixel_out, held, sems):
+def reference_kernel(level, amounts, frames, dark, gain, index, send, r_out, pixel_out, held, sems):
     def part(i):
         span = pl.ds(i * (YS // PARTS), YS // PARTS)
         return pltpu.make_async_copy(frames.at[span], held.at[span], sems.at[i])
@@ -135,8 +134,8 @@
                 jnp.ones((8, 256), BF16), jnp.concatenate([high, low], 1), NT, preferred_element_type=F32
             )
             r_out[y : y + 1, :] = total[0:1] - level[y] * offset
-    s = place[0]
-    g = place[1]
+    s = lax.axis_index("scan")
+    g = lax.axis_index("grp")
     r = r_out[...]
     center = jnp.sum(r) * (1.0 / (YS * XS))
     rest = r - center
@@ -166,22 +165,39 @@
                 send[lax.rem(s + ds, S) * G + lax.rem(g + dg, G)] = chunk(top)
 
 
-def correct_kernel(level, frames, pixel, v_out):
-    y = pl.program_id(0) * (YS // PARTS)
-    for i in range(YS // PARTS):
-        value = (frames[i].astype(F32) - level[y + i] * pixel[0:1, :]) * pixel[1:2, :]
-        v_out[i] = value.astype(BF16)
+def correct_kernel(level, frames, pixel, rows, v_out, left_out, held, ready, in_sems, out_sems):
+    def part(i):
+        return pltpu.make_async_copy(frames.at[pl.ds(i * YP, YP)], held.at[pl.ds(i * YP, YP)], in_sems.at[i])
+
+    def back(i):
+        return pltpu.make_async_copy(ready.at[pl.ds(i * YP, YP)], v_out.at[pl.ds(i * YP, YP)], out_sems.at[i])
+
+    for i in range(PARTS):
+        part(i).start()
+    col = iota((128, 512), 1)
+    spread = ((iota((128, 512), 0) >> 2) == (col >> 4)) & ((iota((128, 512), 0) & 3) == (col & 3))
+    left = jnp.dot(rows[...], spread.astype(F32).astype(BF16), preferred_element_type=F32)
+    left_out[...] = jnp.where(
+        ((iota((BF, 512), 0) >> 2) & 1) == ((iota((BF, 512), 1) >> 3) & 1), left, 0.0
+    ).astype(BF16)
+    for i in range(PARTS):
+        part(i).wait()
+        for y in range(i * YP, (i + 1) * YP):
+            value = (held[y].astype(F32) - level[y] * pixel[0:1, :]) * pixel[1:2, :]
+            ready[y] = value.astype(BF16)
+        back(i).start()
+    for i in range(PARTS):
+        back(i).wait()
 
 
 def strip_kernel(
-    place, recv, r_own, v_hbm, rows, out, total_out, v, moved, hot, main, over, window, table, sems
+    recv, r_own, v_hbm, left, out, total_out, v, moved, hot, main, over, window, table, around, sums, sems
 ):
-    s = place[0]
-    g = place[1]
+    s = lax.axis_index("scan")
+    g = lax.axis_index("grp")
 
     def part(i):
-        span = pl.ds(i * (YS // PARTS), YS // PARTS)
-        return pltpu.make_async_copy(v_hbm.at[span], v.at[span], sems.at[i])
+        return pltpu.make_async_copy(v_hbm.at[pl.ds(i * YP, YP)], v.at[pl.ds(i * YP, YP)], sems.at[i])
 
     for i in range(PARTS):
         part(i).start()
@@ -222,20 +238,20 @@
         code = ((sx >> 2) + 8) * 16 + (sx & 3) * 4 + (sy & 3)
         hot[:, 128 * t : 128 * (t + 1)] = (row == code).astype(F32).astype(BF16)
 
+    for y in range(YS):
+        for b in range(16):
+            around[16 * b : 16 * (b + 1), 128 * y : 128 * (y + 1)] = table[b, y + 1 : y + 17, :].astype(BF16)
+    span = YP * XS
+    corr = jnp.zeros((BF, 256), F32)
     for i in range(PARTS):
         part(i).wait()
-
-    acc = jnp.zeros((256, BF), F32)
-    for j in range(0, YS, 2):
-        left = jnp.concatenate(
-            [
-                jnp.concatenate([table[b, i + 1 : i + 17, :] for b in range(16)], axis=0).astype(BF16)
-                for i in (j, j + 1)
-            ],
-            axis=1,
+        corr = corr + lax.dot_general(
+            v[i * YP : (i + 1) * YP].reshape(span, BF),
+            around[:, span * i : span * (i + 1)],
+            (((0,), (1,)), ((), ())),
+            preferred_element_type=F32,
         )
-        acc = acc + jnp.dot(left, v[j : j + 2].reshape(256, BF), preferred_element_type=F32)
-    out[:, 384:640] = acc.T.astype(BF16)
+    out[:, 384:640] = corr.astype(BF16)
 
     for t in range(8):
         lanes = slice(128 * t, 128 * (t + 1))
@@ -268,21 +284,19 @@
 
     lane = iota((16, 128), 1)
 
-    def group(j, _):
-        block = moved[pl.ds(2 * j, 2)].reshape(256, BF)
-        sums = lax.dot_general(hot[...], block, NT, preferred_element_type=F32)
-        for h in range(2):
-            acc_main = sums[0:16, 128 * h : 128 * (h + 1)]
+    for j in range(4):
+        block = moved[8 * j : 8 * j + 8].reshape(8 * XS, BF)
+        sums[j & 1] = lax.dot_general(hot[...], block, NT, preferred_element_type=F32)
+        for h in range(8):
+            lanes = slice(128 * h, 128 * (h + 1))
+            acc_main = sums[j & 1, 0:16, lanes]
             acc_over = jnp.zeros((16, 128), F32)
             for b in range(1, BX):
-                piece = pltpu.roll(sums[16 * b : 16 * (b + 1), 128 * h : 128 * (h + 1)], b, 1)
+                piece = pltpu.roll(sums[j & 1, 16 * b : 16 * (b + 1), lanes], b, 1)
                 acc_main = acc_main + jnp.where(lane >= b, piece, 0.0)
                 acc_over = acc_over + jnp.where(lane < b, piece, 0.0)
-            main[2 * j + h] = acc_main
-            over[2 * j + h] = acc_over
-        return 0
-
-    lax.fori_loop(0, 16, group, 0)
+            main[8 * j + h] = acc_main
+            over[8 * j + h] = acc_over
 
     sign_y = 1.0 - 2.0 * (iota((32, 16, 128), 0) & 1).astype(F32)
     sign_x = 1.0 - 2.0 * (iota((8, 128), 1) & 1).astype(F32)
@@ -292,13 +306,6 @@
     q_high = q_row.astype(BF16).astype(F32)
     q_row = q_high + pltpu.roll(q_row - q_high, 16, 1)
 
-    col = iota((128, 512), 1)
-    spread = ((iota((128, 512), 0) >> 2) == (col >> 4)) & ((iota((128, 512), 0) & 3) == (col & 3))
-    start = pl.multiple_of(1024 - 64 * s, 64)
-    left = jnp.dot(rows[pl.ds(start, 1024), :], spread.astype(F32).astype(BF16), preferred_element_type=F32)
-    left = jnp.where(
-        ((iota((1024, 512), 0) >> 2) & 1) == ((iota((1024, 512), 1) >> 3) & 1), left, 0.0
-    ).astype(BF16)
     kind = (iota((512, 128), 0) >> 2) & 1
     u_main = main[...].reshape(512, 128)
     u_over = over[...].reshape(512, 128)
@@ -312,12 +319,14 @@
         ],
         axis=1,
     ).astype(BF16)
-    z = jnp.dot(left, right, preferred_element_type=F32)
-    out[:, 0:256] = z[:, 0:256].astype(BF16)
-    out[:, 256:384] = (z[:, 256:384] + q_row).astype(BF16)
-
-
-def finish_kernel(recv, total, t1e, t1o, t2e, t2o, phase, nyquist, out, corr_out, full):
+    z = jnp.dot(left[...], right, preferred_element_type=F32)
+    z = jnp.concatenate([z[:, 0:256], z[:, 256:384] + q_row], axis=1).astype(BF16)
+    for b in range(S):
+        place = pl.multiple_of(64 * lax.rem(s + b, S), 64)
+        out[pl.ds(place, 64), 0:384] = z[64 * b : 64 * (b + 1)]
+
+
+def finish_kernel(recv, total, forward, inverse, phase, nyquist, out, corr_out, full):
     corr = jnp.zeros((8, 256), F32)
     sums = []
     for g in range(G):
@@ -344,10 +353,14 @@
         lanes = slice(128 * g, 128 * (g + 1))
         full[0:8, lanes] = sums[g][:, 0:128] + jnp.where(lane < 16, tail, 0.0)
         full[8:16, lanes] = sums[g][:, 128:256] + jnp.where(lane < 16, pltpu.roll(tail, 112, 1), 0.0)
-    low = full[:, 0:512]
-    high = full[:, 512:1024]
-    lane_e = iota((8, 256), 1)
-    results = []
+    z0, z1, z2, z3 = (full[:, 256 * j : 256 * (j + 1)] for j in range(4))
+    inputs = (
+        (z0 + z1 + z2 + z3, None),
+        (z0 - z2, z3 - z1),
+        (z0 - z1 + z2 - z3, None),
+        (z0 - z2, z1 - z3),
+    )
+    lane_e = iota((8, 128), 1)
     wave_cos = jnp.sum(q_rows * nyquist[0:8, :], axis=1, keepdims=True)
     wave_sin = jnp.sum(q_rows * nyquist[8:16, :], axis=1, keepdims=True)
 
@@ -356,13 +369,21 @@
 
     real_cos = jnp.zeros((8, 128), F32)
     real_sin = jnp.zeros((8, 128), F32)
-    for par, (t1, t2, part) in enumerate(((t1e, t2e, low + high), (t1o, t2o, low - high))):
-        spec = jnp.dot(part.astype(BF16), t1[...], preferred_element_type=F32)
-        re = jnp.zeros((8, 256), F32)
-        im = jnp.zeros((8, 256), F32)
+    results = []
+    for par, (real, imag) in enumerate(inputs):
+        if imag is None:
+            spec = jnp.dot(real.astype(BF16), forward[par], preferred_element_type=F32)
+            cos_part, sin_part = spec[:, 0:128], spec[:, 128:256]
+        else:
+            stacked = jnp.concatenate([real, imag], axis=0).astype(BF16)
+            spec = jnp.dot(stacked, forward[par], preferred_element_type=F32)
+            cos_part = spec[0:16, 0:128] + spec[16:32, 128:256]
+            sin_part = spec[0:16, 128:256] - spec[16:32, 0:128]
+        re = jnp.zeros((8, 128), F32)
+        im = jnp.zeros((8, 128), F32)
         for fxl in range(2):
-            c = spec[8 * fxl : 8 * fxl + 8, 0:256]
-            s = spec[8 * fxl : 8 * fxl + 8, 256:512]
+            c = cos_part[8 * fxl : 8 * fxl + 8]
+            s = sin_part[8 * fxl : 8 * fxl + 8]
             if par == 0:
                 ny = s[:, 0:1]
                 real_cos = real_cos + ny * nyquist[16 + 16 * fxl : 24 + 16 * fxl, :]
@@ -376,18 +397,27 @@
         im = both(im)
         if par == 0:
             re = jnp.where(lane_e == 0, re - total[0:1, 0:1] * (1.0 / SY), re)
-        coef = jnp.concatenate([re, im], axis=1).astype(BF16)
-        results.append(jnp.dot(coef, t2[...], preferred_element_type=F32))
+        coef = jnp.concatenate([re, im], axis=1)
+        if imag is not None:
+            coef = jnp.concatenate([coef, jnp.concatenate([im, -re], axis=1)], axis=0)
+        results.append(jnp.dot(coef.astype(BF16), inverse[par], preferred_element_type=F32))
     wave_cos = wave_cos + both(real_cos)[:, 0:1]
     wave_sin = wave_sin + both(real_sin)[:, 0:1]
-    turn = iota((8, 1024), 1) & 3
+    turn = iota((8, 512), 1) & 3
     wave = wave_cos * jnp.where(turn == 0, 1.0, jnp.where(turn == 2, -1.0, 0.0))
     wave = wave + wave_sin * jnp.where(turn == 1, 1.0, jnp.where(turn == 3, -1.0, 0.0))
     scale = 1.0 / (SX * math.sqrt(BF))
-    even = results[0] + wave
-    odd = results[1]
-    out[:, 0:1024] = ((even + odd) * scale)[0:4]
-    out[:, 1024:2048] = ((even - odd) * scale)[0:4]
+    first = results[0] + wave
+    e1, f1 = results[1][0:8], results[1][8:16]
+    e3, f3 = results[3][0:8], results[3][8:16]
+    quarters = (
+        first + results[2] + e1 + e3,
+        first - results[2] - f1 + f3,
+        first + results[2] - e1 - e3,
+        first - results[2] + f1 - f3,
+    )
+    for j, quarter in enumerate(quarters):
+        out[:, 512 * j : 512 * (j + 1)] = (quarter * scale)[0:4]
 
 
 def exchange(value):
@@ -399,14 +429,13 @@
 
 
 def local(frames, dark_frame, gain_frame, bf_index, row_level, shift_num):
-    place = jnp.stack([lax.axis_index("scan"), lax.axis_index("grp")]).astype(jnp.int32)
     smem = pl.BlockSpec(memory_space=pltpu.SMEM)
     vmem = pl.BlockSpec(memory_space=pltpu.VMEM)
-    hbm = pl.BlockSpec(memory_space=pl.ANY)
+    hbm = pl.BlockSpec(memory_space=pltpu.HBM)
 
     send, r_own, pixel = pl.pallas_call(
         reference_kernel,
-        in_specs=[smem, smem, smem, hbm, vmem, vmem, vmem],
+        in_specs=[smem, smem, hbm, vmem, vmem, vmem],
         out_specs=[vmem, vmem, vmem],
         out_shape=[
             jax.ShapeDtypeStruct((N, 16, 128), BF16),
@@ -417,7 +446,6 @@
         compiler_params=limit(60),
         name="reference_image",
     )(
-        place,
         row_level,
         shift_num,
         frames,
@@ -426,23 +454,27 @@
         bf_index.reshape(1, BF),
     )
     recv = exchange(send)
-    v = pl.pallas_call(
+    v, left = pl.pallas_call(
         correct_kernel,
-        grid=(PARTS,),
-        in_specs=[
-            smem,
-            pl.BlockSpec((YS // PARTS, XS, BF), lambda i: (i, 0, 0)),
-            pl.BlockSpec((8, BF), lambda i: (0, 0)),
-        ],
-        out_specs=pl.BlockSpec((YS // PARTS, XS, BF), lambda i: (i, 0, 0)),
-        out_shape=jax.ShapeDtypeStruct((YS, XS, BF), BF16),
-        compiler_params=limit(24),
+        in_specs=[smem, hbm, vmem, vmem],
+        out_specs=[hbm, vmem],
+        out_shape=[
+            jax.ShapeDtypeStruct((YS, XS, BF), BF16),
+            jax.ShapeDtypeStruct((BF, 512), BF16),
+        ],
+        scratch_shapes=[
+            pltpu.VMEM((YS, XS, BF), BF16),
+            pltpu.VMEM((YS, XS, BF), BF16),
+            pltpu.SemaphoreType.DMA((PARTS,)),
+            pltpu.SemaphoreType.DMA((PARTS,)),
+        ],
+        compiler_params=limit(60),
         cost_estimate=pl.CostEstimate(flops=8 * YS * XS * BF, bytes_accessed=4 * YS * XS * BF, transcendentals=0),
         name="correct",
-    )(row_level, frames, pixel)
+    )(row_level, frames, pixel, jnp.asarray(row_kernel()))
     sums, total = pl.pallas_call(
         strip_kernel,
-        in_specs=[smem, vmem, vmem, hbm, vmem],
+        in_specs=[vmem, vmem, hbm, vmem],
         out_specs=[vmem, vmem],
         out_shape=[
             jax.ShapeDtypeStruct((BF, 640), BF16),
@@ -456,16 +488,18 @@
             pltpu.VMEM((32, 16, 128), F32),
             pltpu.VMEM((32, 384), F32),
             pltpu.VMEM((16, 32, 128), F32),
+            pltpu.VMEM((256, YS * XS), BF16),
+            pltpu.VMEM((2, BX * 16, BF), F32),
             pltpu.SemaphoreType.DMA((PARTS,)),
         ],
-        compiler_params=limit(30),
+        compiler_params=limit(60),
         name="strip",
-    )(place, recv, r_own, v, jnp.asarray(row_kernel()))
+    )(recv, r_own, v, left)
     parts = exchange(sums.reshape(N, 8, 640))
     tables = [jnp.asarray(t) for t in (*col_tables(), phase_tables(), nyquist_tables())]
     return pl.pallas_call(
         finish_kernel,
-        in_specs=[vmem] * 8,
+        in_specs=[vmem] * 6,
         out_specs=[vmem, vmem],
         out_shape=[
             jax.ShapeDtypeStruct((4, 2 * SX), F32),

time: 76 us -> 75.3 us (level)
  local copies, waits for them, and re-layouts: 8.17 us -> 1.5 us
  Pallas kernels: 21.3 us -> 26 us
  waiting for transfers between devices: 7.14 us -> 8.29 us
  blocking collectives: 26.2 us -> 27.1 us
    unnamed x28 -> x12, local copies, waits for them, and re-layouts: 8.17 us -> 1.5 us
    pallas_call x4, Pallas kernels: 21.3 us -> 26 us  [the longest x1 14.3 us: local(): pl.pallas_call(strip_kernel, in_specs=[vmem, vmem, hbm, vmem], out_specs=...]
    all_to_all x1, waiting for transfers between devices: 7.14 us -> 8.29 us  [exchange(): return lax.all_to_all(value, AXES, split_axis=0, concat_axis=0, tiled=True)]
    all_to_all x1, blocking collectives: 26.2 us -> 27.1 us  [exchange(): return lax.all_to_all(value, AXES, split_axis=0, concat_axis=0, tiled=True)]
  transfers between devices with their start and end apart: 1 -> 1, of which waited for: 1 -> 1; matrix products, arithmetic and copies ran while one was open for 0% -> 0% of each run, Pallas kernels for 2% -> 7%
where the time goes in v3:
time: 75.3 us; the launch traced here: 74.7 us
  blocking collectives  27.1 us (36%)
  Pallas kernels  26 us (35%)
  starting transfers between devices  11.1 us (15%)
  waiting for transfers between devices  8.29 us (11%)
  local copies, waits for them, and re-layouts  1.5 us (2%)
    all_to_all x1, blocking collectives, exchange(): return lax.all_to_all(value, AXES, split_axis=0, concat_axis=0, tiled=True)  27.1 us
    pallas_call x1, Pallas kernels, local(): pl.pallas_call(strip_kernel, in_specs=[vmem, vmem, hbm, vmem], out_specs=...  14.3 us
    all_to_all x1, starting transfers between devices, exchange(): return lax.all_to_all(value, AXES, split_axis=0, concat_axis=0, tiled=True)  11.1 us
    all_to_all x1, waiting for transfers between devices, exchange(): return lax.all_to_all(value, AXES, split_axis=0, concat_axis=0, tiled=True)  8.29 us
    pallas_call x1, Pallas kernels, local(): pl.pallas_call(correct_kernel, in_specs=[smem, hbm, vmem, vmem], out_spec...  5.46 us
    pallas_call x1, Pallas kernels, local(): pl.pallas_call(reference_kernel, in_specs=[smem, smem, hbm, vmem, vmem, v...  4.78 us
  transfers between devices with their start and end apart: 1, of which 1 were waited for; matrix products, arithmetic and copies ran while one was open for 0% of the time, Pallas kernels for 7%

profile of v3, /device:TPU:0, one launch (start us, length us, event | category | flops | bytes accessed | tf_op | source)
XLA Modules:
  0.0 74.7 jit_solution(11870406225870365517)
XLA Ops:
  0.6 4.8 %reference_image.1 = (bf16[128,16,128]{2,1,0:T(8,128)(2,1)}, f32[16,128]{1,0:T(8,128)}, f32[8,1024]{1,0:T(8,128)}) custom-call(f32[16]{0:T(128)} %level.3, s32[2,8]{1,0:T(2,128)} %amounts.1, bf16[16,128,1024]{2,1,0:T(8,128)(2,1)} %frames.3, s32[288,128]{1,0:T(8,128)} %bitcast.5, s32[288,128]{1,0:T(8,128)} %bitcast.6, s32[1,1024]{1,0:T(1,128)} %bitcast.7), custom_call_target="tpu_custom_call" | custom-call | tf_op jit(solution)/shard_map/reference_image/pallas_call | solution.py:436
  5.4 11.1 %all-to-all-start = ((bf16[128,16,128]{2,1,0:T(8,128)(2,1)}), bf16[128,16,128]{2,1,0:T(8,128)(2,1)S(1)}, u32[]{:S(2)}, u32[]{:S(2)}) async-start(bf16[128,16,128]{2,1,0:T(8,128)(2,1)} %get-tuple-element.9), calls=%async_computation | async-start | bytes 1048576 | tf_op jit(solution)/shard_map/all_to_all | solution.py:424
  16.6 5.5 %correct.1 = (bf16[16,128,1024]{2,1,0:T(8,128)(2,1)}, bf16[1024,512]{1,0:T(8,128)(2,1)}) custom-call(f32[16]{0:T(128)} %level.3, bf16[16,128,1024]{2,1,0:T(8,128)(2,1)} %frames.3, f32[8,1024]{1,0:T(8,128)} %get-tuple-element.11.pixel, bf16[1024,128]{1,0:T(8,128)(2,1)} %constant.10.clone.rows), custom_call_target="tpu_custom_call" | custom-call | flops 16777216 | bytes 8388608 | tf_op jit(solution)/shard_map/correct/pallas_call | solution.py:457
  22.0 8.3 %all-to-all-done.recv = bf16[128,16,128]{2,1,0:T(8,128)(2,1)S(1)} async-done(((bf16[128,16,128]{2,1,0:T(8,128)(2,1)}), bf16[128,16,128]{2,1,0:T(8,128)(2,1)S(1)}, u32[]{:S(2)}, u32[]{:S(2)}) %all-to-all-start) | async-done | bytes 524320 | tf_op jit(solution)/shard_map/all_to_all | solution.py:424
  30.3 0.0 copy-start.5
  30.3 0.8 %copy-done.5 = bf16[128,16,128]{2,1,0:T(8,128)(2,1)} copy-done((bf16[128,16,128]{2,1,0:T(8,128)(2,1)}, bf16[128,16,128]{2,1,0:T(8,128)(2,1)S(1)}, u32[]{:S(2)}) %copy-start.5) | copy-done | bytes 524312
  31.1 0.0 copy-start
  31.1 0.0 copy-start.1
  31.1 0.0 copy-start.2
  31.1 0.0 copy-start.3
  31.1 14.3 %strip.1 = (bf16[1024,640]{1,0:T(8,128)(2,1)}, f32[8,128]{1,0:T(8,128)}) custom-call(bf16[128,16,128]{2,1,0:T(8,128)(2,1)} %copy-done.5, f32[16,128]{1,0:T(8,128)} %get-tuple-element.10.r_own, bf16[16,128,1024]{2,1,0:T(8,128)(2,1)} %get-tuple-element.12.v_hbm, bf16[1024,512]{1,0:T(8,128)(2,1)} %get-tuple-element.13.left), custom_call_target="tpu_custom_call" | custom-call | tf_op jit(solution)/shard_map/strip/pallas_call | solution.py:475
  45.5 27.1 %all_to_all.10.recv = bf16[128,8,640]{2,1,0:T(8,128)(2,1)S(1)} all-to-all(bf16[128,8,640]{2,1,0:T(8,128)(2,1)} %bitcast.4), channel_id=1, replica_groups=mesh['scan'=16,'grp'=8] {'scan','grp'}, dimensions={0} | all-to-all | bytes 2621440 | tf_op jit(solution)/shard_map/all_to_all | solution.py:424
  72.5 0.0 copy-done
  72.5 0.0 copy-done.1
  72.5 0.0 copy-done.2
  72.5 0.0 copy-done.3
  72.5 0.0 copy-start.4
  72.6 0.7 copy-done.4
  73.2 1.5 %finish.1 = (f32[4,2048]{1,0:T(4,128)}, f32[8,256]{1,0:T(8,128)}) custom-call(bf16[128,8,640]{2,1,0:T(8,128)(2,1)S(1)} %all_to_all.10.recv, f32[8,128]{1,0:T(8,128)S(1)} %copy-done.4, bf16[4,256,256]{2,1,0:T(8,128)(2,1)S(1)} %copy-done.1, bf16[4,256,512]{2,1,0:T(8,128)(2,1)S(1)} %copy-done, f32[128,128]{1,0:T(8,128)S(1)} %copy-done.2, f32[48,128]{1,0:T(8,128)S(1)} %copy-done.3), custom_call_target="tpu_custom_call" | custom-call | tf_op jit(solution)/shard_map/finish/pallas_call | solution.py:500
Async XLA Ops:
  5.4 24.9 %all-to-all-start = ((bf16[128,16,128]{2,1,0:T(8,128)(2,1)}), bf16[128,16,128]{2,1,0:T(8,128)(2,1)S(1)}, u32[]{:S(2)}, u32[]{:S(2)}) async-start(bf16[128,16,128]{2,1,0:T(8,128)(2,1)} %get-tuple-element.9), calls=%async_computation | async-start | bytes 1048576 | tf_op jit(solution)/shard_map/all_to_all | solution.py:424
  30.3 0.8 %copy-start.5 = (bf16[128,16,128]{2,1,0:T(8,128)(2,1)}, bf16[128,16,128]{2,1,0:T(8,128)(2,1)S(1)}, u32[]{:S(2)}) copy-start(bf16[128,16,128]{2,1,0:T(8,128)(2,1)S(1)} %all-to-all-done.recv) | copy-start | bytes 1572868
  31.1 41.4 %copy-start = (bf16[4,256,512]{2,1,0:T(8,128)(2,1)S(1)}, bf16[4,256,512]{2,1,0:T(8,128)(2,1)}, u32[]{:S(2)}) copy-start(bf16[4,256,512]{2,1,0:T(8,128)(2,1)} %constant.12.clone.inverse) | copy-start | bytes 3145732
  31.1 41.4 %copy-start.1 = (bf16[4,256,256]{2,1,0:T(8,128)(2,1)S(1)}, bf16[4,256,256]{2,1,0:T(8,128)(2,1)}, u32[]{:S(2)}) copy-start(bf16[4,256,256]{2,1,0:T(8,128)(2,1)} %constant.11.clone.forward) | copy-start | bytes 1572868
  31.1 41.4 %copy-start.2 = (f32[128,128]{1,0:T(8,128)S(1)}, f32[128,128]{1,0:T(8,128)}, u32[]{:S(2)}) copy-start(f32[128,128]{1,0:T(8,128)} %constant.13.clone.phase) | copy-start | bytes 196612
  31.1 41.4 %copy-start.3 = (f32[48,128]{1,0:T(8,128)S(1)}, f32[48,128]{1,0:T(8,128)}, u32[]{:S(2)}) copy-start(f32[48,128]{1,0:T(8,128)} %constant.14.clone.nyquist) | copy-start | bytes 73732
  72.5 0.7 copy-start.4

commit v4 on v3

--- a/solution.py
+++ b/solution.py
@@ -165,39 +165,14 @@
                 send[lax.rem(s + ds, S) * G + lax.rem(g + dg, G)] = chunk(top)
 
 
-def correct_kernel(level, frames, pixel, rows, v_out, left_out, held, ready, in_sems, out_sems):
-    def part(i):
-        return pltpu.make_async_copy(frames.at[pl.ds(i * YP, YP)], held.at[pl.ds(i * YP, YP)], in_sems.at[i])
-
-    def back(i):
-        return pltpu.make_async_copy(ready.at[pl.ds(i * YP, YP)], v_out.at[pl.ds(i * YP, YP)], out_sems.at[i])
-
-    for i in range(PARTS):
-        part(i).start()
-    col = iota((128, 512), 1)
-    spread = ((iota((128, 512), 0) >> 2) == (col >> 4)) & ((iota((128, 512), 0) & 3) == (col & 3))
-    left = jnp.dot(rows[...], spread.astype(F32).astype(BF16), preferred_element_type=F32)
-    left_out[...] = jnp.where(
-        ((iota((BF, 512), 0) >> 2) & 1) == ((iota((BF, 512), 1) >> 3) & 1), left, 0.0
-    ).astype(BF16)
-    for i in range(PARTS):
-        part(i).wait()
-        for y in range(i * YP, (i + 1) * YP):
-            value = (held[y].astype(F32) - level[y] * pixel[0:1, :]) * pixel[1:2, :]
-            ready[y] = value.astype(BF16)
-        back(i).start()
-    for i in range(PARTS):
-        back(i).wait()
-
-
 def strip_kernel(
-    recv, r_own, v_hbm, left, out, total_out, v, moved, hot, main, over, window, table, around, sums, sems
+    level, recv, r_own, pixel, frames, rows, out, held, v, moved, hot, main, over, window, table, around, sums, sems
 ):
     s = lax.axis_index("scan")
     g = lax.axis_index("grp")
 
     def part(i):
-        return pltpu.make_async_copy(v_hbm.at[pl.ds(i * YP, YP)], v.at[pl.ds(i * YP, YP)], sems.at[i])
+        return pltpu.make_async_copy(frames.at[pl.ds(i * YP, YP)], held.at[pl.ds(i * YP, YP)], sems.at[i])
 
     for i in range(PARTS):
         part(i).start()
@@ -211,7 +186,9 @@
         feet.append(foot)
         centers = centers + foot
     mean = jnp.sum(jnp.where(iota((1, 128), 1) < 3, centers[2:3], 0.0), axis=1, keepdims=True) * (1.0 / N)
-    total_out[...] = jnp.broadcast_to(mean * (SY * SX), (8, 128))
+    total_row = jnp.zeros((1, 128), F32)
+    for i, piece in enumerate(three_parts(mean * (SY * SX))):
+        total_row = jnp.where(iota((1, 128), 1) == 96 + i, piece, total_row)
 
     def neighbour(ds, dg):
         got = recv[lax.rem(s + ds, S) * G + lax.rem(g + dg, G)].astype(F32)
@@ -245,6 +222,9 @@
     corr = jnp.zeros((BF, 256), F32)
     for i in range(PARTS):
         part(i).wait()
+        for y in range(i * YP, (i + 1) * YP):
+            value = (held[y].astype(F32) - level[y] * pixel[0:1, :]) * pixel[1:2, :]
+            v[y] = value.astype(BF16)
         corr = corr + lax.dot_general(
             v[i * YP : (i + 1) * YP].reshape(span, BF),
             around[:, span * i : span * (i + 1)],
@@ -306,6 +286,10 @@
     q_high = q_row.astype(BF16).astype(F32)
     q_row = q_high + pltpu.roll(q_row - q_high, 16, 1)
 
+    col = iota((128, 512), 1)
+    spread = ((iota((128, 512), 0) >> 2) == (col >> 4)) & ((iota((128, 512), 0) & 3) == (col & 3))
+    left = jnp.dot(rows[...], spread.astype(F32).astype(BF16), preferred_element_type=F32)
+    left = jnp.where(((iota((BF, 512), 0) >> 2) & 1) == ((iota((BF, 512), 1) >> 3) & 1), left, 0.0).astype(BF16)
     kind = (iota((512, 128), 0) >> 2) & 1
     u_main = main[...].reshape(512, 128)
     u_over = over[...].reshape(512, 128)
@@ -319,14 +303,14 @@
         ],
         axis=1,
     ).astype(BF16)
-    z = jnp.dot(left[...], right, preferred_element_type=F32)
-    z = jnp.concatenate([z[:, 0:256], z[:, 256:384] + q_row], axis=1).astype(BF16)
+    z = jnp.dot(left, right, preferred_element_type=F32)
+    z = jnp.concatenate([z[:, 0:256], z[:, 256:384] + (q_row + total_row)], axis=1).astype(BF16)
     for b in range(S):
         place = pl.multiple_of(64 * lax.rem(s + b, S), 64)
         out[pl.ds(place, 64), 0:384] = z[64 * b : 64 * (b + 1)]
 
 
-def finish_kernel(recv, total, forward, inverse, phase, nyquist, out, corr_out, full):
+def finish_kernel(recv, forward, inverse, phase, nyquist, out, corr_out, full):
     corr = jnp.zeros((8, 256), F32)
     sums = []
     for g in range(G):
@@ -346,6 +330,8 @@
         preferred_element_type=F32,
     )
     lane = iota((8, 128), 1)
+    foot = recv[0].astype(F32)[:, 256:384]
+    total = jnp.sum(jnp.where((lane >= 96) & (lane < 99), foot, 0.0), axis=1, keepdims=True)
     q_rows = jnp.zeros((8, 128), F32)
     for g in range(G):
         tail = sums[(g - 1) % G][:, 256:384]
@@ -396,7 +382,7 @@
         re = both(re)
         im = both(im)
         if par == 0:
-            re = jnp.where(lane_e == 0, re - total[0:1, 0:1] * (1.0 / SY), re)
+            re = jnp.where(lane_e == 0, re - total * (1.0 / SY), re)
         coef = jnp.concatenate([re, im], axis=1)
         if imag is not None:
             coef = jnp.concatenate([coef, jnp.concatenate([im, -re], axis=1)], axis=0)
@@ -454,33 +440,13 @@
         bf_index.reshape(1, BF),
     )
     recv = exchange(send)
-    v, left = pl.pallas_call(
-        correct_kernel,
-        in_specs=[smem, hbm, vmem, vmem],
-        out_specs=[hbm, vmem],
-        out_shape=[
-            jax.ShapeDtypeStruct((YS, XS, BF), BF16),
-            jax.ShapeDtypeStruct((BF, 512), BF16),
-        ],
+    sums = pl.pallas_call(
+        strip_kernel,
+        in_specs=[smem, vmem, vmem, vmem, hbm, vmem],
+        out_specs=vmem,
+        out_shape=jax.ShapeDtypeStruct((BF, 640), BF16),
         scratch_shapes=[
             pltpu.VMEM((YS, XS, BF), BF16),
-            pltpu.VMEM((YS, XS, BF), BF16),
-            pltpu.SemaphoreType.DMA((PARTS,)),
-            pltpu.SemaphoreType.DMA((PARTS,)),
-        ],
-        compiler_params=limit(60),
-        cost_estimate=pl.CostEstimate(flops=8 * YS * XS * BF, bytes_accessed=4 * YS * XS * BF, transcendentals=0),
-        name="correct",
-    )(row_level, frames, pixel, jnp.asarray(row_kernel()))
-    sums, total = pl.pallas_call(
-        strip_kernel,
-        in_specs=[vmem, vmem, hbm, vmem],
-        out_specs=[vmem, vmem],
-        out_shape=[
-            jax.ShapeDtypeStruct((BF, 640), BF16),
-            jax.ShapeDtypeStruct((8, 128), F32),
-        ],
-        scratch_shapes=[
             pltpu.VMEM((YS, XS, BF), BF16),
             pltpu.VMEM((32, XS, BF), BF16),
             pltpu.VMEM((BX * 16, BF), BF16),
@@ -492,14 +458,14 @@
             pltpu.VMEM((2, BX * 16, BF), F32),
             pltpu.SemaphoreType.DMA((PARTS,)),
         ],
-        compiler_params=limit(60),
+        compiler_params=limit(50),
         name="strip",
-    )(recv, r_own, v, left)
+    )(row_level, recv, r_own, pixel, frames, jnp.asarray(row_kernel()))
     parts = exchange(sums.reshape(N, 8, 640))
     tables = [jnp.asarray(t) for t in (*col_tables(), phase_tables(), nyquist_tables())]
     return pl.pallas_call(
         finish_kernel,
-        in_specs=[vmem] * 6,
+        in_specs=[vmem] * 5,
         out_specs=[vmem, vmem],
         out_shape=[
             jax.ShapeDtypeStruct((4, 2 * SX), F32),
@@ -508,7 +474,7 @@
         scratch_shapes=[pltpu.VMEM((16, SX), F32)],
         compiler_params=limit(24),
         name="finish",
-    )(parts, total, *tables)
+    )(parts, *tables)
 
 
 def solution(mesh):

time: 75.3 us -> 73.1 us (0.971)
  blocking collectives: 27.1 us -> 51.2 us
  starting transfers between devices: 11.1 us -> 0 us
  waiting for transfers between devices: 8.29 us -> 0 us
  Pallas kernels: 26 us -> 19 us
    all_to_all x1 -> x2, blocking collectives: 27.1 us -> 51.2 us  [exchange(): return lax.all_to_all(value, AXES, split_axis=0, concat_axis=0, tiled=True)]
    all_to_all x1 -> x0, starting transfers between devices: 11.1 us -> none  [exchange(): return lax.all_to_all(value, AXES, split_axis=0, concat_axis=0, tiled=True)]
    all_to_all x1 -> x0, waiting for transfers between devices: 8.29 us -> none  [exchange(): return lax.all_to_all(value, AXES, split_axis=0, concat_axis=0, tiled=True)]
    pallas_call x3 -> x2, Pallas kernels: 21.2 us -> 14.2 us  [the longest x1 12.7 us: local(): pl.pallas_call(strip_kernel, in_specs=[smem, vmem, vmem, vmem, hbm, vmem]...]
  transfers between devices with their start and end apart: 1 -> 0, of which waited for: 1 -> 0; matrix products, arithmetic and copies ran while one was open for 0% -> 0% of each run, Pallas kernels for 7% -> 0%
where the time goes in v4:
time: 73.1 us; the launch traced here: 72.5 us
  blocking collectives  51.2 us (70%)
  Pallas kernels  19 us (26%)
  local copies, waits for them, and re-layouts  1.49 us (2%)
    all_to_all x2, blocking collectives, exchange(): return lax.all_to_all(value, AXES, split_axis=0, concat_axis=0, tiled=True)  51.2 us
    pallas_call x1, Pallas kernels, local(): pl.pallas_call(strip_kernel, in_specs=[smem, vmem, vmem, vmem, hbm, vmem]...  12.7 us
    pallas_call x1, Pallas kernels, local(): pl.pallas_call(reference_kernel, in_specs=[smem, smem, hbm, vmem, vmem, v...  4.81 us
    unnamed x16, local copies, waits for them, and re-layouts  1.49 us
    pallas_call x1, Pallas kernels, local(): pl.pallas_call(finish_kernel, in_specs=[vmem] * 5, out_specs=[vmem, vmem]...  1.48 us

profile of v4, /device:TPU:0, one launch (start us, length us, event | category | flops | bytes accessed | tf_op | source)
XLA Modules:
  0.0 72.5 jit_solution(6168348054801367082)
XLA Ops:
  0.6 0.0 copy-start.2
  0.6 0.0 copy-start.7
  0.7 4.8 %reference_image.1 = (bf16[128,16,128]{2,1,0:T(8,128)(2,1)}, f32[16,128]{1,0:T(8,128)}, f32[8,1024]{1,0:T(8,128)}) custom-call(f32[16]{0:T(128)} %level.3, s32[2,8]{1,0:T(2,128)} %amounts.1, bf16[16,128,1024]{2,1,0:T(8,128)(2,1)} %frames.3, s32[288,128]{1,0:T(8,128)} %bitcast.5, s32[288,128]{1,0:T(8,128)} %bitcast.6, s32[1,1024]{1,0:T(1,128)} %bitcast.7), custom_call_target="tpu_custom_call" | custom-call | tf_op jit(solution)/shard_map/reference_image/pallas_call | solution.py:422
  5.5 24.9 %all_to_all.10.recv = bf16[128,16,128]{2,1,0:T(8,128)(2,1)S(1)} all-to-all(bf16[128,16,128]{2,1,0:T(8,128)(2,1)} %get-tuple-element.5), channel_id=1, replica_groups=mesh['scan'=16,'grp'=8] {'scan','grp'}, dimensions={0} | all-to-all | bytes 1048576 | tf_op jit(solution)/shard_map/all_to_all | solution.py:410
  30.4 0.0 copy-done.2
  30.4 0.0 copy-done.7
  30.4 0.0 copy-start.4
  30.4 0.8 %copy-done.4 = f32[8,1024]{1,0:T(8,128)S(1)} copy-done((f32[8,1024]{1,0:T(8,128)S(1)}, f32[8,1024]{1,0:T(8,128)}, u32[]{:S(2)}) %copy-start.4) | copy-done | bytes 32792
  31.2 0.0 copy-start.6
  31.2 0.7 copy-done.6
  31.9 12.7 %strip.1 = bf16[1024,640]{1,0:T(8,128)(2,1)S(1)} custom-call(f32[16]{0:T(128)S(1)} %copy-done.7, bf16[128,16,128]{2,1,0:T(8,128)(2,1)S(1)} %all_to_all.10.recv, f32[16,128]{1,0:T(8,128)S(1)} %copy-done.6, f32[8,1024]{1,0:T(8,128)S(1)} %copy-done.4, bf16[16,128,1024]{2,1,0:T(8,128)(2,1)} %frames.3, bf16[1024,128]{1,0:T(8,128)(2,1)S(1)} %copy-done.2), custom_call_target="tpu_custom_call" | custom-call | tf_op jit(solution)/shard_map/strip/pallas_call | solution.py:443
  44.6 0.0 copy-start
  44.6 0.0 copy-start.1
  44.6 0.0 copy-start.3
  44.6 0.0 copy-start.5
  44.7 26.3 %all_to_all.11.recv = bf16[128,8,640]{2,1,0:T(8,128)(2,1)S(1)} all-to-all(bf16[128,8,640]{2,1,0:T(8,128)(2,1)S(1)} %bitcast.4), channel_id=1, replica_groups=mesh['scan'=16,'grp'=8] {'scan','grp'}, dimensions={0} | all-to-all | bytes 2621440 | tf_op jit(solution)/shard_map/all_to_all | solution.py:410
  71.0 0.0 copy-done
  71.0 0.0 copy-done.1
  71.0 0.0 copy-done.3
  71.0 0.0 copy-done.5
  71.0 1.5 %finish.1 = (f32[4,2048]{1,0:T(4,128)}, f32[8,256]{1,0:T(8,128)}) custom-call(bf16[128,8,640]{2,1,0:T(8,128)(2,1)S(1)} %all_to_all.11.recv, bf16[4,256,256]{2,1,0:T(8,128)(2,1)S(1)} %copy-done.1, bf16[4,256,512]{2,1,0:T(8,128)(2,1)S(1)} %copy-done, f32[128,128]{1,0:T(8,128)S(1)} %copy-done.3, f32[48,128]{1,0:T(8,128)S(1)} %copy-done.5), custom_call_target="tpu_custom_call" | custom-call | tf_op jit(solution)/shard_map/finish/pallas_call | solution.py:466
Async XLA Ops:
  0.6 29.8 %copy-start.2 = (bf16[1024,128]{1,0:T(8,128)(2,1)S(1)}, bf16[1024,128]{1,0:T(8,128)(2,1)}, u32[]{:S(2)}) copy-start(bf16[1024,128]{1,0:T(8,128)(2,1)} %constant.10.clone.rows) | copy-start | bytes 786436
  0.6 29.8 %copy-start.7 = (f32[16]{0:T(128)S(1)}, f32[16]{0:T(128)}, u32[]{:S(2)}) copy-start(f32[16]{0:T(128)} %level.3) | copy-start | bytes 196
  30.4 0.8 %copy-start.4 = (f32[8,1024]{1,0:T(8,128)S(1)}, f32[8,1024]{1,0:T(8,128)}, u32[]{:S(2)}) copy-start(f32[8,1024]{1,0:T(8,128)} %get-tuple-element.7.pixel) | copy-start | bytes 98308
  31.2 0.7 copy-start.6
  44.6 26.4 %copy-start = (bf16[4,256,512]{2,1,0:T(8,128)(2,1)S(1)}, bf16[4,256,512]{2,1,0:T(8,128)(2,1)}, u32[]{:S(2)}) copy-start(bf16[4,256,512]{2,1,0:T(8,128)(2,1)} %constant.12.clone.inverse) | copy-start | bytes 3145732
  44.6 26.3 %copy-start.1 = (bf16[4,256,256]{2,1,0:T(8,128)(2,1)S(1)}, bf16[4,256,256]{2,1,0:T(8,128)(2,1)}, u32[]{:S(2)}) copy-start(bf16[4,256,256]{2,1,0:T(8,128)(2,1)} %constant.11.clone.forward) | copy-start | bytes 1572868
  44.6 26.3 %copy-start.3 = (f32[128,128]{1,0:T(8,128)S(1)}, f32[128,128]{1,0:T(8,128)}, u32[]{:S(2)}) copy-start(f32[128,128]{1,0:T(8,128)} %constant.13.clone.phase) | copy-start | bytes 196612
  44.6 26.3 %copy-start.5 = (f32[48,128]{1,0:T(8,128)S(1)}, f32[48,128]{1,0:T(8,128)}, u32[]{:S(2)}) copy-start(f32[48,128]{1,0:T(8,128)} %constant.14.clone.nyquist) | copy-start | bytes 73732

commit v5 on v4

--- a/solution.py
+++ b/solution.py
@@ -96,7 +96,7 @@
     return high, mid, value - high - mid
 
 
-def reference_kernel(level, amounts, frames, dark, gain, index, send, r_out, pixel_out, held, sems):
+def reference_kernel(level, amounts, frames, dark, gain, index, send, keep, held, sems):
     def part(i):
         span = pl.ds(i * (YS // PARTS), YS // PARTS)
         return pltpu.make_async_copy(frames.at[span], held.at[span], sems.at[i])
@@ -117,8 +117,8 @@
 
     dark_px = pick(0) * (1.0 / 256.0)
     gain_px = (pick(1) * 32.0 + pick(2)) * (1.0 / 4096.0)
-    pixel_out[0:1, :] = dark_px
-    pixel_out[1:2, :] = gain_px
+    keep[0:1, :] = dark_px
+    keep[1:2, :] = gain_px
     offset = jnp.sum(dark_px * gain_px)
     for i in range(PARTS):
         part(i).wait()
@@ -133,10 +133,10 @@
             total = lax.dot_general(
                 jnp.ones((8, 256), BF16), jnp.concatenate([high, low], 1), NT, preferred_element_type=F32
             )
-            r_out[y : y + 1, :] = total[0:1] - level[y] * offset
+            keep[8 + y : 9 + y, 0:128] = total[0:1] - level[y] * offset
     s = lax.axis_index("scan")
     g = lax.axis_index("grp")
-    r = r_out[...]
+    r = keep[8:24, 0:128]
     center = jnp.sum(r) * (1.0 / (YS * XS))
     rest = r - center
     lane = iota((1, 128), 1)
@@ -166,7 +166,7 @@
 
 
 def strip_kernel(
-    level, recv, r_own, pixel, frames, rows, out, held, v, moved, hot, main, over, window, table, around, sums, sems
+    level, recv, keep, frames, rows, out, held, v, moved, hot, main, over, window, table, around, sums, sems
 ):
     s = lax.axis_index("scan")
     g = lax.axis_index("grp")
@@ -204,7 +204,7 @@
             window[8:16, lanes] = side
             window[16:24, lanes] = pltpu.roll(side, 64, 1)
         else:
-            window[8:24, lanes] = r_own[...] - mean
+            window[8:24, lanes] = keep[8:24, 0:128] - mean
     for b in range(16):
         table[b] = pltpu.roll(window[...], (b - 8) % 384, 1)[:, 128:256]
 
@@ -218,20 +218,14 @@
     for y in range(YS):
         for b in range(16):
             around[16 * b : 16 * (b + 1), 128 * y : 128 * (y + 1)] = table[b, y + 1 : y + 17, :].astype(BF16)
-    span = YP * XS
-    corr = jnp.zeros((BF, 256), F32)
     for i in range(PARTS):
         part(i).wait()
         for y in range(i * YP, (i + 1) * YP):
-            value = (held[y].astype(F32) - level[y] * pixel[0:1, :]) * pixel[1:2, :]
+            value = (held[y].astype(F32) - level[y] * keep[0:1, :]) * keep[1:2, :]
             v[y] = value.astype(BF16)
-        corr = corr + lax.dot_general(
-            v[i * YP : (i + 1) * YP].reshape(span, BF),
-            around[:, span * i : span * (i + 1)],
-            (((0,), (1,)), ((), ())),
-            preferred_element_type=F32,
-        )
-    out[:, 384:640] = corr.astype(BF16)
+    out[:, 384:640] = lax.dot_general(
+        v[...].reshape(YS * XS, BF), around[...], (((0,), (1,)), ((), ())), preferred_element_type=F32
+    ).astype(BF16)
 
     for t in range(8):
         lanes = slice(128 * t, 128 * (t + 1))
@@ -240,10 +234,9 @@
             jnp.broadcast_to(((by >> b) & 1).astype(F32), (16, 128)).astype(BF16) > 0.5 for b in range(5)
         ]
 
-        def barrel(i, _, lanes=lanes, masks=masks):
-            x0 = pl.multiple_of(i * 16, 16)
-            rows_in = [v[y, pl.ds(x0, 16), lanes] for y in range(YS)]
-            zero = jnp.zeros((16, 128), BF16)
+        zero = jnp.zeros((16, 128), BF16)
+        for x0 in range(0, XS, 16):
+            rows_in = [v[y, x0 : x0 + 16, lanes] for y in range(YS)]
             for b in range(5):
                 step = 1 << b
                 size = min(len(rows_in) + step, 32)
@@ -257,10 +250,7 @@
                     for j in range(size)
                 ]
             for j in range(32):
-                moved[j, pl.ds(x0, 16), lanes] = rows_in[j]
-            return 0
-
-        lax.fori_loop(0, 8, barrel, 0)
+                moved[j, x0 : x0 + 16, lanes] = rows_in[j]
 
     lane = iota((16, 128), 1)
 
@@ -419,14 +409,13 @@
     vmem = pl.BlockSpec(memory_space=pltpu.VMEM)
     hbm = pl.BlockSpec(memory_space=pltpu.HBM)
 
-    send, r_own, pixel = pl.pallas_call(
+    send, keep = pl.pallas_call(
         reference_kernel,
         in_specs=[smem, smem, hbm, vmem, vmem, vmem],
-        out_specs=[vmem, vmem, vmem],
+        out_specs=[vmem, vmem],
         out_shape=[
             jax.ShapeDtypeStruct((N, 16, 128), BF16),
-            jax.ShapeDtypeStruct((YS, XS), F32),
-            jax.ShapeDtypeStruct((8, BF), F32),
+            jax.ShapeDtypeStruct((24, BF), F32),
         ],
         scratch_shapes=[pltpu.VMEM((YS, XS, BF), BF16), pltpu.SemaphoreType.DMA((PARTS,))],
         compiler_params=limit(60),
@@ -442,7 +431,7 @@
     recv = exchange(send)
     sums = pl.pallas_call(
         strip_kernel,
-        in_specs=[smem, vmem, vmem, vmem, hbm, vmem],
+        in_specs=[smem, vmem, vmem, hbm, vmem],
         out_specs=vmem,
         out_shape=jax.ShapeDtypeStruct((BF, 640), BF16),
         scratch_shapes=[
@@ -460,7 +449,7 @@
         ],
         compiler_params=limit(50),
         name="strip",
-    )(row_level, recv, r_own, pixel, frames, jnp.asarray(row_kernel()))
+    )(row_level, recv, keep, frames, jnp.asarray(row_kernel()))
     parts = exchange(sums.reshape(N, 8, 640))
     tables = [jnp.asarray(t) for t in (*col_tables(), phase_tables(), nyquist_tables())]
     return pl.pallas_call(

time: 73.1 us -> 69.2 us (0.947)
  Pallas kernels: 19 us -> 15.8 us
    pallas_call x1, Pallas kernels: 12.7 us -> 9.48 us  [local(): pl.pallas_call(strip_kernel, in_specs=[smem, vmem, vmem, hbm, vmem], out_...]
    unnamed x16 -> x14, local copies, waits for them, and re-layouts: 1.49 us -> 0.93 us
where the time goes in v5:
time: 69.2 us; the launch traced here: 68.6 us
  blocking collectives  51.2 us (74%)
  Pallas kernels  15.8 us (23%)
  local copies, waits for them, and re-layouts  0.93 us (1%)
  between operations  0.71 us (1%)
    all_to_all x2, blocking collectives, exchange(): return lax.all_to_all(value, AXES, split_axis=0, concat_axis=0, tiled=True)  51.2 us
    pallas_call x1, Pallas kernels, local(): pl.pallas_call(strip_kernel, in_specs=[smem, vmem, vmem, hbm, vmem], out_...  9.48 us
    pallas_call x1, Pallas kernels, local(): pl.pallas_call(reference_kernel, in_specs=[smem, smem, hbm, vmem, vmem, v...  4.8 us
    pallas_call x1, Pallas kernels, local(): pl.pallas_call(finish_kernel, in_specs=[vmem] * 5, out_specs=[vmem, vmem]...  1.48 us

profile of v5, /device:TPU:0, one launch (start us, length us, event | category | flops | bytes accessed | tf_op | source)
XLA Modules:
  0.0 68.6 jit_solution(11521671028720823722)
XLA Ops:
  0.6 0.0 copy-start.2
  0.6 0.0 copy-start.6
  0.7 4.8 %reference_image.1 = (bf16[128,16,128]{2,1,0:T(8,128)(2,1)}, f32[24,1024]{1,0:T(8,128)}) custom-call(f32[16]{0:T(128)} %level.3, s32[2,8]{1,0:T(2,128)} %amounts.1, bf16[16,128,1024]{2,1,0:T(8,128)(2,1)} %frames.3, s32[288,128]{1,0:T(8,128)} %bitcast.5, s32[288,128]{1,0:T(8,128)} %bitcast.6, s32[1,1024]{1,0:T(1,128)} %bitcast.7), custom_call_target="tpu_custom_call" | custom-call | tf_op jit(solution)/shard_map/reference_image/pallas_call | solution.py:412
  5.5 24.9 %all_to_all.10.recv = bf16[128,16,128]{2,1,0:T(8,128)(2,1)S(1)} all-to-all(bf16[128,16,128]{2,1,0:T(8,128)(2,1)} %get-tuple-element.4), channel_id=1, replica_groups=mesh['scan'=16,'grp'=8] {'scan','grp'}, dimensions={0} | all-to-all | bytes 1048576 | tf_op jit(solution)/shard_map/all_to_all | solution.py:400
  30.4 0.0 copy-done.2
  30.4 0.0 copy-done.6
  30.4 0.0 copy-start.3
  30.4 0.9 %copy-done.3 = f32[24,1024]{1,0:T(8,128)S(1)} copy-done((f32[24,1024]{1,0:T(8,128)S(1)}, f32[24,1024]{1,0:T(8,128)}, u32[]{:S(2)}) %copy-start.3) | copy-done | bytes 98328
  31.3 9.5 %strip.1 = bf16[1024,640]{1,0:T(8,128)(2,1)S(1)} custom-call(f32[16]{0:T(128)S(1)} %copy-done.6, bf16[128,16,128]{2,1,0:T(8,128)(2,1)S(1)} %all_to_all.10.recv, f32[24,1024]{1,0:T(8,128)S(1)} %copy-done.3, bf16[16,128,1024]{2,1,0:T(8,128)(2,1)} %frames.3, bf16[1024,128]{1,0:T(8,128)(2,1)S(1)} %copy-done.2), custom_call_target="tpu_custom_call" | custom-call | tf_op jit(solution)/shard_map/strip/pallas_call | solution.py:432
  40.8 0.0 copy-start
  40.8 0.0 copy-start.1
  40.8 0.0 copy-start.4
  40.8 0.0 copy-start.5
  40.8 26.3 %all_to_all.11.recv = bf16[128,8,640]{2,1,0:T(8,128)(2,1)S(1)} all-to-all(bf16[128,8,640]{2,1,0:T(8,128)(2,1)S(1)} %bitcast.4), channel_id=1, replica_groups=mesh['scan'=16,'grp'=8] {'scan','grp'}, dimensions={0} | all-to-all | bytes 2621440 | tf_op jit(solution)/shard_map/all_to_all | solution.py:400
  67.1 0.0 copy-done
  67.1 0.0 copy-done.1
  67.1 0.0 copy-done.4
  67.1 0.0 copy-done.5
  67.1 1.5 %finish.1 = (f32[4,2048]{1,0:T(4,128)}, f32[8,256]{1,0:T(8,128)}) custom-call(bf16[128,8,640]{2,1,0:T(8,128)(2,1)S(1)} %all_to_all.11.recv, bf16[4,256,256]{2,1,0:T(8,128)(2,1)S(1)} %copy-done.1, bf16[4,256,512]{2,1,0:T(8,128)(2,1)S(1)} %copy-done, f32[128,128]{1,0:T(8,128)S(1)} %copy-done.4, f32[48,128]{1,0:T(8,128)S(1)} %copy-done.5), custom_call_target="tpu_custom_call" | custom-call | tf_op jit(solution)/shard_map/finish/pallas_call | solution.py:455
Async XLA Ops:
  0.6 29.8 %copy-start.2 = (bf16[1024,128]{1,0:T(8,128)(2,1)S(1)}, bf16[1024,128]{1,0:T(8,128)(2,1)}, u32[]{:S(2)}) copy-start(bf16[1024,128]{1,0:T(8,128)(2,1)} %constant.10.clone.rows) | copy-start | bytes 786436
  0.6 29.7 %copy-start.6 = (f32[16]{0:T(128)S(1)}, f32[16]{0:T(128)}, u32[]{:S(2)}) copy-start(f32[16]{0:T(128)} %level.3) | copy-start | bytes 196
  30.4 0.9 %copy-start.3 = (f32[24,1024]{1,0:T(8,128)S(1)}, f32[24,1024]{1,0:T(8,128)}, u32[]{:S(2)}) copy-start(f32[24,1024]{1,0:T(8,128)} %get-tuple-element.5.keep) | copy-start | bytes 294916
  40.8 26.4 %copy-start = (bf16[4,256,512]{2,1,0:T(8,128)(2,1)S(1)}, bf16[4,256,512]{2,1,0:T(8,128)(2,1)}, u32[]{:S(2)}) copy-start(bf16[4,256,512]{2,1,0:T(8,128)(2,1)} %constant.12.clone.inverse) | copy-start | bytes 3145732
  40.8 26.3 %copy-start.1 = (bf16[4,256,256]{2,1,0:T(8,128)(2,1)S(1)}, bf16[4,256,256]{2,1,0:T(8,128)(2,1)}, u32[]{:S(2)}) copy-start(bf16[4,256,256]{2,1,0:T(8,128)(2,1)} %constant.11.clone.forward) | copy-start | bytes 1572868
  40.8 26.3 %copy-start.4 = (f32[128,128]{1,0:T(8,128)S(1)}, f32[128,128]{1,0:T(8,128)}, u32[]{:S(2)}) copy-start(f32[128,128]{1,0:T(8,128)} %constant.13.clone.phase) | copy-start | bytes 196612
  40.8 26.3 %copy-start.5 = (f32[48,128]{1,0:T(8,128)S(1)}, f32[48,128]{1,0:T(8,128)}, u32[]{:S(2)}) copy-start(f32[48,128]{1,0:T(8,128)} %constant.14.clone.nyquist) | copy-start | bytes 73732

commit v6 on v5

--- a/solution.py
+++ b/solution.py
@@ -7,13 +7,14 @@
 from jax import lax
 from jax.experimental import pallas as pl
 from jax.experimental.pallas import tpu as pltpu
+from jax.sharding import Mesh
 from jax.sharding import PartitionSpec as P
 
 SY = 256
 SX = 1024
 BF = 1024
 DET = 36864
-AXES = ("scan", "grp")
+AXES = ("pair", "core", "grp")
 S = 16
 G = 8
 N = S * G
@@ -134,7 +135,7 @@
                 jnp.ones((8, 256), BF16), jnp.concatenate([high, low], 1), NT, preferred_element_type=F32
             )
             keep[8 + y : 9 + y, 0:128] = total[0:1] - level[y] * offset
-    s = lax.axis_index("scan")
+    s = lax.axis_index("pair") * 2 + lax.axis_index("core")
     g = lax.axis_index("grp")
     r = keep[8:24, 0:128]
     center = jnp.sum(r) * (1.0 / (YS * XS))
@@ -166,9 +167,9 @@
 
 
 def strip_kernel(
-    level, recv, keep, frames, rows, out, held, v, moved, hot, main, over, window, table, around, sums, sems
+    level, recv, keep, frames, rows, mine, theirs, corr, held, v, moved, hot, main, over, window, table, around, sums, sems
 ):
-    s = lax.axis_index("scan")
+    s = lax.axis_index("pair") * 2 + lax.axis_index("core")
     g = lax.axis_index("grp")
 
     def part(i):
@@ -223,9 +224,13 @@
         for y in range(i * YP, (i + 1) * YP):
             value = (held[y].astype(F32) - level[y] * keep[0:1, :]) * keep[1:2, :]
             v[y] = value.astype(BF16)
-    out[:, 384:640] = lax.dot_general(
+    corr[...] = lax.dot_general(
         v[...].reshape(YS * XS, BF), around[...], (((0,), (1,)), ((), ())), preferred_element_type=F32
     ).astype(BF16)
+    core = lax.axis_index("core")
+    for a in range(S // 2):
+        for to, c in ((mine, core), (theirs, 1 - core)):
+            to[64 * a : 64 * (a + 1), 384:640] = corr[pl.ds(pl.multiple_of(64 * (2 * a + c), 64), 64), :]
 
     for t in range(8):
         lanes = slice(128 * t, 128 * (t + 1))
@@ -296,8 +301,9 @@
     z = jnp.dot(left, right, preferred_element_type=F32)
     z = jnp.concatenate([z[:, 0:256], z[:, 256:384] + (q_row + total_row)], axis=1).astype(BF16)
     for b in range(S):
-        place = pl.multiple_of(64 * lax.rem(s + b, S), 64)
-        out[pl.ds(place, 64), 0:384] = z[64 * b : 64 * (b + 1)]
+        place = pl.multiple_of(64 * (lax.rem(s + b, S) >> 1), 64)
+        to = theirs if b & 1 else mine
+        to[pl.ds(place, 64), 0:384] = z[64 * b : 64 * (b + 1)]
 
 
 def finish_kernel(recv, forward, inverse, phase, nyquist, out, corr_out, full):
@@ -305,8 +311,8 @@
     sums = []
     for g in range(G):
         acc = jnp.zeros((8, 384), F32)
-        for s in range(S):
-            got = recv[s * G + g].astype(F32)
+        for a in range(S // 2):
+            got = recv[a * G + g].astype(F32)
             acc = acc + got[:, 0:384]
             corr = corr + got[:, 384:640]
         sums.append(acc)
@@ -321,7 +327,7 @@
     )
     lane = iota((8, 128), 1)
     foot = recv[0].astype(F32)[:, 256:384]
-    total = jnp.sum(jnp.where((lane >= 96) & (lane < 99), foot, 0.0), axis=1, keepdims=True)
+    total = jnp.sum(jnp.where((lane >= 96) & (lane < 99), foot, 0.0), axis=1, keepdims=True) * 0.5
     q_rows = jnp.zeros((8, 128), F32)
     for g in range(G):
         tail = sums[(g - 1) % G][:, 256:384]
@@ -396,8 +402,8 @@
         out[:, 512 * j : 512 * (j + 1)] = (quarter * scale)[0:4]
 
 
-def exchange(value):
-    return lax.all_to_all(value, AXES, split_axis=0, concat_axis=0, tiled=True)
+def exchange(value, axes):
+    return lax.all_to_all(value, axes, split_axis=0, concat_axis=0, tiled=True)
 
 
 def limit(mib):
@@ -428,13 +434,14 @@
         gain_frame.reshape(ROWS, 128),
         bf_index.reshape(1, BF),
     )
-    recv = exchange(send)
-    sums = pl.pallas_call(
+    recv = exchange(send, AXES)
+    mine, theirs = pl.pallas_call(
         strip_kernel,
         in_specs=[smem, vmem, vmem, hbm, vmem],
-        out_specs=vmem,
-        out_shape=jax.ShapeDtypeStruct((BF, 640), BF16),
+        out_specs=[vmem, vmem],
+        out_shape=[jax.ShapeDtypeStruct((BF // 2, 640), BF16)] * 2,
         scratch_shapes=[
+            pltpu.VMEM((BF, 256), BF16),
             pltpu.VMEM((YS, XS, BF), BF16),
             pltpu.VMEM((YS, XS, BF), BF16),
             pltpu.VMEM((32, XS, BF), BF16),
@@ -450,7 +457,9 @@
         compiler_params=limit(50),
         name="strip",
     )(row_level, recv, keep, frames, jnp.asarray(row_kernel()))
-    parts = exchange(sums.reshape(N, 8, 640))
+    swapped = lax.ppermute(theirs, "core", [(0, 1), (1, 0)])
+    both = (mine.astype(F32) + swapped.astype(F32)).astype(BF16)
+    parts = exchange(both.reshape(N // 2, 8, 640), ("pair", "grp"))
     tables = [jnp.asarray(t) for t in (*col_tables(), phase_tables(), nyquist_tables())]
     return pl.pallas_call(
         finish_kernel,
@@ -467,10 +476,11 @@
 
 
 def solution(mesh):
+    scan = ("pair", "core")
     return jax.shard_map(
         local,
-        mesh=mesh,
-        in_specs=(P("scan", "grp", None), P(), P(), P(), P("scan"), P(None, AXES)),
+        mesh=Mesh(mesh.devices.reshape(S // 2, 2, G), AXES),
+        in_specs=(P(scan, "grp", None), P(), P(), P(), P(scan), P(None, AXES)),
         out_specs=(P(AXES, None), P(AXES, None)),
         check_vma=False,
     )

time: 69.2 us -> 64.1 us (0.926)
  blocking collectives: 51.2 us -> 44.3 us
  waiting for transfers between devices: 0 us -> 2.08 us
    all_to_all x2, blocking collectives: 51.2 us -> 44.3 us  [exchange(): return lax.all_to_all(value, axes, split_axis=0, concat_axis=0, tiled=True)]
    ppermute x0 -> x1, waiting for transfers between devices: none -> 2.08 us  [local(): swapped = lax.ppermute(theirs, 'core', [(0, 1), (1, 0)])]
  transfers between devices with their start and end apart: 0 -> 1, of which waited for: 0 -> 1; matrix products, arithmetic and copies ran while one was open for 0% -> 0% of each run, Pallas kernels for 0% -> 0%
where the time goes in v6:
time: 64.1 us; the launch traced here: 63.9 us
  blocking collectives  44.3 us (69%)
  Pallas kernels  15.6 us (24%)
  waiting for transfers between devices  2.08 us (3%)
  local copies, waits for them, and re-layouts  0.92 us (1%)
  between operations  0.69 us (1%)
    all_to_all x2, blocking collectives, exchange(): return lax.all_to_all(value, axes, split_axis=0, concat_axis=0, tiled=True)  44.3 us
    pallas_call x1, Pallas kernels, local(): pl.pallas_call(strip_kernel, in_specs=[smem, vmem, vmem, hbm, vmem], out_...  9.42 us
    pallas_call x1, Pallas kernels, local(): pl.pallas_call(reference_kernel, in_specs=[smem, smem, hbm, vmem, vmem, v...  4.81 us
    ppermute x1, waiting for transfers between devices, local(): swapped = lax.ppermute(theirs, 'core', [(0, 1), (1, 0)])  2.08 us
    pallas_call x1, Pallas kernels, local(): pl.pallas_call(finish_kernel, in_specs=[vmem] * 5, out_specs=[vmem, vmem]...  1.41 us
  transfers between devices with their start and end apart: 1, of which 1 were waited for; matrix products, arithmetic and copies ran while one was open for 0% of the time, Pallas kernels for 0%

profile of v6, /device:TPU:0, one launch (start us, length us, event | category | flops | bytes accessed | tf_op | source)
XLA Modules:
  0.0 63.9 jit_solution(15777170121371733445)
XLA Ops:
  0.6 0.0 copy-start.2
  0.6 0.0 copy-start.6
  0.7 4.8 %reference_image.1 = (bf16[128,16,128]{2,1,0:T(8,128)(2,1)}, f32[24,1024]{1,0:T(8,128)}) custom-call(f32[16]{0:T(128)} %level.3, s32[2,8]{1,0:T(2,128)} %amounts.1, bf16[16,128,1024]{2,1,0:T(8,128)(2,1)} %frames.3, s32[288,128]{1,0:T(8,128)} %bitcast.5, s32[288,128]{1,0:T(8,128)} %bitcast.6, s32[1,1024]{1,0:T(1,128)} %bitcast.7), custom_call_target="tpu_custom_call" | custom-call | tf_op jit(solution)/shard_map/reference_image/pallas_call | solution.py:418
  5.5 24.9 %all_to_all.10.recv = bf16[128,16,128]{2,1,0:T(8,128)(2,1)S(1)} all-to-all(bf16[128,16,128]{2,1,0:T(8,128)(2,1)} %get-tuple-element.6), channel_id=1, replica_groups=mesh['pair'=8,'core'=2,'grp'=8] {'pair','core','grp'}, dimensions={0} | all-to-all | bytes 1048576 | tf_op jit(solution)/shard_map/all_to_all | solution.py:406
  30.4 0.0 copy-done.2
  30.4 0.0 copy-done.6
  30.4 0.0 copy-start.3
  30.4 0.9 %copy-done.3 = f32[24,1024]{1,0:T(8,128)S(1)} copy-done((f32[24,1024]{1,0:T(8,128)S(1)}, f32[24,1024]{1,0:T(8,128)}, u32[]{:S(2)}) %copy-start.3) | copy-done | bytes 98328
  31.3 9.4 %strip.1 = (bf16[512,640]{1,0:T(8,128)(2,1)S(1)}, bf16[512,640]{1,0:T(8,128)(2,1)S(1)}) custom-call(f32[16]{0:T(128)S(1)} %copy-done.6, bf16[128,16,128]{2,1,0:T(8,128)(2,1)S(1)} %all_to_all.10.recv, f32[24,1024]{1,0:T(8,128)S(1)} %copy-done.3, bf16[16,128,1024]{2,1,0:T(8,128)(2,1)} %frames.3, bf16[1024,128]{1,0:T(8,128)(2,1)S(1)} %copy-done.2), custom_call_target="tpu_custom_call" | custom-call | tf_op jit(solution)/shard_map/strip/pallas_call | solution.py:438
  40.7 0.1 collective-permute-start
  40.8 2.1 %collective-permute-done = bf16[512,640]{1,0:T(8,128)(2,1)S(1)} collective-permute-done((bf16[512,640]{1,0:T(8,128)(2,1)S(1)}, bf16[512,640]{1,0:T(8,128)(2,1)S(1)}, u32[]{:S(2)}, u32[]{:S(2)}) %collective-permute-start) | collective-permute-done | bytes 655392 | tf_op jit(solution)/shard_map/ppermute | solution.py:460
  42.9 0.0 copy-start
  42.9 0.0 copy-start.1
  42.9 0.0 copy-start.4
  42.9 0.0 copy-start.5
  42.9 0.2 fusion
  43.1 19.4 %all_to_all.11.recv = bf16[64,8,640]{2,1,0:T(8,128)(2,1)S(1)} all-to-all(bf16[64,8,640]{2,1,0:T(8,128)(2,1)S(1)} %fusion), channel_id=1, replica_groups=mesh['pair'=8,'core'=2,'grp'=8] {'pair','grp'}, dimensions={0} | all-to-all | bytes 1310720 | tf_op jit(solution)/shard_map/all_to_all | solution.py:406
  62.4 0.0 copy-done
  62.4 0.0 copy-done.1
  62.4 0.0 copy-done.4
  62.4 0.0 copy-done.5
  62.5 1.4 %finish.1 = (f32[4,2048]{1,0:T(4,128)}, f32[8,256]{1,0:T(8,128)}) custom-call(bf16[64,8,640]{2,1,0:T(8,128)(2,1)S(1)} %all_to_all.11.recv, bf16[4,256,256]{2,1,0:T(8,128)(2,1)S(1)} %copy-done.1, bf16[4,256,512]{2,1,0:T(8,128)(2,1)S(1)} %copy-done, f32[128,128]{1,0:T(8,128)S(1)} %copy-done.4, f32[48,128]{1,0:T(8,128)S(1)} %copy-done.5), custom_call_target="tpu_custom_call" | custom-call | tf_op jit(solution)/shard_map/finish/pallas_call | solution.py:464
Async XLA Ops:
  0.6 29.8 %copy-start.2 = (bf16[1024,128]{1,0:T(8,128)(2,1)S(1)}, bf16[1024,128]{1,0:T(8,128)(2,1)}, u32[]{:S(2)}) copy-start(bf16[1024,128]{1,0:T(8,128)(2,1)} %constant.10.clone.rows) | copy-start | bytes 786436
  0.6 29.7 %copy-start.6 = (f32[16]{0:T(128)S(1)}, f32[16]{0:T(128)}, u32[]{:S(2)}) copy-start(f32[16]{0:T(128)} %level.3) | copy-start | bytes 196
  30.4 0.9 %copy-start.3 = (f32[24,1024]{1,0:T(8,128)S(1)}, f32[24,1024]{1,0:T(8,128)}, u32[]{:S(2)}) copy-start(f32[24,1024]{1,0:T(8,128)} %get-tuple-element.7.keep) | copy-start | bytes 294916
  40.7 2.2 %collective-permute-start = (bf16[512,640]{1,0:T(8,128)(2,1)S(1)}, bf16[512,640]{1,0:T(8,128)(2,1)S(1)}, u32[]{:S(2)}, u32[]{:S(2)}) collective-permute-start(bf16[512,640]{1,0:T(8,128)(2,1)S(1)} %get-tuple-element.9), channel_id=1, source_target_pairs={{0,8},{8,0},{1,9},{9,1},{2,10},{10,2},{3,11},{11,3},{4,12},{12,4},... | collective-permute-start | bytes 1966088 | tf_op jit(solution)/shard_map/ppermute | solution.py:460
  42.9 19.5 %copy-start = (bf16[4,256,512]{2,1,0:T(8,128)(2,1)S(1)}, bf16[4,256,512]{2,1,0:T(8,128)(2,1)}, u32[]{:S(2)}) copy-start(bf16[4,256,512]{2,1,0:T(8,128)(2,1)} %constant.12.clone.inverse) | copy-start | bytes 3145732
  42.9 19.5 %copy-start.1 = (bf16[4,256,256]{2,1,0:T(8,128)(2,1)S(1)}, bf16[4,256,256]{2,1,0:T(8,128)(2,1)}, u32[]{:S(2)}) copy-start(bf16[4,256,256]{2,1,0:T(8,128)(2,1)} %constant.11.clone.forward) | copy-start | bytes 1572868
  42.9 19.5 %copy-start.4 = (f32[128,128]{1,0:T(8,128)S(1)}, f32[128,128]{1,0:T(8,128)}, u32[]{:S(2)}) copy-start(f32[128,128]{1,0:T(8,128)} %constant.13.clone.phase) | copy-start | bytes 196612
  42.9 19.6 %copy-start.5 = (f32[48,128]{1,0:T(8,128)S(1)}, f32[48,128]{1,0:T(8,128)}, u32[]{:S(2)}) copy-start(f32[48,128]{1,0:T(8,128)} %constant.14.clone.nyquist) | copy-start | bytes 73732

commit v7 on v6

--- a/solution.py
+++ b/solution.py
@@ -29,6 +29,8 @@
 TN = (((0,), (0,)), ((), ()))
 MIB = 1024 * 1024
 YP = YS // PARTS
+FOOT = 32
+KEEP_ROWS = 1024
 
 
 def iota(shape, dim):
@@ -97,7 +99,13 @@
     return high, mid, value - high - mid
 
 
-def reference_kernel(level, amounts, frames, dark, gain, index, send, keep, held, sems):
+def reference_kernel(
+    level, amounts, frames, dark, gain, index, send, foot_out, keep_out, held, keep, sems, keep_sems
+):
+    def stay(i):
+        span = pl.ds(8 * i, 8 + 8 * i)
+        return pltpu.make_async_copy(keep.at[span], keep_out.at[span], keep_sems.at[i])
+
     def part(i):
         span = pl.ds(i * (YS // PARTS), YS // PARTS)
         return pltpu.make_async_copy(frames.at[span], held.at[span], sems.at[i])
@@ -120,6 +128,7 @@
     gain_px = (pick(1) * 32.0 + pick(2)) * (1.0 / 4096.0)
     keep[0:1, :] = dark_px
     keep[1:2, :] = gain_px
+    stay(0).start()
     offset = jnp.sum(dark_px * gain_px)
     for i in range(PARTS):
         part(i).wait()
@@ -135,39 +144,40 @@
                 jnp.ones((8, 256), BF16), jnp.concatenate([high, low], 1), NT, preferred_element_type=F32
             )
             keep[8 + y : 9 + y, 0:128] = total[0:1] - level[y] * offset
+    stay(1).start()
     s = lax.axis_index("pair") * 2 + lax.axis_index("core")
     g = lax.axis_index("grp")
     r = keep[8:24, 0:128]
     center = jnp.sum(r) * (1.0 / (YS * XS))
     rest = r - center
-    lane = iota((1, 128), 1)
-    base = 8 * lax.rem(s * G + g, 16)
-    row_sy = jnp.zeros((1, 128), F32)
-    row_sx = jnp.zeros((1, 128), F32)
+    lane = iota((8, 128), 1)
+    top = iota((8, 128), 0) == 0
+    foot = jnp.zeros((8, 128), F32)
     for i in range(8):
-        row_sy = jnp.where(lane == base + i, amounts[0, i].astype(F32), row_sy)
-        row_sx = jnp.where(lane == base + i, amounts[1, i].astype(F32), row_sx)
-    row_center = jnp.zeros((1, 128), F32)
-    for i, piece in enumerate(three_parts(jnp.full((1, 128), center))):
-        row_center = jnp.where(lane == i, piece, row_center)
-    foot = jnp.concatenate([row_sy, row_sx, row_center, jnp.zeros((5, 128), F32)], axis=0)
-
-    def chunk(top):
-        return jnp.concatenate([top, foot], axis=0).astype(BF16)
-
-    plain = chunk(jnp.zeros((8, 128), F32))
+        foot = jnp.where(lane == FOOT + i, amounts[0, i].astype(F32), foot)
+        foot = jnp.where(lane == FOOT + 8 + i, amounts[1, i].astype(F32), foot)
+    for i, piece in enumerate(three_parts(jnp.full((8, 128), center))):
+        foot = jnp.where(lane == FOOT + 16 + i, piece, foot)
+    foot = jnp.where(top, foot, 0.0)
+    foot_out[...] = foot.astype(BF16)
+    plain = foot.astype(BF16)
     for d in range(N):
         send[d] = plain
-    lanes = iota((8, 128), 1)
-    sides = jnp.where((lanes >= 32) & (lanes < 96), pltpu.roll(rest[8:16], 64, 1), rest[0:8])
-    for ds, top in ((S - 1, rest[0:8]), (0, sides), (1, rest[8:16])):
+    here = top & (lane >= FOOT) & (lane < FOOT + 24)
+    first = rest[0:8]
+    last = jnp.where(top, foot, rest[8:16])
+    sides = jnp.where((lane >= 32) & (lane < 96), pltpu.roll(rest[8:16], 64, 1), first)
+    for ds, block in ((S - 1, first), (0, sides), (1, last)):
         for dg in (G - 1, 0, 1):
             if ds or dg:
-                send[lax.rem(s + ds, S) * G + lax.rem(g + dg, G)] = chunk(top)
+                whole = block if ds == S - 1 and dg == 0 else jnp.where(here, foot, block)
+                send[lax.rem(s + ds, S) * G + lax.rem(g + dg, G)] = whole.astype(BF16)
+    for i in range(2):
+        stay(i).wait()
 
 
 def strip_kernel(
-    level, recv, keep, frames, rows, mine, theirs, corr, held, v, moved, hot, main, over, window, table, around, sums, sems
+    level, recv, below, keep_hbm, frames, rows, mine, theirs, corr, keep, feet, held, v, moved, hot, main, over, window, table, around, sums, sems, keep_sem
 ):
     s = lax.axis_index("pair") * 2 + lax.axis_index("core")
     g = lax.axis_index("grp")
@@ -178,23 +188,30 @@
     for i in range(PARTS):
         part(i).start()
 
-    centers = jnp.zeros((8, 128), F32)
-    feet = []
-    for t in range(8):
-        foot = jnp.zeros((8, 128), F32)
-        for i in range(16):
-            foot = foot + recv[16 * t + i].astype(F32)[8:16]
-        feet.append(foot)
-        centers = centers + foot
-    mean = jnp.sum(jnp.where(iota((1, 128), 1) < 3, centers[2:3], 0.0), axis=1, keepdims=True) * (1.0 / N)
+    kept = pltpu.make_async_copy(keep_hbm.at[pl.ds(0, 24)], keep, keep_sem)
+    kept.start()
+
+    for d in range(N):
+        feet[d : d + 1, :] = recv[d].astype(F32)[0:1, :]
+    feet[pl.ds(lax.rem(s + 1, S) * G + g, 1), :] = below[...].astype(F32)[0:1, :]
+    lane = iota((N, 128), 1)
+    means = jnp.where((lane >= FOOT + 16) & (lane < FOOT + 19), feet[...], 0.0)
+    mean = jnp.sum(jnp.sum(means, axis=0, keepdims=True), axis=1, keepdims=True) * (1.0 / N)
     total_row = jnp.zeros((1, 128), F32)
     for i, piece in enumerate(three_parts(mean * (SY * SX))):
         total_row = jnp.where(iota((1, 128), 1) == 96 + i, piece, total_row)
+    wide = iota((128, 256), 1)
+    pick = iota((128, 256), 0) == FOOT + 8 * (wide >> 7) + (wide & 7)
+    shifts = jnp.dot(feet[...].astype(BF16), pick.astype(F32).astype(BF16), preferred_element_type=F32)
+    shifts = jnp.where((iota((N, 256), 0) & 15) == ((wide & 127) >> 3), shifts, 0.0)
+    shifts = jnp.sum(shifts.reshape(8, 16, 256), axis=1).astype(jnp.int32)
+    kept.wait()
 
     def neighbour(ds, dg):
-        got = recv[lax.rem(s + ds, S) * G + lax.rem(g + dg, G)].astype(F32)
-        center = jnp.sum(jnp.where(iota((1, 128), 1) < 3, got[10:11], 0.0), axis=1, keepdims=True)
-        return got[0:8] + (center - mean)
+        src = lax.rem(s + ds, S) * G + lax.rem(g + dg, G)
+        spot = iota((1, 128), 1)
+        row = jnp.where((spot >= FOOT + 16) & (spot < FOOT + 19), feet[pl.ds(src, 1), :], 0.0)
+        return recv[src].astype(F32) + (jnp.sum(row, axis=1, keepdims=True) - mean)
 
     for j, dg in enumerate((G - 1, 0, 1)):
         lanes = slice(128 * j, 128 * (j + 1))
@@ -211,8 +228,8 @@
 
     row = iota((BX * 16, 128), 0)
     for t in range(8):
-        sy = feet[t][0:1].astype(jnp.int32)
-        sx = feet[t][1:2].astype(jnp.int32)
+        sy = shifts[t : t + 1, 0:128]
+        sx = shifts[t : t + 1, 128:256]
         code = ((sx >> 2) + 8) * 16 + (sx & 3) * 4 + (sy & 3)
         hot[:, 128 * t : 128 * (t + 1)] = (row == code).astype(F32).astype(BF16)
 
@@ -234,7 +251,7 @@
 
     for t in range(8):
         lanes = slice(128 * t, 128 * (t + 1))
-        by = (feet[t][0:1].astype(jnp.int32) >> 2) + 8
+        by = (shifts[t : t + 1, 0:128] >> 2) + 8
         masks = [
             jnp.broadcast_to(((by >> b) & 1).astype(F32), (16, 128)).astype(BF16) > 0.5 for b in range(5)
         ]
@@ -402,6 +419,10 @@
         out[:, 512 * j : 512 * (j + 1)] = (quarter * scale)[0:4]
 
 
+def permute(value, axes, pairs):
+    return lax.ppermute(value, axes, pairs)
+
+
 def exchange(value, axes):
     return lax.all_to_all(value, axes, split_axis=0, concat_axis=0, tiled=True)
 
@@ -415,15 +436,21 @@
     vmem = pl.BlockSpec(memory_space=pltpu.VMEM)
     hbm = pl.BlockSpec(memory_space=pltpu.HBM)
 
-    send, keep = pl.pallas_call(
+    send, foot, keep = pl.pallas_call(
         reference_kernel,
         in_specs=[smem, smem, hbm, vmem, vmem, vmem],
-        out_specs=[vmem, vmem],
+        out_specs=[vmem, vmem, hbm],
         out_shape=[
-            jax.ShapeDtypeStruct((N, 16, 128), BF16),
-            jax.ShapeDtypeStruct((24, BF), F32),
+            jax.ShapeDtypeStruct((N, 8, 128), BF16),
+            jax.ShapeDtypeStruct((8, 128), BF16),
+            jax.ShapeDtypeStruct((KEEP_ROWS, BF), F32),
         ],
-        scratch_shapes=[pltpu.VMEM((YS, XS, BF), BF16), pltpu.SemaphoreType.DMA((PARTS,))],
+        scratch_shapes=[
+            pltpu.VMEM((YS, XS, BF), BF16),
+            pltpu.VMEM((24, BF), F32),
+            pltpu.SemaphoreType.DMA((PARTS,)),
+            pltpu.SemaphoreType.DMA((2,)),
+        ],
         compiler_params=limit(60),
         name="reference_image",
     )(
@@ -434,14 +461,17 @@
         gain_frame.reshape(ROWS, 128),
         bf_index.reshape(1, BF),
     )
+    below = permute(foot, ("pair", "core"), [(i, (i - 1) % S) for i in range(S)])
     recv = exchange(send, AXES)
     mine, theirs = pl.pallas_call(
         strip_kernel,
-        in_specs=[smem, vmem, vmem, hbm, vmem],
+        in_specs=[smem, vmem, vmem, hbm, hbm, vmem],
         out_specs=[vmem, vmem],
         out_shape=[jax.ShapeDtypeStruct((BF // 2, 640), BF16)] * 2,
         scratch_shapes=[
             pltpu.VMEM((BF, 256), BF16),
+            pltpu.VMEM((24, BF), F32),
+            pltpu.VMEM((N, 128), F32),
             pltpu.VMEM((YS, XS, BF), BF16),
             pltpu.VMEM((YS, XS, BF), BF16),
             pltpu.VMEM((32, XS, BF), BF16),
@@ -453,11 +483,12 @@
             pltpu.VMEM((256, YS * XS), BF16),
             pltpu.VMEM((2, BX * 16, BF), F32),
             pltpu.SemaphoreType.DMA((PARTS,)),
+            pltpu.SemaphoreType.DMA,
         ],
         compiler_params=limit(50),
         name="strip",
-    )(row_level, recv, keep, frames, jnp.asarray(row_kernel()))
-    swapped = lax.ppermute(theirs, "core", [(0, 1), (1, 0)])
+    )(row_level, recv, below, keep, frames, jnp.asarray(row_kernel()))
+    swapped = permute(theirs, "core", [(0, 1), (1, 0)])
     both = (mine.astype(F32) + swapped.astype(F32)).astype(BF16)
     parts = exchange(both.reshape(N // 2, 8, 640), ("pair", "grp"))
     tables = [jnp.asarray(t) for t in (*col_tables(), phase_tables(), nyquist_tables())]

time: 64.1 us -> 63.5 us (level)
  blocking collectives: 44.3 us -> 20.6 us
  starting transfers between devices: 0.09 us -> 16.1 us
  waiting for transfers between devices: 2.08 us -> 8.19 us
  Pallas kernels: 15.6 us -> 17.6 us
  local copies, waits for them, and re-layouts: 0.92 us -> 0.03 us
    all_to_all x2 -> x1, blocking collectives: 44.3 us -> 20.6 us  [exchange(): return lax.all_to_all(value, axes, split_axis=0, concat_axis=0, tiled=True)]
    all_to_all x0 -> x1, starting transfers between devices: none -> 11.1 us  [exchange(): return lax.all_to_all(value, axes, split_axis=0, concat_axis=0, tiled=True)]
    ppermute x1 -> x2, starting transfers between devices: 0.09 us -> 4.92 us  [permute(): return lax.ppermute(value, axes, pairs)]
    all_to_all x0 -> x1, waiting for transfers between devices: none -> 4.59 us  [exchange(): return lax.all_to_all(value, axes, split_axis=0, concat_axis=0, tiled=True)]
    pallas_call x1, Pallas kernels: 9.42 us -> 11 us  [local(): pl.pallas_call(strip_kernel, in_specs=[smem, vmem, vmem, hbm, hbm, vmem],...]
    ppermute x1 -> x2, waiting for transfers between devices: 2.08 us -> 3.6 us  [permute(): return lax.ppermute(value, axes, pairs)]
    unnamed x14 -> x12, local copies, waits for them, and re-layouts: 0.92 us -> 0.03 us
  transfers between devices with their start and end apart: 1 -> 3, of which waited for: 1 -> 3; matrix products, arithmetic and copies ran while one was open for 0% -> 0% of each run, Pallas kernels for 0% -> 0%
where the time goes in v7:
time: 63.5 us; the launch traced here: 63.3 us
  blocking collectives  20.6 us (32%)
  Pallas kernels  17.6 us (28%)
  starting transfers between devices  16.1 us (25%)
  waiting for transfers between devices  8.19 us (13%)
  between operations  0.71 us (1%)
    all_to_all x1, blocking collectives, exchange(): return lax.all_to_all(value, axes, split_axis=0, concat_axis=0, tiled=True)  20.6 us
    all_to_all x1, starting transfers between devices, exchange(): return lax.all_to_all(value, axes, split_axis=0, concat_axis=0, tiled=True)  11.1 us
    pallas_call x1, Pallas kernels, local(): pl.pallas_call(strip_kernel, in_specs=[smem, vmem, vmem, hbm, hbm, vmem],...  11 us
    pallas_call x1, Pallas kernels, local(): pl.pallas_call(reference_kernel, in_specs=[smem, smem, hbm, vmem, vmem, v...  5.16 us
    ppermute x2, starting transfers between devices, permute(): return lax.ppermute(value, axes, pairs)  4.92 us
    all_to_all x1, waiting for transfers between devices, exchange(): return lax.all_to_all(value, axes, split_axis=0, concat_axis=0, tiled=True)  4.59 us
    ppermute x2, waiting for transfers between devices, permute(): return lax.ppermute(value, axes, pairs)  3.6 us
    pallas_call x1, Pallas kernels, local(): pl.pallas_call(finish_kernel, in_specs=[vmem] * 5, out_specs=[vmem, vmem]...  1.41 us
  transfers between devices with their start and end apart: 3, of which 3 were waited for; matrix products, arithmetic and copies ran while one was open for 0% of the time, Pallas kernels for 0%

profile of v7, /device:TPU:0, one launch (start us, length us, event | category | flops | bytes accessed | tf_op | source)
XLA Modules:
  0.0 63.3 jit_solution(10976179082163439453)
XLA Ops:
  0.6 0.0 copy-start.2
  0.6 0.0 copy-start.5
  0.7 5.2 %reference_image.1 = (bf16[128,8,128]{2,1,0:T(8,128)(2,1)}, bf16[8,128]{1,0:T(8,128)(2,1)}, f32[1024,1024]{1,0:T(8,128)}) custom-call(f32[16]{0:T(128)} %level.3, s32[2,8]{1,0:T(2,128)} %amounts.1, bf16[16,128,1024]{2,1,0:T(8,128)(2,1)} %frames.3, s32[288,128]{1,0:T(8,128)} %bitcast.5, s32[288,128]{1,0:T(8,128)} %bitcast.6, s32[1,1024]{1,0:T(1,128)} %bitcast.7), custom_call_target="tpu_custom_call" | custom-call | tf_op jit(solution)/shard_map/reference_image/pallas_call | solution.py:439
  5.8 11.1 %all-to-all-start = ((bf16[128,8,128]{2,1,0:T(8,128)(2,1)}), bf16[128,8,128]{2,1,0:T(8,128)(2,1)S(1)}, u32[]{:S(2)}, u32[]{:S(2)}) async-start(bf16[128,8,128]{2,1,0:T(8,128)(2,1)} %get-tuple-element.7), calls=%async_computation | async-start | bytes 524288 | tf_op jit(solution)/shard_map/all_to_all | solution.py:427
  17.0 4.8 %collective-permute-start = (bf16[8,128]{1,0:T(8,128)(2,1)}, bf16[8,128]{1,0:T(8,128)(2,1)S(1)}, u32[]{:S(2)}, u32[]{:S(2)}) collective-permute-start(bf16[8,128]{1,0:T(8,128)(2,1)} %get-tuple-element.8), channel_id=1, source_target_pairs={{0,120},{8,0},{16,8},{24,16},{32,24},{40,32},{48,40},{56,48},{64,5... | collective-permute-start | bytes 6152 | tf_op jit(solution)/shard_map/ppermute | solution.py:423
  21.8 1.5 %collective-permute-done.below = bf16[8,128]{1,0:T(8,128)(2,1)S(1)} collective-permute-done((bf16[8,128]{1,0:T(8,128)(2,1)}, bf16[8,128]{1,0:T(8,128)(2,1)S(1)}, u32[]{:S(2)}, u32[]{:S(2)}) %collective-permute-start) | collective-permute-done | bytes 2080 | tf_op jit(solution)/shard_map/ppermute | solution.py:423
  23.3 4.6 %all-to-all-done.recv = bf16[128,8,128]{2,1,0:T(8,128)(2,1)S(1)} async-done(((bf16[128,8,128]{2,1,0:T(8,128)(2,1)}), bf16[128,8,128]{2,1,0:T(8,128)(2,1)S(1)}, u32[]{:S(2)}, u32[]{:S(2)}) %all-to-all-start) | async-done | bytes 262176 | tf_op jit(solution)/shard_map/all_to_all | solution.py:427
  27.9 0.0 copy-done.2
  27.9 0.0 copy-done.5
  27.9 11.0 %strip.1 = (bf16[512,640]{1,0:T(8,128)(2,1)S(1)}, bf16[512,640]{1,0:T(8,128)(2,1)S(1)}) custom-call(f32[16]{0:T(128)S(1)} %copy-done.5, bf16[128,8,128]{2,1,0:T(8,128)(2,1)S(1)} %all-to-all-done.recv, bf16[8,128]{1,0:T(8,128)(2,1)S(1)} %collective-permute-done.below, f32[1024,1024]{1,0:T(8,128)} %get-tuple-element.9.keep_hbm, bf16[16,128,1024]{2,1,0:T(8,128)(2,1)} %frames.3, ...), custom_call_target="tpu_custom_call" | custom-call | tf_op jit(solution)/shard_map/strip/pallas_call | solution.py:466
  39.0 0.1 collective-permute-start.1
  39.0 2.1 %collective-permute-done.1 = bf16[512,640]{1,0:T(8,128)(2,1)S(1)} collective-permute-done((bf16[512,640]{1,0:T(8,128)(2,1)S(1)}, bf16[512,640]{1,0:T(8,128)(2,1)S(1)}, u32[]{:S(2)}, u32[]{:S(2)}) %collective-permute-start.1) | collective-permute-done | bytes 655392 | tf_op jit(solution)/shard_map/ppermute | solution.py:423
  41.1 0.0 copy-start
  41.1 0.0 copy-start.1
  41.1 0.0 copy-start.3
  41.1 0.0 copy-start.4
  41.1 0.2 fusion
  41.3 20.6 %all_to_all.10.recv = bf16[64,8,640]{2,1,0:T(8,128)(2,1)S(1)} all-to-all(bf16[64,8,640]{2,1,0:T(8,128)(2,1)S(1)} %fusion), channel_id=1, replica_groups=mesh['pair'=8,'core'=2,'grp'=8] {'pair','grp'}, dimensions={0} | all-to-all | bytes 1310720 | tf_op jit(solution)/shard_map/all_to_all | solution.py:427
  61.9 0.0 copy-done
  61.9 0.0 copy-done.1
  61.9 0.0 copy-done.3
  61.9 0.0 copy-done.4
  61.9 1.4 %finish.1 = (f32[4,2048]{1,0:T(4,128)}, f32[8,256]{1,0:T(8,128)}) custom-call(bf16[64,8,640]{2,1,0:T(8,128)(2,1)S(1)} %all_to_all.10.recv, bf16[4,256,256]{2,1,0:T(8,128)(2,1)S(1)} %copy-done.1, bf16[4,256,512]{2,1,0:T(8,128)(2,1)S(1)} %copy-done, f32[128,128]{1,0:T(8,128)S(1)} %copy-done.3, f32[48,128]{1,0:T(8,128)S(1)} %copy-done.4), custom_call_target="tpu_custom_call" | custom-call | tf_op jit(solution)/shard_map/finish/pallas_call | solution.py:495
Async XLA Ops:
  0.6 27.3 %copy-start.2 = (bf16[1024,128]{1,0:T(8,128)(2,1)S(1)}, bf16[1024,128]{1,0:T(8,128)(2,1)}, u32[]{:S(2)}) copy-start(bf16[1024,128]{1,0:T(8,128)(2,1)} %constant.10.clone.rows) | copy-start | bytes 786436
  0.6 27.3 %copy-start.5 = (f32[16]{0:T(128)S(1)}, f32[16]{0:T(128)}, u32[]{:S(2)}) copy-start(f32[16]{0:T(128)} %level.3) | copy-start | bytes 196
  5.8 22.1 %all-to-all-start = ((bf16[128,8,128]{2,1,0:T(8,128)(2,1)}), bf16[128,8,128]{2,1,0:T(8,128)(2,1)S(1)}, u32[]{:S(2)}, u32[]{:S(2)}) async-start(bf16[128,8,128]{2,1,0:T(8,128)(2,1)} %get-tuple-element.7), calls=%async_computation | async-start | bytes 524288 | tf_op jit(solution)/shard_map/all_to_all | solution.py:427
  17.0 6.4 %collective-permute-start = (bf16[8,128]{1,0:T(8,128)(2,1)}, bf16[8,128]{1,0:T(8,128)(2,1)S(1)}, u32[]{:S(2)}, u32[]{:S(2)}) collective-permute-start(bf16[8,128]{1,0:T(8,128)(2,1)} %get-tuple-element.8), channel_id=1, source_target_pairs={{0,120},{8,0},{16,8},{24,16},{32,24},{40,32},{48,40},{56,48},{64,5... | collective-permute-start | bytes 6152 | tf_op jit(solution)/shard_map/ppermute | solution.py:423
  39.0 2.2 %collective-permute-start.1 = (bf16[512,640]{1,0:T(8,128)(2,1)S(1)}, bf16[512,640]{1,0:T(8,128)(2,1)S(1)}, u32[]{:S(2)}, u32[]{:S(2)}) collective-permute-start(bf16[512,640]{1,0:T(8,128)(2,1)S(1)} %get-tuple-element.11), channel_id=1, source_target_pairs={{0,8},{8,0},{1,9},{9,1},{2,10},{10,2},{3,11},{11,3},{4,12},{12,4},... | collective-permute-start | bytes 1966088 | tf_op jit(solution)/shard_map/ppermute | solution.py:423
  41.1 20.8 %copy-start = (bf16[4,256,512]{2,1,0:T(8,128)(2,1)S(1)}, bf16[4,256,512]{2,1,0:T(8,128)(2,1)}, u32[]{:S(2)}) copy-start(bf16[4,256,512]{2,1,0:T(8,128)(2,1)} %constant.12.clone.inverse) | copy-start | bytes 3145732
  41.1 20.8 %copy-start.1 = (bf16[4,256,256]{2,1,0:T(8,128)(2,1)S(1)}, bf16[4,256,256]{2,1,0:T(8,128)(2,1)}, u32[]{:S(2)}) copy-start(bf16[4,256,256]{2,1,0:T(8,128)(2,1)} %constant.11.clone.forward) | copy-start | bytes 1572868
  41.1 20.8 %copy-start.3 = (f32[128,128]{1,0:T(8,128)S(1)}, f32[128,128]{1,0:T(8,128)}, u32[]{:S(2)}) copy-start(f32[128,128]{1,0:T(8,128)} %constant.13.clone.phase) | copy-start | bytes 196612
  41.1 20.8 %copy-start.4 = (f32[48,128]{1,0:T(8,128)S(1)}, f32[48,128]{1,0:T(8,128)}, u32[]{:S(2)}) copy-start(f32[48,128]{1,0:T(8,128)} %constant.14.clone.nyquist) | copy-start | bytes 73732

commit v8 on v7

--- a/solution.py
+++ b/solution.py
@@ -42,7 +42,7 @@
     q = np.arange(1024)
     d = np.cos(2 * np.pi * k[None, :] * q[:, None] / 1024).sum(1) / 256
     r = np.arange(1024)
-    yp = 4 * (r // 8) + r % 4
+    yp = np.where(r < 512, r, (r - 512) ^ 4)
     yy = np.repeat(np.arange(32), 4)
     fy = np.tile(np.arange(4), 32)
     return d[(2 * yp[:, None] - fy[None, :] - 4 * (yy[None, :] - 8)) % 1024].astype(ml_dtypes.bfloat16)
@@ -177,7 +177,7 @@
 
 
 def strip_kernel(
-    level, recv, below, keep_hbm, frames, rows, mine, theirs, corr, keep, feet, held, v, moved, hot, main, over, window, table, around, sums, sems, keep_sem
+    level, recv, below, keep_hbm, frames, rows, mine, theirs, corr, keep, feet, held, v, moved, hot, main, over, window, table, around, sums, left, sems, keep_sem
 ):
     s = lax.axis_index("pair") * 2 + lax.axis_index("core")
     g = lax.axis_index("grp")
@@ -185,11 +185,16 @@
     def part(i):
         return pltpu.make_async_copy(frames.at[pl.ds(i * YP, YP)], held.at[pl.ds(i * YP, YP)], sems.at[i])
 
+    kept = pltpu.make_async_copy(keep_hbm.at[pl.ds(0, 24)], keep, keep_sem)
+    kept.start()
     for i in range(PARTS):
         part(i).start()
 
-    kept = pltpu.make_async_copy(keep_hbm.at[pl.ds(0, 24)], keep, keep_sem)
-    kept.start()
+    col = iota((128, 256), 1)
+    spread = ((iota((128, 256), 0) >> 2) == (col >> 3)) & ((iota((128, 256), 0) & 3) == (col & 3))
+    left[...] = jnp.dot(
+        rows[...], spread.astype(F32).astype(BF16), preferred_element_type=F32
+    ).astype(BF16)
 
     for d in range(N):
         feet[d : d + 1, :] = recv[d].astype(F32)[0:1, :]
@@ -285,9 +290,9 @@
             acc_over = jnp.zeros((16, 128), F32)
             for b in range(1, BX):
                 piece = pltpu.roll(sums[j & 1, 16 * b : 16 * (b + 1), lanes], b, 1)
-                acc_main = acc_main + jnp.where(lane >= b, piece, 0.0)
+                acc_main = acc_main + piece
                 acc_over = acc_over + jnp.where(lane < b, piece, 0.0)
-            main[8 * j + h] = acc_main
+            main[8 * j + h] = acc_main - acc_over
             over[8 * j + h] = acc_over
 
     sign_y = 1.0 - 2.0 * (iota((32, 16, 128), 0) & 1).astype(F32)
@@ -298,32 +303,35 @@
     q_high = q_row.astype(BF16).astype(F32)
     q_row = q_high + pltpu.roll(q_row - q_high, 16, 1)
 
-    col = iota((128, 512), 1)
-    spread = ((iota((128, 512), 0) >> 2) == (col >> 4)) & ((iota((128, 512), 0) & 3) == (col & 3))
-    left = jnp.dot(rows[...], spread.astype(F32).astype(BF16), preferred_element_type=F32)
-    left = jnp.where(((iota((BF, 512), 0) >> 2) & 1) == ((iota((BF, 512), 1) >> 3) & 1), left, 0.0).astype(BF16)
-    kind = (iota((512, 128), 0) >> 2) & 1
-    u_main = main[...].reshape(512, 128)
-    u_over = over[...].reshape(512, 128)
-    first = jnp.where(kind == 0, u_over, 0.0)
-    second = jnp.where(kind == 1, u_over, 0.0)
-    right = jnp.concatenate(
-        [
-            jnp.where(kind == 0, u_main, 0.0),
-            jnp.where(kind == 1, u_main, 0.0),
-            first + pltpu.roll(second, 16, 1),
-        ],
-        axis=1,
-    ).astype(BF16)
-    z = jnp.dot(left, right, preferred_element_type=F32)
-    z = jnp.concatenate([z[:, 0:256], z[:, 256:384] + (q_row + total_row)], axis=1).astype(BF16)
+    kind = (iota((256, 128), 0) >> 2) & 1
+    z = []
+    for h in range(2):
+        u_main = main[:, 8 * h : 8 * h + 8, :].reshape(256, 128)
+        u_over = over[:, 8 * h : 8 * h + 8, :].reshape(256, 128)
+        right = jnp.concatenate(
+            [
+                jnp.where(kind == 0, u_main, 0.0),
+                jnp.where(kind == 1, u_main, 0.0),
+                jnp.where(kind == 0, u_over, 0.0) + pltpu.roll(jnp.where(kind == 1, u_over, 0.0), 16, 1),
+            ],
+            axis=1,
+        ).astype(BF16)
+        z.append(jnp.dot(left[512 * h : 512 * (h + 1), :], right, preferred_element_type=F32))
+    extra = jnp.concatenate([jnp.zeros((1, 256), F32), q_row + total_row], axis=1)
+    lower = iota((8, 384), 0) < 4
     for b in range(S):
+        pieces = []
+        for j in range(4 * b, 4 * b + 4):
+            z0 = z[0][8 * j : 8 * j + 8]
+            z1 = z[1][8 * j : 8 * j + 8]
+            pieces += [jnp.where(lower, z0, z1) + extra, jnp.where(lower, z1, z0) + extra]
         place = pl.multiple_of(64 * (lax.rem(s + b, S) >> 1), 64)
         to = theirs if b & 1 else mine
-        to[pl.ds(place, 64), 0:384] = z[64 * b : 64 * (b + 1)]
+        to[pl.ds(place, 64), 0:384] = jnp.concatenate(pieces, axis=0).astype(BF16)
 
 
 def finish_kernel(recv, forward, inverse, phase, nyquist, out, corr_out, full):
+    swap = (jnp.zeros((8, 384), jnp.int32) + lax.axis_index("grp")) & 1 == 1
     corr = jnp.zeros((8, 256), F32)
     sums = []
     for g in range(G):
@@ -332,7 +340,7 @@
             got = recv[a * G + g].astype(F32)
             acc = acc + got[:, 0:384]
             corr = corr + got[:, 384:640]
-        sums.append(acc)
+        sums.append(jnp.where(swap, pltpu.roll(acc, 4, 0), acc))
     n = iota((256, 256), 0)
     m = iota((256, 256), 1)
     order = ((n >> 4) == (m & 15)) & ((15 - (n & 15)) == (m >> 4))
@@ -482,6 +490,7 @@
             pltpu.VMEM((16, 32, 128), F32),
             pltpu.VMEM((256, YS * XS), BF16),
             pltpu.VMEM((2, BX * 16, BF), F32),
+            pltpu.VMEM((BF, 256), BF16),
             pltpu.SemaphoreType.DMA((PARTS,)),
             pltpu.SemaphoreType.DMA,
         ],

time: 63.5 us -> 61.8 us (0.973)
  Pallas kernels: 17.6 us -> 15.8 us
    pallas_call x1, Pallas kernels: 11 us -> 9.22 us  [local(): pl.pallas_call(strip_kernel, in_specs=[smem, vmem, vmem, hbm, hbm, vmem],...]
where the time goes in v8:
time: 61.8 us; the launch traced here: 61.5 us
  blocking collectives  20.6 us (33%)
  starting transfers between devices  16.1 us (26%)
  Pallas kernels  15.8 us (26%)
  waiting for transfers between devices  8.19 us (13%)
  between operations  0.71 us (1%)
    all_to_all x1, blocking collectives, exchange(): return lax.all_to_all(value, axes, split_axis=0, concat_axis=0, tiled=True)  20.6 us
    all_to_all x1, starting transfers between devices, exchange(): return lax.all_to_all(value, axes, split_axis=0, concat_axis=0, tiled=True)  11.1 us
    pallas_call x1, Pallas kernels, local(): pl.pallas_call(strip_kernel, in_specs=[smem, vmem, vmem, hbm, hbm, vmem],...  9.22 us
    pallas_call x1, Pallas kernels, local(): pl.pallas_call(reference_kernel, in_specs=[smem, smem, hbm, vmem, vmem, v...  5.16 us
    ppermute x2, starting transfers between devices, permute(): return lax.ppermute(value, axes, pairs)  4.92 us
    all_to_all x1, waiting for transfers between devices, exchange(): return lax.all_to_all(value, axes, split_axis=0, concat_axis=0, tiled=True)  4.59 us
    ppermute x2, waiting for transfers between devices, permute(): return lax.ppermute(value, axes, pairs)  3.6 us
    pallas_call x1, Pallas kernels, local(): pl.pallas_call(finish_kernel, in_specs=[vmem] * 5, out_specs=[vmem, vmem]...  1.43 us
  transfers between devices with their start and end apart: 3, of which 3 were waited for; matrix products, arithmetic and copies ran while one was open for 0% of the time, Pallas kernels for 0%

profile of v8, /device:TPU:0, one launch (start us, length us, event | category | flops | bytes accessed | tf_op | source)
XLA Modules:
  0.0 61.5 jit_solution(11372355664757648224)
XLA Ops:
  0.6 0.0 copy-start.2
  0.6 0.0 copy-start.5
  0.7 5.2 %reference_image.1 = (bf16[128,8,128]{2,1,0:T(8,128)(2,1)}, bf16[8,128]{1,0:T(8,128)(2,1)}, f32[1024,1024]{1,0:T(8,128)}) custom-call(f32[16]{0:T(128)} %level.3, s32[2,8]{1,0:T(2,128)} %amounts.1, bf16[16,128,1024]{2,1,0:T(8,128)(2,1)} %frames.3, s32[288,128]{1,0:T(8,128)} %bitcast.5, s32[288,128]{1,0:T(8,128)} %bitcast.6, s32[1,1024]{1,0:T(1,128)} %bitcast.7), custom_call_target="tpu_custom_call" | custom-call | tf_op jit(solution)/shard_map/reference_image/pallas_call | solution.py:447
  5.8 11.1 %all-to-all-start = ((bf16[128,8,128]{2,1,0:T(8,128)(2,1)}), bf16[128,8,128]{2,1,0:T(8,128)(2,1)S(1)}, u32[]{:S(2)}, u32[]{:S(2)}) async-start(bf16[128,8,128]{2,1,0:T(8,128)(2,1)} %get-tuple-element.7), calls=%async_computation | async-start | bytes 524288 | tf_op jit(solution)/shard_map/all_to_all | solution.py:435
  17.0 4.8 %collective-permute-start = (bf16[8,128]{1,0:T(8,128)(2,1)}, bf16[8,128]{1,0:T(8,128)(2,1)S(1)}, u32[]{:S(2)}, u32[]{:S(2)}) collective-permute-start(bf16[8,128]{1,0:T(8,128)(2,1)} %get-tuple-element.8), channel_id=1, source_target_pairs={{0,120},{8,0},{16,8},{24,16},{32,24},{40,32},{48,40},{56,48},{64,5... | collective-permute-start | bytes 6152 | tf_op jit(solution)/shard_map/ppermute | solution.py:431
  21.8 1.5 %collective-permute-done.below = bf16[8,128]{1,0:T(8,128)(2,1)S(1)} collective-permute-done((bf16[8,128]{1,0:T(8,128)(2,1)}, bf16[8,128]{1,0:T(8,128)(2,1)S(1)}, u32[]{:S(2)}, u32[]{:S(2)}) %collective-permute-start) | collective-permute-done | bytes 2080 | tf_op jit(solution)/shard_map/ppermute | solution.py:431
  23.3 4.6 %all-to-all-done.recv = bf16[128,8,128]{2,1,0:T(8,128)(2,1)S(1)} async-done(((bf16[128,8,128]{2,1,0:T(8,128)(2,1)}), bf16[128,8,128]{2,1,0:T(8,128)(2,1)S(1)}, u32[]{:S(2)}, u32[]{:S(2)}) %all-to-all-start) | async-done | bytes 262176 | tf_op jit(solution)/shard_map/all_to_all | solution.py:435
  27.9 0.0 copy-done.2
  27.9 0.0 copy-done.5
  27.9 9.2 %strip.1 = (bf16[512,640]{1,0:T(8,128)(2,1)S(1)}, bf16[512,640]{1,0:T(8,128)(2,1)S(1)}) custom-call(f32[16]{0:T(128)S(1)} %copy-done.5, bf16[128,8,128]{2,1,0:T(8,128)(2,1)S(1)} %all-to-all-done.recv, bf16[8,128]{1,0:T(8,128)(2,1)S(1)} %collective-permute-done.below, f32[1024,1024]{1,0:T(8,128)} %get-tuple-element.9.keep_hbm, bf16[16,128,1024]{2,1,0:T(8,128)(2,1)} %frames.3, ...), custom_call_target="tpu_custom_call" | custom-call | tf_op jit(solution)/shard_map/strip/pallas_call | solution.py:474
  37.2 0.1 collective-permute-start.1
  37.2 2.1 %collective-permute-done.1 = bf16[512,640]{1,0:T(8,128)(2,1)S(1)} collective-permute-done((bf16[512,640]{1,0:T(8,128)(2,1)S(1)}, bf16[512,640]{1,0:T(8,128)(2,1)S(1)}, u32[]{:S(2)}, u32[]{:S(2)}) %collective-permute-start.1) | collective-permute-done | bytes 655392 | tf_op jit(solution)/shard_map/ppermute | solution.py:431
  39.3 0.0 copy-start
  39.3 0.0 copy-start.1
  39.3 0.0 copy-start.3
  39.3 0.0 copy-start.4
  39.3 0.2 fusion
  39.5 20.6 %all_to_all.10.recv = bf16[64,8,640]{2,1,0:T(8,128)(2,1)S(1)} all-to-all(bf16[64,8,640]{2,1,0:T(8,128)(2,1)S(1)} %fusion), channel_id=1, replica_groups=mesh['pair'=8,'core'=2,'grp'=8] {'pair','grp'}, dimensions={0} | all-to-all | bytes 1310720 | tf_op jit(solution)/shard_map/all_to_all | solution.py:435
  60.1 0.0 copy-done
  60.1 0.0 copy-done.1
  60.1 0.0 copy-done.3
  60.1 0.0 copy-done.4
  60.1 1.4 %finish.1 = (f32[4,2048]{1,0:T(4,128)}, f32[8,256]{1,0:T(8,128)}) custom-call(bf16[64,8,640]{2,1,0:T(8,128)(2,1)S(1)} %all_to_all.10.recv, bf16[4,256,256]{2,1,0:T(8,128)(2,1)S(1)} %copy-done.1, bf16[4,256,512]{2,1,0:T(8,128)(2,1)S(1)} %copy-done, f32[128,128]{1,0:T(8,128)S(1)} %copy-done.3, f32[48,128]{1,0:T(8,128)S(1)} %copy-done.4), custom_call_target="tpu_custom_call" | custom-call | tf_op jit(solution)/shard_map/finish/pallas_call | solution.py:504
Async XLA Ops:
  0.6 27.3 %copy-start.2 = (bf16[1024,128]{1,0:T(8,128)(2,1)S(1)}, bf16[1024,128]{1,0:T(8,128)(2,1)}, u32[]{:S(2)}) copy-start(bf16[1024,128]{1,0:T(8,128)(2,1)} %constant.10.clone.rows) | copy-start | bytes 786436
  0.6 27.3 %copy-start.5 = (f32[16]{0:T(128)S(1)}, f32[16]{0:T(128)}, u32[]{:S(2)}) copy-start(f32[16]{0:T(128)} %level.3) | copy-start | bytes 196
  5.8 22.1 %all-to-all-start = ((bf16[128,8,128]{2,1,0:T(8,128)(2,1)}), bf16[128,8,128]{2,1,0:T(8,128)(2,1)S(1)}, u32[]{:S(2)}, u32[]{:S(2)}) async-start(bf16[128,8,128]{2,1,0:T(8,128)(2,1)} %get-tuple-element.7), calls=%async_computation | async-start | bytes 524288 | tf_op jit(solution)/shard_map/all_to_all | solution.py:435
  17.0 6.4 %collective-permute-start = (bf16[8,128]{1,0:T(8,128)(2,1)}, bf16[8,128]{1,0:T(8,128)(2,1)S(1)}, u32[]{:S(2)}, u32[]{:S(2)}) collective-permute-start(bf16[8,128]{1,0:T(8,128)(2,1)} %get-tuple-element.8), channel_id=1, source_target_pairs={{0,120},{8,0},{16,8},{24,16},{32,24},{40,32},{48,40},{56,48},{64,5... | collective-permute-start | bytes 6152 | tf_op jit(solution)/shard_map/ppermute | solution.py:431
  37.2 2.2 %collective-permute-start.1 = (bf16[512,640]{1,0:T(8,128)(2,1)S(1)}, bf16[512,640]{1,0:T(8,128)(2,1)S(1)}, u32[]{:S(2)}, u32[]{:S(2)}) collective-permute-start(bf16[512,640]{1,0:T(8,128)(2,1)S(1)} %get-tuple-element.11), channel_id=1, source_target_pairs={{0,8},{8,0},{1,9},{9,1},{2,10},{10,2},{3,11},{11,3},{4,12},{12,4},... | collective-permute-start | bytes 1966088 | tf_op jit(solution)/shard_map/ppermute | solution.py:431
  39.3 20.8 %copy-start = (bf16[4,256,512]{2,1,0:T(8,128)(2,1)S(1)}, bf16[4,256,512]{2,1,0:T(8,128)(2,1)}, u32[]{:S(2)}) copy-start(bf16[4,256,512]{2,1,0:T(8,128)(2,1)} %constant.12.clone.inverse) | copy-start | bytes 3145732
  39.3 20.8 %copy-start.1 = (bf16[4,256,256]{2,1,0:T(8,128)(2,1)S(1)}, bf16[4,256,256]{2,1,0:T(8,128)(2,1)}, u32[]{:S(2)}) copy-start(bf16[4,256,256]{2,1,0:T(8,128)(2,1)} %constant.11.clone.forward) | copy-start | bytes 1572868
  39.3 20.8 %copy-start.3 = (f32[128,128]{1,0:T(8,128)S(1)}, f32[128,128]{1,0:T(8,128)}, u32[]{:S(2)}) copy-start(f32[128,128]{1,0:T(8,128)} %constant.13.clone.phase) | copy-start | bytes 196612
  39.3 20.8 %copy-start.4 = (f32[48,128]{1,0:T(8,128)S(1)}, f32[48,128]{1,0:T(8,128)}, u32[]{:S(2)}) copy-start(f32[48,128]{1,0:T(8,128)} %constant.14.clone.nyquist) | copy-start | bytes 73732

commit v9 on v8

--- a/solution.py
+++ b/solution.py
@@ -176,18 +176,34 @@
         stay(i).wait()
 
 
+def early_kernel(level, keep_hbm, frames, v_out, held, keep, sems):
+    copies = [
+        pltpu.make_async_copy(keep_hbm.at[pl.ds(0, 8)], keep, sems.at[2]),
+        pltpu.make_async_copy(frames.at[pl.ds(0, 4)], held.at[pl.ds(0, 4)], sems.at[0]),
+        pltpu.make_async_copy(frames.at[pl.ds(4, 4)], held.at[pl.ds(4, 4)], sems.at[1]),
+    ]
+    for copy in copies:
+        copy.start()
+    copies[0].wait()
+    for i in range(2):
+        copies[1 + i].wait()
+        for y in range(4 * i, 4 * i + 4):
+            value = (held[y].astype(F32) - level[y] * keep[0:1, :]) * keep[1:2, :]
+            v_out[y] = value.astype(BF16)
+
+
 def strip_kernel(
-    level, recv, below, keep_hbm, frames, rows, mine, theirs, corr, keep, feet, held, v, moved, hot, main, over, window, table, around, sums, left, sems, keep_sem
+    level, recv, below, keep_hbm, frames, early, rows, mine, theirs, corr, keep, feet, held, v, moved, hot, main, over, window, table, around, sums, left, sems, keep_sem
 ):
     s = lax.axis_index("pair") * 2 + lax.axis_index("core")
     g = lax.axis_index("grp")
 
     def part(i):
-        return pltpu.make_async_copy(frames.at[pl.ds(i * YP, YP)], held.at[pl.ds(i * YP, YP)], sems.at[i])
+        return pltpu.make_async_copy(frames.at[pl.ds(8 + 4 * i, 4)], held.at[pl.ds(4 * i, 4)], sems.at[i])
 
     kept = pltpu.make_async_copy(keep_hbm.at[pl.ds(0, 24)], keep, keep_sem)
     kept.start()
-    for i in range(PARTS):
+    for i in range(2):
         part(i).start()
 
     col = iota((128, 256), 1)
@@ -241,13 +257,19 @@
     for y in range(YS):
         for b in range(16):
             around[16 * b : 16 * (b + 1), 128 * y : 128 * (y + 1)] = table[b, y + 1 : y + 17, :].astype(BF16)
-    for i in range(PARTS):
+    for i in range(2):
         part(i).wait()
-        for y in range(i * YP, (i + 1) * YP):
-            value = (held[y].astype(F32) - level[y] * keep[0:1, :]) * keep[1:2, :]
+        for y in range(4 * i, 4 * i + 4):
+            value = (held[y].astype(F32) - level[8 + y] * keep[0:1, :]) * keep[1:2, :]
             v[y] = value.astype(BF16)
-    corr[...] = lax.dot_general(
-        v[...].reshape(YS * XS, BF), around[...], (((0,), (1,)), ((), ())), preferred_element_type=F32
+    half = YS * XS // 2
+    corr[...] = (
+        lax.dot_general(
+            early[...].reshape(half, BF), around[:, 0:half], (((0,), (1,)), ((), ())), preferred_element_type=F32
+        )
+        + lax.dot_general(
+            v[...].reshape(half, BF), around[:, half:], (((0,), (1,)), ((), ())), preferred_element_type=F32
+        )
     ).astype(BF16)
     core = lax.axis_index("core")
     for a in range(S // 2):
@@ -263,7 +285,8 @@
 
         zero = jnp.zeros((16, 128), BF16)
         for x0 in range(0, XS, 16):
-            rows_in = [v[y, x0 : x0 + 16, lanes] for y in range(YS)]
+            rows_in = [early[y, x0 : x0 + 16, lanes] for y in range(8)]
+            rows_in += [v[y, x0 : x0 + 16, lanes] for y in range(8)]
             for b in range(5):
                 step = 1 << b
                 size = min(len(rows_in) + step, 32)
@@ -471,17 +494,31 @@
     )
     below = permute(foot, ("pair", "core"), [(i, (i - 1) % S) for i in range(S)])
     recv = exchange(send, AXES)
+    early = pl.pallas_call(
+        early_kernel,
+        in_specs=[smem, hbm, hbm],
+        out_specs=vmem,
+        out_shape=jax.ShapeDtypeStruct((8, XS, BF), BF16),
+        scratch_shapes=[
+            pltpu.VMEM((8, XS, BF), BF16),
+            pltpu.VMEM((8, BF), F32),
+            pltpu.SemaphoreType.DMA((3,)),
+        ],
+        compiler_params=limit(50),
+        cost_estimate=pl.CostEstimate(flops=4 * YS * XS * BF, bytes_accessed=2 * YS * XS * BF, transcendentals=0),
+        name="early",
+    )(row_level, keep, frames)
     mine, theirs = pl.pallas_call(
         strip_kernel,
-        in_specs=[smem, vmem, vmem, hbm, hbm, vmem],
+        in_specs=[smem, vmem, vmem, hbm, hbm, vmem, vmem],
         out_specs=[vmem, vmem],
         out_shape=[jax.ShapeDtypeStruct((BF // 2, 640), BF16)] * 2,
         scratch_shapes=[
             pltpu.VMEM((BF, 256), BF16),
             pltpu.VMEM((24, BF), F32),
             pltpu.VMEM((N, 128), F32),
-            pltpu.VMEM((YS, XS, BF), BF16),
-            pltpu.VMEM((YS, XS, BF), BF16),
+            pltpu.VMEM((8, XS, BF), BF16),
+            pltpu.VMEM((8, XS, BF), BF16),
             pltpu.VMEM((32, XS, BF), BF16),
             pltpu.VMEM((BX * 16, BF), BF16),
             pltpu.VMEM((32, 16, 128), F32),
@@ -491,12 +528,12 @@
             pltpu.VMEM((256, YS * XS), BF16),
             pltpu.VMEM((2, BX * 16, BF), F32),
             pltpu.VMEM((BF, 256), BF16),
-            pltpu.SemaphoreType.DMA((PARTS,)),
+            pltpu.SemaphoreType.DMA((2,)),
             pltpu.SemaphoreType.DMA,
         ],
         compiler_params=limit(50),
         name="strip",
-    )(row_level, recv, below, keep, frames, jnp.asarray(row_kernel()))
+    )(row_level, recv, below, keep, frames, early, jnp.asarray(row_kernel()))
     swapped = permute(theirs, "core", [(0, 1), (1, 0)])
     both = (mine.astype(F32) + swapped.astype(F32)).astype(BF16)
     parts = exchange(both.reshape(N // 2, 8, 640), ("pair", "grp"))

time: 61.8 us -> 61.1 us (0.989)
  waiting for transfers between devices: 8.19 us -> 5.8 us
  Pallas kernels: 15.8 us -> 17.6 us
    pallas_call x1 -> x2, Pallas kernels: 9.22 us -> 11.1 us  [the longest x1 8.71 us: local(): pl.pallas_call(strip_kernel, in_specs=[smem, vmem, vmem, hbm, hbm, vmem,...]
    ppermute x2, waiting for transfers between devices: 3.6 us -> 2.09 us  [permute(): return lax.ppermute(value, axes, pairs)]
    all_to_all x1, waiting for transfers between devices: 4.59 us -> 3.71 us  [exchange(): return lax.all_to_all(value, axes, split_axis=0, concat_axis=0, tiled=True)]
  transfers between devices with their start and end apart: 3 -> 3, of which waited for: 3 -> 2; matrix products, arithmetic and copies ran while one was open for 0% -> 0% of each run, Pallas kernels for 0% -> 4%
where the time goes in v9:
time: 61.1 us; the launch traced here: 60.9 us
  blocking collectives  20.4 us (33%)
  Pallas kernels  17.6 us (29%)
  starting transfers between devices  16.1 us (26%)
  waiting for transfers between devices  5.8 us (9%)
  between operations  0.74 us (1%)
    all_to_all x1, blocking collectives, exchange(): return lax.all_to_all(value, axes, split_axis=0, concat_axis=0, tiled=True)  20.4 us
    all_to_all x1, starting transfers between devices, exchange(): return lax.all_to_all(value, axes, split_axis=0, concat_axis=0, tiled=True)  11.1 us
    pallas_call x1, Pallas kernels, local(): pl.pallas_call(strip_kernel, in_specs=[smem, vmem, vmem, hbm, hbm, vmem,...  8.71 us
    pallas_call x1, Pallas kernels, local(): pl.pallas_call(reference_kernel, in_specs=[smem, smem, hbm, vmem, vmem, v...  5.12 us
    ppermute x2, starting transfers between devices, permute(): return lax.ppermute(value, axes, pairs)  4.92 us
    all_to_all x1, waiting for transfers between devices, exchange(): return lax.all_to_all(value, axes, split_axis=0, concat_axis=0, tiled=True)  3.71 us
    pallas_call x1, Pallas kernels, local(): pl.pallas_call(early_kernel, in_specs=[smem, hbm, hbm], out_specs=vmem, o...  2.38 us
    ppermute x2, waiting for transfers between devices, permute(): return lax.ppermute(value, axes, pairs)  2.09 us
  transfers between devices with their start and end apart: 3, of which 2 were waited for; matrix products, arithmetic and copies ran while one was open for 0% of the time, Pallas kernels for 4%

profile of v9, /device:TPU:0, one launch (start us, length us, event | category | flops | bytes accessed | tf_op | source)
XLA Modules:
  0.0 60.9 jit_solution(2658771810086732218)
XLA Ops:
  0.6 0.0 copy-start.5
  0.6 5.1 %reference_image.1 = (bf16[128,8,128]{2,1,0:T(8,128)(2,1)}, bf16[8,128]{1,0:T(8,128)(2,1)}, f32[1024,1024]{1,0:T(8,128)}) custom-call(f32[16]{0:T(128)} %level.5, s32[2,8]{1,0:T(2,128)} %amounts.1, bf16[16,128,1024]{2,1,0:T(8,128)(2,1)} %frames.5, s32[288,128]{1,0:T(8,128)} %bitcast.5, s32[288,128]{1,0:T(8,128)} %bitcast.6, s32[1,1024]{1,0:T(1,128)} %bitcast.7), custom_call_target="tpu_custom_call" | custom-call | tf_op jit(solution)/shard_map/reference_image/pallas_call | solution.py:470
  5.8 11.1 %all-to-all-start = ((bf16[128,8,128]{2,1,0:T(8,128)(2,1)}), bf16[128,8,128]{2,1,0:T(8,128)(2,1)S(1)}, u32[]{:S(2)}, u32[]{:S(2)}) async-start(bf16[128,8,128]{2,1,0:T(8,128)(2,1)} %get-tuple-element.7), calls=%async_computation | async-start | bytes 524288 | tf_op jit(solution)/shard_map/all_to_all | solution.py:458
  16.9 4.8 %collective-permute-start = (bf16[8,128]{1,0:T(8,128)(2,1)}, bf16[8,128]{1,0:T(8,128)(2,1)S(1)}, u32[]{:S(2)}, u32[]{:S(2)}) collective-permute-start(bf16[8,128]{1,0:T(8,128)(2,1)} %get-tuple-element.8), channel_id=1, source_target_pairs={{0,120},{8,0},{16,8},{24,16},{32,24},{40,32},{48,40},{56,48},{64,5... | collective-permute-start | bytes 6152 | tf_op jit(solution)/shard_map/ppermute | solution.py:454
  21.8 0.0 copy-done.5
  21.8 0.0 copy-start.2
  21.8 2.4 %early.1 = bf16[8,128,1024]{2,1,0:T(8,128)(2,1)S(1)} custom-call(f32[16]{0:T(128)S(1)} %copy-done.5, f32[1024,1024]{1,0:T(8,128)} %get-tuple-element.9.keep_hbm, bf16[16,128,1024]{2,1,0:T(8,128)(2,1)} %frames.5), custom_call_target="tpu_custom_call" | custom-call | flops 8388608 | bytes 4194304 | tf_op jit(solution)/shard_map/early/pallas_call | solution.py:497
  24.1 0.0 collective-permute-done.below
  24.2 3.7 %all-to-all-done.recv = bf16[128,8,128]{2,1,0:T(8,128)(2,1)S(1)} async-done(((bf16[128,8,128]{2,1,0:T(8,128)(2,1)}), bf16[128,8,128]{2,1,0:T(8,128)(2,1)S(1)}, u32[]{:S(2)}, u32[]{:S(2)}) %all-to-all-start) | async-done | bytes 262176 | tf_op jit(solution)/shard_map/all_to_all | solution.py:458
  27.9 0.0 copy-done.2
  27.9 8.7 %strip.1 = (bf16[512,640]{1,0:T(8,128)(2,1)S(1)}, bf16[512,640]{1,0:T(8,128)(2,1)S(1)}) custom-call(f32[16]{0:T(128)S(1)} %copy-done.5, bf16[128,8,128]{2,1,0:T(8,128)(2,1)S(1)} %all-to-all-done.recv, bf16[8,128]{1,0:T(8,128)(2,1)S(1)} %collective-permute-done.below, f32[1024,1024]{1,0:T(8,128)} %get-tuple-element.9.keep_hbm, bf16[16,128,1024]{2,1,0:T(8,128)(2,1)} %frames.5, ...), custom_call_target="tpu_custom_call" | custom-call | tf_op jit(solution)/shard_map/strip/pallas_call | solution.py:511
  36.6 0.0 copy-start
  36.6 0.0 copy-start.1
  36.6 0.0 copy-start.3
  36.6 0.0 copy-start.4
  36.6 0.1 collective-permute-start.1
  36.7 2.1 %collective-permute-done.1 = bf16[512,640]{1,0:T(8,128)(2,1)S(1)} collective-permute-done((bf16[512,640]{1,0:T(8,128)(2,1)S(1)}, bf16[512,640]{1,0:T(8,128)(2,1)S(1)}, u32[]{:S(2)}, u32[]{:S(2)}) %collective-permute-start.1) | collective-permute-done | bytes 655392 | tf_op jit(solution)/shard_map/ppermute | solution.py:454
  38.8 0.2 fusion
  39.0 20.4 %all_to_all.10.recv = bf16[64,8,640]{2,1,0:T(8,128)(2,1)S(1)} all-to-all(bf16[64,8,640]{2,1,0:T(8,128)(2,1)S(1)} %fusion), channel_id=1, replica_groups=mesh['pair'=8,'core'=2,'grp'=8] {'pair','grp'}, dimensions={0} | all-to-all | bytes 1310720 | tf_op jit(solution)/shard_map/all_to_all | solution.py:458
  59.4 0.0 copy-done
  59.4 0.0 copy-done.1
  59.4 0.0 copy-done.3
  59.4 0.0 copy-done.4
  59.4 1.4 %finish.1 = (f32[4,2048]{1,0:T(4,128)}, f32[8,256]{1,0:T(8,128)}) custom-call(bf16[64,8,640]{2,1,0:T(8,128)(2,1)S(1)} %all_to_all.10.recv, bf16[4,256,256]{2,1,0:T(8,128)(2,1)S(1)} %copy-done.1, bf16[4,256,512]{2,1,0:T(8,128)(2,1)S(1)} %copy-done, f32[128,128]{1,0:T(8,128)S(1)} %copy-done.3, f32[48,128]{1,0:T(8,128)S(1)} %copy-done.4), custom_call_target="tpu_custom_call" | custom-call | tf_op jit(solution)/shard_map/finish/pallas_call | solution.py:541
Async XLA Ops:
  0.6 21.1 %copy-start.5 = (f32[16]{0:T(128)S(1)}, f32[16]{0:T(128)}, u32[]{:S(2)}) copy-start(f32[16]{0:T(128)} %level.5) | copy-start | bytes 196
  5.8 22.1 %all-to-all-start = ((bf16[128,8,128]{2,1,0:T(8,128)(2,1)}), bf16[128,8,128]{2,1,0:T(8,128)(2,1)S(1)}, u32[]{:S(2)}, u32[]{:S(2)}) async-start(bf16[128,8,128]{2,1,0:T(8,128)(2,1)} %get-tuple-element.7), calls=%async_computation | async-start | bytes 524288 | tf_op jit(solution)/shard_map/all_to_all | solution.py:458
  16.9 7.2 %collective-permute-start = (bf16[8,128]{1,0:T(8,128)(2,1)}, bf16[8,128]{1,0:T(8,128)(2,1)S(1)}, u32[]{:S(2)}, u32[]{:S(2)}) collective-permute-start(bf16[8,128]{1,0:T(8,128)(2,1)} %get-tuple-element.8), channel_id=1, source_target_pairs={{0,120},{8,0},{16,8},{24,16},{32,24},{40,32},{48,40},{56,48},{64,5... | collective-permute-start | bytes 6152 | tf_op jit(solution)/shard_map/ppermute | solution.py:454
  21.8 6.1 %copy-start.2 = (bf16[1024,128]{1,0:T(8,128)(2,1)S(1)}, bf16[1024,128]{1,0:T(8,128)(2,1)}, u32[]{:S(2)}) copy-start(bf16[1024,128]{1,0:T(8,128)(2,1)} %constant.10.clone.rows) | copy-start | bytes 786436
  36.6 22.8 %copy-start = (bf16[4,256,512]{2,1,0:T(8,128)(2,1)S(1)}, bf16[4,256,512]{2,1,0:T(8,128)(2,1)}, u32[]{:S(2)}) copy-start(bf16[4,256,512]{2,1,0:T(8,128)(2,1)} %constant.12.clone.inverse) | copy-start | bytes 3145732
  36.6 22.8 %copy-start.1 = (bf16[4,256,256]{2,1,0:T(8,128)(2,1)S(1)}, bf16[4,256,256]{2,1,0:T(8,128)(2,1)}, u32[]{:S(2)}) copy-start(bf16[4,256,256]{2,1,0:T(8,128)(2,1)} %constant.11.clone.forward) | copy-start | bytes 1572868
  36.6 22.8 %copy-start.3 = (f32[128,128]{1,0:T(8,128)S(1)}, f32[128,128]{1,0:T(8,128)}, u32[]{:S(2)}) copy-start(f32[128,128]{1,0:T(8,128)} %constant.13.clone.phase) | copy-start | bytes 196612
  36.6 22.8 %copy-start.4 = (f32[48,128]{1,0:T(8,128)S(1)}, f32[48,128]{1,0:T(8,128)}, u32[]{:S(2)}) copy-start(f32[48,128]{1,0:T(8,128)} %constant.14.clone.nyquist) | copy-start | bytes 73732
  36.6 2.2 %collective-permute-start.1 = (bf16[512,640]{1,0:T(8,128)(2,1)S(1)}, bf16[512,640]{1,0:T(8,128)(2,1)S(1)}, u32[]{:S(2)}, u32[]{:S(2)}) collective-permute-start(bf16[512,640]{1,0:T(8,128)(2,1)S(1)} %get-tuple-element.11), channel_id=1, source_target_pairs={{0,8},{8,0},{1,9},{9,1},{2,10},{10,2},{3,11},{11,3},{4,12},{12,4},... | collective-permute-start | bytes 1966088 | tf_op jit(solution)/shard_map/ppermute | solution.py:454
